TPU v7x, 32 devices: a whole 2x2x4 slice. The times are simulated.
32 devices in a mesh: groups: 2 (over y), tile: 16 (over z, x, core).
Axes of the slice: x: 2, y: 2, z: 4, core: 2. Of those that a mesh axis runs over, the one named last changes fastest.
Arguments:
- object_field: float32 [4, 2, 2048, 1024], P('groups', None, 'tile'), parts along dimension 0, may hold values from -7.6 to 7.6
- probe_modes: float32 [8, 2, 128, 128], P('groups'), parts along dimension 0, may hold values from -2.1 to 2.1
- measured: float32 [192, 128, 128], P(('groups', 'tile')), parts along dimension 0, may hold values from 0 to 2
- row_offset: int32 [192], P(('groups', 'tile')), parts along dimension 0, may hold values from 0 to 127, as said below
- col_offset: int32 [192], P(('groups', 'tile')), parts along dimension 0, may hold values from 0 to 896
- tile_counts: int32 [32], P('groups'), parts along dimension 0, may hold values from 1 to 6, as said below
Outputs:
- updated_object: float32 [4, 2, 2048, 1024], P('groups', None, 'tile'), parts along dimension 0
- updated_probe: float32 [8, 2, 128, 128], P('groups'), parts along dimension 0
There are 2 independent parts, one for each index of `groups`. A program takes and returns all parts, laid end to end along the dimension named above; each array names one. Nothing has to cross between parts.
Inputs may be any that keep to these rules, and one draw needn't show every extreme that they name: `row_offset`: on the last tile a window's first row is at most 0, so windows never leave the object. The live positions of tile t fill its first tile_counts[t] slots; offsets and patterns of the other slots are unused.
All inputs are finite; a program needn't handle non-finite values.
Results may differ from a plain program's by a relative error of at most 0.0001.
Values sent between devices are 32-bit elements; how exact they have to be, the bound alone decides.
No kernel may reach another device: no remote copies, remote signals or barrier semaphores. Data moves between devices by JAX's collectives and lax.ppermute only.
A program may use at most 128 MiB of HBM per device.

v0:
```python
import functools
import math

import jax
import jax.numpy as jnp
import ml_dtypes
import numpy as np
from jax import lax
from jax.experimental import pallas as pl
from jax.experimental.pallas import tpu as pltpu
from jax.sharding import PartitionSpec as P

F32, BF16 = jnp.float32, jnp.bfloat16


def passed_along(value, axis, steps):
    count = lax.axis_size(axis)
    leading, last = (max(0, -steps), min(count, count - steps))
    return lax.ppermute(value, axis, [(source, source + steps) for source in range(leading, last)])


def complex_tables(width):
    index = np.arange(width)
    angle = 2.0 * math.pi / width * (index[:, None] * index[None, :] % width)
    dft = np.exp(-1j * angle) / math.sqrt(width)
    frequency = np.where(index < width // 2, index, index - width).astype(np.float64)
    phase = np.exp(-0.5j * math.pi / width * frequency**2)
    return dft, np.conj(dft) @ (phase[:, None] * dft)


def real_forms(table):
    re, im = table.real, table.imag
    right = np.block([[re, im], [-im, re]])
    left = np.block([[re, -im], [im, re]])

    def parts(matrix):
        high = matrix.astype(ml_dtypes.bfloat16)
        low = (matrix - high.astype(np.float64)).astype(ml_dtypes.bfloat16)
        return high, low

    right_high, right_low = parts(right)
    left_high, left_low = parts(left)
    return np.stack([right_high, right_low]), np.concatenate([left_high, left_low], 0)


def halves(value):
    high = value.astype(BF16)
    return high, (value - high.astype(F32)).astype(BF16)


def dot(left, right):
    return jnp.dot(left, right, preferred_element_type=F32)


def two_sided(blocks, right_ref, left_ref):
    modes, width = len(blocks), blocks[0][0].shape[0]
    rows = jnp.concatenate([jnp.concatenate(pair, 1) for pair in blocks], 0)
    high, low = halves(rows)
    both = dot(jnp.concatenate([high, low], 0), right_ref[0])
    first = both[: modes * width] + both[modes * width :] + dot(high, right_ref[1])
    cols = jnp.concatenate(
        [
            jnp.concatenate(
                [first[m * width : (m + 1) * width, part * width : (part + 1) * width] for m in range(modes)], 1
            )
            for part in range(2)
        ],
        0,
    )
    high, low = halves(cols)
    both = dot(left_ref[...], high)
    second = both[: 2 * width] + both[2 * width :] + dot(left_ref[: 2 * width], low)
    return [
        (second[:width, m * width : (m + 1) * width], second[width:, m * width : (m + 1) * width])
        for m in range(modes)
    ]


def times(left, right):
    return left[0] * right[0] - left[1] * right[1], left[0] * right[1] + left[1] * right[0]


def window_place(row_start, col_start, width, blocks):
    block = col_start // width
    shift = col_start - block * width
    lane = lax.broadcasted_iota(jnp.int32, (width, width), 1)
    row = lax.broadcasted_iota(jnp.int32, (width, width), 0)
    first = pl.ds(pl.multiple_of(block * width, width), width)
    second = pl.ds(pl.multiple_of(jnp.minimum(block + 1, blocks - 1) * width, width), width)
    return row >= row_start, lane >= shift, shift, first, second


def gradient_kernel(
    place_ref, object_ref, rim_ref, probe_ref, measured_ref, fr_ref, fl_ref, pr_ref, pl_ref,
    own_ref, next_ref, sums_ref,
):
    slices, _, _, tile_cols = object_ref.shape
    modes, _, width, _ = probe_ref.shape
    slots = measured_ref.shape[0]
    own_ref[...] = jnp.zeros(own_ref.shape, F32)
    next_ref[...] = jnp.zeros(next_ref.shape, F32)
    sums_ref[...] = jnp.zeros(sums_ref.shape, F32)

    def visit(slot, carry):
        row_start, col_start = place_ref[1 + slot], place_ref[1 + slots + slot]
        in_own, in_first, shift, first, second = window_place(row_start, col_start, width, tile_cols // width)

        def window(s, part):
            own = jnp.where(in_first, object_ref[s, part, :, first], object_ref[s, part, :, second])
            rim = jnp.where(in_first, rim_ref[s, part, :, first], rim_ref[s, part, :, second])
            stored = jnp.where(in_own, own, rim)
            stored = pltpu.roll(stored, lax.rem(width - row_start, width), 0)
            return pltpu.roll(stored, lax.rem(width - shift, width), 1)

        def put(s, part, value):
            value = pltpu.roll(pltpu.roll(value, row_start, 0), shift, 1)
            zero = jnp.zeros_like(value)
            own, rim = jnp.where(in_own, value, zero), jnp.where(in_own, zero, value)
            own_ref[s, part, :, first] += jnp.where(in_first, own, zero)
            own_ref[s, part, :, second] += jnp.where(in_first, zero, own)
            next_ref[s, part, :, first] += jnp.where(in_first, rim, zero)
            next_ref[s, part, :, second] += jnp.where(in_first, zero, rim)

        layer_one = (window(0, 0), window(0, 1))
        layer_two = (window(1, 0), window(1, 1))
        probe = [(probe_ref[m, 0], probe_ref[m, 1]) for m in range(modes)]
        moved = two_sided([times(p, layer_one) for p in probe], pr_ref, pl_ref)
        far = two_sided([times(w, layer_two) for w in moved], fr_ref, fl_ref)
        intensity = sum(re * re + im * im for re, im in far)
        residue = 2.0 * (intensity - measured_ref[slot])
        back = two_sided([(residue * re, -(residue * im)) for re, im in far], fr_ref, fl_ref)
        terms = [times(w, g) for w, g in zip(moved, back)]
        put(1, 0, sum(t[0] for t in terms))
        put(1, 1, -sum(t[1] for t in terms))
        back = two_sided([times(g, layer_two) for g in back], pr_ref, pl_ref)
        terms = [times(p, g) for p, g in zip(probe, back)]
        put(0, 0, sum(t[0] for t in terms))
        put(0, 1, -sum(t[1] for t in terms))
        for m in range(modes):
            grad = times(layer_one, back[m])
            sums_ref[2 * m] += grad[0]
            sums_ref[2 * m + 1] -= grad[1]
        sums_ref[2 * modes] += layer_one[0] * layer_one[0] + layer_one[1] * layer_one[1]
        return carry

    lax.fori_loop(0, place_ref[0], visit, 0)


def illumination_kernel(place_ref, before_ref, probe_ref, lit_ref):
    tile_cols = lit_ref.shape[1]
    modes, _, width, _ = probe_ref.shape
    slots = (place_ref.shape[0] - 1) // 2
    lit_ref[...] = jnp.zeros(lit_ref.shape, F32)
    power = sum(probe_ref[m, part] * probe_ref[m, part] for m in range(modes) for part in range(2))

    def add(slot, ref, own):
        row_start, col_start = ref[1 + slot], ref[1 + slots + slot]
        in_own, in_first, shift, first, second = window_place(row_start, col_start, width, tile_cols // width)
        value = pltpu.roll(pltpu.roll(power, row_start, 0), shift, 1)
        zero = jnp.zeros_like(value)
        value = jnp.where(in_own, value, zero) if own else jnp.where(in_own, zero, value)
        lit_ref[:, first] += jnp.where(in_first, value, zero)
        lit_ref[:, second] += jnp.where(in_first, zero, value)

    @pl.loop(0, place_ref[0])
    def _(slot):
        add(slot, place_ref, True)

    @pl.loop(0, before_ref[0])
    def _(slot):
        add(slot, before_ref, False)


def all_sum(value, axis):
    count = lax.axis_size(axis)
    index = lax.axis_index(axis)
    bits = [1 << b for b in range(count.bit_length() - 1)]
    halved = []
    for bit in bits:
        pairs = [(i, i ^ bit) for i in range(count)]
        low_side = (index // bit) % 2 == 0
        half = value.shape[0] // 2
        if len(halved) < 3:
            low, high = value[:half], value[half:]
            kept, sent = jnp.where(low_side, low, high), jnp.where(low_side, high, low)
            value = kept + lax.ppermute(sent, axis, pairs)
            halved.append((pairs, low_side))
        else:
            value = value + lax.ppermute(value, axis, pairs)
    for pairs, low_side in reversed(halved):
        got = lax.ppermute(value, axis, pairs)
        value = jnp.concatenate([jnp.where(low_side, value, got), jnp.where(low_side, got, value)], 0)
    return value


def body(object_field, probe_modes, measured, row_offset, col_offset, tile_counts):
    slices, _, tile_rows, tile_cols = object_field.shape
    modes, _, width, _ = probe_modes.shape
    dft, move = complex_tables(width)
    tables = [jnp.asarray(t) for t in (*real_forms(dft), *real_forms(move))]
    tile_idx = lax.axis_index("tile")
    counts = lax.dynamic_slice(jnp.concatenate([jnp.zeros((1,), jnp.int32), tile_counts]), (tile_idx,), (2,))
    place = jnp.concatenate([counts[1:], row_offset, col_offset])
    before = passed_along(place, "tile", 1)
    rim_rows = passed_along(object_field, "tile", -1)
    smem = pl.BlockSpec(memory_space=pltpu.SMEM)
    vmem = pl.BlockSpec(memory_space=pltpu.VMEM)
    params = pltpu.CompilerParams(vmem_limit_bytes=56 << 20)
    illumination = pl.pallas_call(
        illumination_kernel,
        out_shape=jax.ShapeDtypeStruct((tile_rows, tile_cols), F32),
        in_specs=[smem, smem, vmem],
        out_specs=vmem,
        compiler_params=params,
    )(place, before, probe_modes)
    grad_own, grad_next, sums = pl.pallas_call(
        gradient_kernel,
        out_shape=(
            jax.ShapeDtypeStruct(object_field.shape, F32),
            jax.ShapeDtypeStruct((slices, 2, width, tile_cols), F32),
            jax.ShapeDtypeStruct((2 * modes + 1, width, width), F32),
        ),
        in_specs=[smem] + [vmem] * 8,
        out_specs=(vmem,) * 3,
        compiler_params=params,
    )(place, object_field, rim_rows, probe_modes, measured, *tables)
    arrived = passed_along(grad_next, "tile", 1)
    total = all_sum(sums.reshape(-1, width), "tile").reshape(sums.shape)
    updated_object = object_field - 0.5 * (grad_own + arrived) / (illumination + 1.0)
    grad_total = total[: 2 * modes].reshape(probe_modes.shape)
    updated_probe = probe_modes - 0.5 * grad_total / (total[2 * modes] + 1.0)
    return (updated_object, updated_probe)


def solution(mesh):
    return jax.shard_map(
        body,
        mesh=mesh,
        in_specs=(
            P("groups", None, "tile", None),
            P("groups", None, None, None),
            P(("groups", "tile"), None, None),
            P(("groups", "tile")),
            P(("groups", "tile")),
            P("groups"),
        ),
        out_specs=(P("groups", None, "tile", None), P("groups", None, None, None)),
        check_vma=False,
    )
```

profile of v0, /device:TPU:12, one launch (start us, length us, event | category | flops | bytes accessed | tf_op | source)
XLA Modules:
  0.0 123.1 jit_solution(4806429638958689157)
XLA Ops:
  0.6 2.7 %collective-permute-start = (f32[2,2,128,1024]{3,2,1,0:T(8,128)}, f32[2,2,128,1024]{3,2,1,0:T(8,128)S(1)}, u32[]{:S(2)}, u32[]{:S(2)}) collective-permute-start(f32[2,2,128,1024]{3,2,1,0:T(8,128)} %object_ref.1), channel_id=1, source_target_pairs={{1,0},{2,1},{3,2},{4,3},{5,4},{6,5},{7,6},{8,7},{9,8},{10,9},{11,1... | collective-permute-start | bytes 6291464 | tf_op jit(solution)/shard_map/ppermute | solution.py:19
  4.8 2.0 %pad_add_fusion.1.place_ref = s32[13]{0:T(128)} fusion(s32[6]{0:T(128)} %param.14, s32[6]{0:T(128)} %param.13, s32[1]{0:T(128)} %slice.30), kind=kLoop, calls=%fused_computation.21 | loop fusion | flops 26 | bytes 104 | tf_op jit(solution)/shard_map/concatenate | solution.py:203
  6.7 20.5 %collective-permute-done.rim_ref = f32[2,2,128,1024]{3,2,1,0:T(8,128)S(1)} collective-permute-done((f32[2,2,128,1024]{3,2,1,0:T(8,128)}, f32[2,2,128,1024]{3,2,1,0:T(8,128)S(1)}, u32[]{:S(2)}, u32[]{:S(2)}) %collective-permute-start) | collective-permute-done | bytes 2097184 | tf_op jit(solution)/shard_map/ppermute | solution.py:19
  27.2 1.3 %copy-done.3 = f32[2,2,128,1024]{3,2,1,0:T(8,128)} copy-done((f32[2,2,128,1024]{3,2,1,0:T(8,128)}, f32[2,2,128,1024]{3,2,1,0:T(8,128)S(1)}, u32[]{:S(2)}) %copy-start.3) | copy-done | bytes 2097176
  28.5 9.6 %shard_map.113 = (f32[2,2,128,1024]{3,2,1,0:T(8,128)}, f32[2,2,128,1024]{3,2,1,0:T(8,128)}, f32[9,128,128]{2,1,0:T(8,128)}) custom-call(s32[13]{0:T(128)} %pad_add_fusion.1.place_ref, f32[2,2,128,1024]{3,2,1,0:T(8,128)} %object_ref.1, f32[2,2,128,1024]{3,2,1,0:T(8,128)} %copy-done.3, f32[4,2,128,128]{3,2,1,0:T(8,128)} %probe_ref.3, ...), custom_call_target="tpu_custom_call" | custom-call | tf_op jit(solution)/shard_map/pallas_call | solution.py:216
  38.1 1.2 %slice_select_fusion = f32[576,128]{1,0:T(8,128)S(1)} fusion(f32[1152,128]{1,0:T(8,128)} %bitcast.2, pred[]{:T(512)S(6)} %eq.13), kind=kLoop, calls=%fused_computation.6 | loop fusion | flops 73728 | bytes 884737 | tf_op jit(solution)/shard_map/jit(_where)/select_n | solution.py:185
  39.4 18.4 %collective-permute-start.3 = (f32[576,128]{1,0:T(8,128)S(1)}, f32[576,128]{1,0:T(8,128)S(1)}, u32[]{:S(2)}, u32[]{:S(2)}) collective-permute-start(f32[576,128]{1,0:T(8,128)S(1)} %slice_select_fusion), channel_id=1, source_target_pairs={{0,1},{1,0},{2,3},{3,2},{4,5},{5,4},{6,7},{7,6},{8,9},{9,8},{10,11... | collective-permute-start | bytes 884744 | tf_op jit(solution)/shard_map/ppermute | solution.py:186
  57.8 1.2 collective-permute-done.3
  59.0 1.1 select_add_fusion
  60.3 6.1 %collective-permute-done.4 = f32[288,128]{1,0:T(8,128)S(1)} collective-permute-done((f32[288,128]{1,0:T(8,128)S(1)}, f32[288,128]{1,0:T(8,128)S(1)}, u32[]{:S(2)}, u32[]{:S(2)}) %collective-permute-start.4) | collective-permute-done | bytes 147488 | tf_op jit(solution)/shard_map/ppermute | solution.py:186
  66.5 4.3 %collective-permute-done.5 = f32[144,128]{1,0:T(8,128)S(1)} collective-permute-done((f32[144,128]{1,0:T(8,128)S(1)}, f32[144,128]{1,0:T(8,128)S(1)}, u32[]{:S(2)}, u32[]{:S(2)}) %collective-permute-start.5) | collective-permute-done | bytes 73760 | tf_op jit(solution)/shard_map/ppermute | solution.py:186
  70.8 5.3 %collective-permute-start.6 = (f32[144,128]{1,0:T(8,128)S(1)}, f32[144,128]{1,0:T(8,128)S(1)}, u32[]{:S(2)}, u32[]{:S(2)}) collective-permute-start(f32[144,128]{1,0:T(8,128)S(1)} %select_add_fusion.2), channel_id=1, source_target_pairs={{0,8},{1,9},{2,10},{3,11},{4,12},{5,13},{6,14},{7,15},{8,0},{9,1},... | collective-permute-start | bytes 221192 | tf_op jit(solution)/shard_map/ppermute | solution.py:189
  76.1 1.9 %collective-permute-start.1 = (f32[2,2,128,1024]{3,2,1,0:T(8,128)S(1)}, f32[2,2,128,1024]{3,2,1,0:T(8,128)S(1)}, u32[]{:S(2)}, u32[]{:S(2)}) collective-permute-start(f32[2,2,128,1024]{3,2,1,0:T(8,128)S(1)} %copy-done.6), channel_id=1, source_target_pairs={{0,1},{1,2},{2,3},{3,4},{4,5},{5,6},{6,7},{7,8},{8,9},{9,10},{10,1... | collective-permute-start | bytes 6291464 | tf_op jit(solution)/shard_map/ppermute | solution.py:19
  78.6 4.7 %collective-permute-done.7 = f32[144,128]{1,0:T(8,128)S(1)} collective-permute-done((f32[144,128]{1,0:T(8,128)S(1)}, f32[144,128]{1,0:T(8,128)S(1)}, u32[]{:S(2)}, u32[]{:S(2)}) %collective-permute-start.7) | collective-permute-done | bytes 73760 | tf_op jit(solution)/shard_map/ppermute | solution.py:191
  83.3 2.9 %collective-permute-start.8 = (f32[288,128]{1,0:T(8,128)S(1)}, f32[288,128]{1,0:T(8,128)S(1)}, u32[]{:S(2)}, u32[]{:S(2)}) collective-permute-start(f32[288,128]{1,0:T(8,128)S(1)} %pad_maximum_fusion.2), channel_id=1, source_target_pairs={{0,2},{1,3},{2,0},{3,1},{4,6},{5,7},{6,4},{7,5},{8,10},{9,11},{10,... | collective-permute-start | bytes 442376 | tf_op jit(solution)/shard_map/ppermute | solution.py:191
  86.2 20.6 %collective-permute-done.8 = f32[288,128]{1,0:T(8,128)S(1)} collective-permute-done((f32[288,128]{1,0:T(8,128)S(1)}, f32[288,128]{1,0:T(8,128)S(1)}, u32[]{:S(2)}, u32[]{:S(2)}) %collective-permute-start.8) | collective-permute-done | bytes 147488 | tf_op jit(solution)/shard_map/ppermute | solution.py:191
  106.8 2.4 %collective-permute-start.9 = (f32[576,128]{1,0:T(8,128)S(1)}, f32[576,128]{1,0:T(8,128)S(1)}, u32[]{:S(2)}, u32[]{:S(2)}) collective-permute-start(f32[576,128]{1,0:T(8,128)S(1)} %pad_maximum_fusion.1), channel_id=1, source_target_pairs={{0,1},{1,0},{2,3},{3,2},{4,5},{5,4},{6,7},{7,6},{8,9},{9,8},{10,11... | collective-permute-start | bytes 884744 | tf_op jit(solution)/shard_map/ppermute | solution.py:191
  109.2 2.1 %collective-permute-start.2 = (s32[13]{0:T(128)S(1)}, s32[13]{0:T(128)S(1)}, u32[]{:S(2)}, u32[]{:S(2)}) collective-permute-start(s32[13]{0:T(128)S(1)} %copy-done.4), channel_id=1, source_target_pairs={{0,1},{1,2},{2,3},{3,4},{4,5},{5,6},{6,7},{7,8},{8,9},{9,10},{10,1... | collective-permute-start | bytes 164 | tf_op jit(solution)/shard_map/ppermute | solution.py:19
  111.2 3.7 %collective-permute-done.2.before_ref = s32[13]{0:T(128)S(1)} collective-permute-done((s32[13]{0:T(128)S(1)}, s32[13]{0:T(128)S(1)}, u32[]{:S(2)}, u32[]{:S(2)}) %collective-permute-start.2) | collective-permute-done | bytes 84 | tf_op jit(solution)/shard_map/ppermute | solution.py:19
  115.4 2.2 %shard_map.114 = f32[128,1024]{1,0:T(8,128)} custom-call(s32[13]{0:T(128)} %pad_add_fusion.1.place_ref, s32[13]{0:T(128)} %copy-done.5, f32[4,2,128,128]{3,2,1,0:T(8,128)} %probe_ref.3), custom_call_target="tpu_custom_call" | custom-call | tf_op jit(solution)/shard_map/pallas_call | solution.py:209
  117.7 1.2 broadcast_add_fusion
  119.1 0.9 divide_subtract_fusion.1
  119.9 0.9 copy-done
  120.8 2.3 %divide_subtract_fusion = f32[2,2,128,1024]{3,2,1,0:T(8,128)} fusion(f32[2,2,128,1024]{3,2,1,0:T(8,128)S(1)} %copy-done, f32[2,2,128,1024]{3,2,1,0:T(8,128)S(1)} %copy-done.2, f32[2,2,128,1024]{3,2,1,0:T(8,128)S(1)} %collective-permute-done.1, f32[128,1024]{1,0:T(8,128)S(1)} %broadcast_add_fusion), kind=kLoop, calls=%fused_computation | loop fusion | flops 2097152 | bytes 8912896 | tf_op jit(solution)/shard_map/sub | solution.py:229
  (33 shorter events, 2.8 us)
Async XLA Ops:
  0.6 26.6 %collective-permute-start = (f32[2,2,128,1024]{3,2,1,0:T(8,128)}, f32[2,2,128,1024]{3,2,1,0:T(8,128)S(1)}, u32[]{:S(2)}, u32[]{:S(2)}) collective-permute-start(f32[2,2,128,1024]{3,2,1,0:T(8,128)} %object_ref.1), channel_id=1, source_target_pairs={{1,0},{2,1},{3,2},{4,3},{5,4},{6,5},{7,6},{8,7},{9,8},{10,9},{11,1... | collective-permute-start | bytes 6291464 | tf_op jit(solution)/shard_map/ppermute | solution.py:19
  27.2 1.3 %copy-start.3 = (f32[2,2,128,1024]{3,2,1,0:T(8,128)}, f32[2,2,128,1024]{3,2,1,0:T(8,128)S(1)}, u32[]{:S(2)}) copy-start(f32[2,2,128,1024]{3,2,1,0:T(8,128)S(1)} %collective-permute-done.rim_ref) | copy-start | bytes 6291460
  38.1 38.0 %copy-start.6 = (f32[2,2,128,1024]{3,2,1,0:T(8,128)S(1)}, f32[2,2,128,1024]{3,2,1,0:T(8,128)}, u32[]{:S(2)}) copy-start(f32[2,2,128,1024]{3,2,1,0:T(8,128)} %get-tuple-element.6) | copy-start | bytes 6291460
  39.4 19.7 %collective-permute-start.3 = (f32[576,128]{1,0:T(8,128)S(1)}, f32[576,128]{1,0:T(8,128)S(1)}, u32[]{:S(2)}, u32[]{:S(2)}) collective-permute-start(f32[576,128]{1,0:T(8,128)S(1)} %slice_select_fusion), channel_id=1, source_target_pairs={{0,1},{1,0},{2,3},{3,2},{4,5},{5,4},{6,7},{7,6},{8,9},{9,8},{10,11... | collective-permute-start | bytes 884744 | tf_op jit(solution)/shard_map/ppermute | solution.py:186
  57.8 51.4 %copy-start.4 = (s32[13]{0:T(128)S(1)}, s32[13]{0:T(128)}, u32[]{:S(2)}) copy-start(s32[13]{0:T(128)} %pad_add_fusion.1.place_ref) | copy-start | bytes 160
  60.2 6.2 %collective-permute-start.4 = (f32[288,128]{1,0:T(8,128)S(1)}, f32[288,128]{1,0:T(8,128)S(1)}, u32[]{:S(2)}, u32[]{:S(2)}) collective-permute-start(f32[288,128]{1,0:T(8,128)S(1)} %slice_select_fusion.1), channel_id=1, source_target_pairs={{0,2},{1,3},{2,0},{3,1},{4,6},{5,7},{6,4},{7,5},{8,10},{9,11},{10,... | collective-permute-start | bytes 442376 | tf_op jit(solution)/shard_map/ppermute | solution.py:186
  66.4 4.4 %collective-permute-start.5 = (f32[144,128]{1,0:T(8,128)S(1)}, f32[144,128]{1,0:T(8,128)S(1)}, u32[]{:S(2)}, u32[]{:S(2)}) collective-permute-start(f32[144,128]{1,0:T(8,128)S(1)} %slice_select_fusion.2), channel_id=1, source_target_pairs={{0,4},{1,5},{2,6},{3,7},{4,0},{5,1},{6,2},{7,3},{8,12},{9,13},{10,... | collective-permute-start | bytes 221192 | tf_op jit(solution)/shard_map/ppermute | solution.py:186
  70.8 7.6 %collective-permute-start.6 = (f32[144,128]{1,0:T(8,128)S(1)}, f32[144,128]{1,0:T(8,128)S(1)}, u32[]{:S(2)}, u32[]{:S(2)}) collective-permute-start(f32[144,128]{1,0:T(8,128)S(1)} %select_add_fusion.2), channel_id=1, source_target_pairs={{0,8},{1,9},{2,10},{3,11},{4,12},{5,13},{6,14},{7,15},{8,0},{9,1},... | collective-permute-start | bytes 221192 | tf_op jit(solution)/shard_map/ppermute | solution.py:189
  76.1 43.8 %collective-permute-start.1 = (f32[2,2,128,1024]{3,2,1,0:T(8,128)S(1)}, f32[2,2,128,1024]{3,2,1,0:T(8,128)S(1)}, u32[]{:S(2)}, u32[]{:S(2)}) collective-permute-start(f32[2,2,128,1024]{3,2,1,0:T(8,128)S(1)} %copy-done.6), channel_id=1, source_target_pairs={{0,1},{1,2},{2,3},{3,4},{4,5},{5,6},{6,7},{7,8},{8,9},{9,10},{10,1... | collective-permute-start | bytes 6291464 | tf_op jit(solution)/shard_map/ppermute | solution.py:19
  78.5 4.8 %collective-permute-start.7 = (f32[144,128]{1,0:T(8,128)S(1)}, f32[144,128]{1,0:T(8,128)S(1)}, u32[]{:S(2)}, u32[]{:S(2)}) collective-permute-start(f32[144,128]{1,0:T(8,128)S(1)} %add.55), channel_id=1, source_target_pairs={{0,4},{1,5},{2,6},{3,7},{4,0},{5,1},{6,2},{7,3},{8,12},{9,13},{10,... | collective-permute-start | bytes 221192 | tf_op jit(solution)/shard_map/ppermute | solution.py:191
  83.3 23.4 %collective-permute-start.8 = (f32[288,128]{1,0:T(8,128)S(1)}, f32[288,128]{1,0:T(8,128)S(1)}, u32[]{:S(2)}, u32[]{:S(2)}) collective-permute-start(f32[288,128]{1,0:T(8,128)S(1)} %pad_maximum_fusion.2), channel_id=1, source_target_pairs={{0,2},{1,3},{2,0},{3,1},{4,6},{5,7},{6,4},{7,5},{8,10},{9,11},{10,... | collective-permute-start | bytes 442376 | tf_op jit(solution)/shard_map/ppermute | solution.py:191
  106.8 12.2 %copy-start.1 = (f32[4,2,128,128]{3,2,1,0:T(8,128)S(1)}, f32[4,2,128,128]{3,2,1,0:T(8,128)}, u32[]{:S(2)}) copy-start(f32[4,2,128,128]{3,2,1,0:T(8,128)} %probe_ref.3) | copy-start | bytes 1572868
  106.8 12.1 %collective-permute-start.9 = (f32[576,128]{1,0:T(8,128)S(1)}, f32[576,128]{1,0:T(8,128)S(1)}, u32[]{:S(2)}, u32[]{:S(2)}) collective-permute-start(f32[576,128]{1,0:T(8,128)S(1)} %pad_maximum_fusion.1), channel_id=1, source_target_pairs={{0,1},{1,0},{2,3},{3,2},{4,5},{5,4},{6,7},{7,6},{8,9},{9,8},{10,11... | collective-permute-start | bytes 884744 | tf_op jit(solution)/shard_map/ppermute | solution.py:191
  109.2 5.7 %collective-permute-start.2 = (s32[13]{0:T(128)S(1)}, s32[13]{0:T(128)S(1)}, u32[]{:S(2)}, u32[]{:S(2)}) collective-permute-start(s32[13]{0:T(128)S(1)} %copy-done.4), channel_id=1, source_target_pairs={{0,1},{1,2},{2,3},{3,4},{4,5},{5,6},{6,7},{7,8},{8,9},{9,10},{10,1... | collective-permute-start | bytes 164 | tf_op jit(solution)/shard_map/ppermute | solution.py:19
  114.9 0.5 copy-start.5
  117.7 2.2 %copy-start.2 = (f32[2,2,128,1024]{3,2,1,0:T(8,128)S(1)}, f32[2,2,128,1024]{3,2,1,0:T(8,128)}, u32[]{:S(2)}) copy-start(f32[2,2,128,1024]{3,2,1,0:T(8,128)} %get-tuple-element.5) | copy-start | bytes 6291460
  118.9 1.9 %copy-start = (f32[2,2,128,1024]{3,2,1,0:T(8,128)S(1)}, f32[2,2,128,1024]{3,2,1,0:T(8,128)}, u32[]{:S(2)}) copy-start(f32[2,2,128,1024]{3,2,1,0:T(8,128)} %object_ref.1) | copy-start | bytes 6291460
where the time goes:
time: 123 us
  waiting for transfers between devices  61.5 us (50%)
  starting transfers between devices  35.9 us (29%)
  Pallas kernels  11.8 us (10%)
  other arithmetic  9.63 us (8%)
  local copies, waits for them, and re-layouts  3.41 us (3%)
    ppermute x3, waiting for transfers between devices, all_sum(): got = lax.ppermute(value, axis, pairs)  25.3 us
    ppermute x3, waiting for transfers between devices, passed_along(): lax.ppermute(value, axis, [(source, source + steps) for source in range(l...  24.1 us
    ppermute x3, starting transfers between devices, all_sum(): value = kept + lax.ppermute(sent, axis, pairs)  18.6 us
    ppermute x3, waiting for transfers between devices, all_sum(): value = kept + lax.ppermute(sent, axis, pairs)  11.6 us
    pallas_call x1, Pallas kernels, body(): pl.pallas_call(gradient_kernel, out_shape=(jax.ShapeDtypeStruct(object_fi...  9.61 us
    ppermute x3, starting transfers between devices, passed_along(): lax.ppermute(value, axis, [(source, source + steps) for source in range(l...  6.7 us
    ppermute x3, starting transfers between devices, all_sum(): got = lax.ppermute(value, axis, pairs)  5.32 us
    ppermute x1, starting transfers between devices, all_sum(): value = value + lax.ppermute(value, axis, pairs)  5.3 us
  transfers between devices with their start and end apart: 10, of which 8 were waited for; matrix products, arithmetic and copies ran while one was open for 5% of the time, Pallas kernels for 2%

commit v1 on v0

v1 whole, which is shorter than its diff:
```python
import functools
import math

import jax
import jax.numpy as jnp
import ml_dtypes
import numpy as np
from jax import lax
from jax.experimental import pallas as pl
from jax.experimental.pallas import tpu as pltpu
from jax.sharding import PartitionSpec as P

F32, BF16 = jnp.float32, jnp.bfloat16


def passed_along(value, axis, steps):
    count = lax.axis_size(axis)
    leading, last = (max(0, -steps), min(count, count - steps))
    return lax.ppermute(value, axis, [(source, source + steps) for source in range(leading, last)])


def complex_tables(width):
    index = np.arange(width)
    angle = 2.0 * math.pi / width * (index[:, None] * index[None, :] % width)
    dft = np.exp(-1j * angle) / math.sqrt(width)
    frequency = np.where(index < width // 2, index, index - width).astype(np.float64)
    phase = np.exp(-0.5j * math.pi / width * frequency**2)
    return dft, np.conj(dft) @ (phase[:, None] * dft)


def real_forms(table):
    re, im = table.real, table.imag
    right = np.block([[re, im], [-im, re]])
    left = np.block([[re, -im], [im, re]])

    def parts(matrix):
        high = matrix.astype(ml_dtypes.bfloat16)
        low = (matrix - high.astype(np.float64)).astype(ml_dtypes.bfloat16)
        return high, low

    right_high, right_low = parts(right)
    left_high, left_low = parts(left)
    return np.stack([right_high, right_low]), np.concatenate([left_high, left_low], 0)


def halves(value):
    high = value.astype(BF16)
    return high, (value - high.astype(F32)).astype(BF16)


def dot(left, right):
    return jnp.dot(left, right, preferred_element_type=F32)


def right_stage(blocks, right_ref):
    rows = jnp.concatenate([jnp.concatenate(pair, 1) for pair in blocks], 0)
    high, low = halves(rows)
    table = jnp.concatenate([right_ref[0], right_ref[0], right_ref[1]], 0)
    return dot(jnp.concatenate([high, low, high], 1), table)


def left_stage(first, width, left_ref):
    modes = first.shape[0] // width
    cols = jnp.concatenate(
        [
            jnp.concatenate(
                [first[m * width : (m + 1) * width, part * width : (part + 1) * width] for m in range(modes)], 1
            )
            for part in range(2)
        ],
        0,
    )
    high, low = halves(cols)
    table = jnp.concatenate([left_ref[: 2 * width], left_ref[: 2 * width], left_ref[2 * width :]], 1)
    second = dot(table, jnp.concatenate([high, low, high], 0))
    return [
        (second[:width, m * width : (m + 1) * width], second[width:, m * width : (m + 1) * width])
        for m in range(modes)
    ]


def two_sided(blocks, right_ref, left_ref, group=2):
    width = blocks[0][0].shape[0]
    firsts = [right_stage(blocks[i : i + group], right_ref) for i in range(0, len(blocks), group)]
    return [block for first in firsts for block in left_stage(first, width, left_ref)]


def times(left, right):
    return left[0] * right[0] - left[1] * right[1], left[0] * right[1] + left[1] * right[0]


def window_place(place_ref, slot, slots, width, blocks):
    row_start, col_start = place_ref[slot], place_ref[slots + slot]
    block = col_start // width
    shift = col_start - block * width
    lane = lax.broadcasted_iota(jnp.int32, (width, width), 1)
    row = lax.broadcasted_iota(jnp.int32, (width, width), 0)
    first = pl.ds(pl.multiple_of(block * width, width), width)
    second = pl.ds(pl.multiple_of(jnp.minimum(block + 1, blocks - 1) * width, width), width)
    return row >= row_start, lane >= shift, shift, first, second


def load_kernel(*refs):
    count = len(refs) // 2
    for source, target in zip(refs[:count], refs[count:]):
        target[...] = source[...]


def strip_kernel(start, before_ref, object_ref, strip_ref):
    size, planes, width, _ = strip_ref.shape
    slots = before_ref.shape[0] // 2
    for i in range(size):
        _, in_first, _, first, second = window_place(before_ref, start + i, slots, width, object_ref.shape[-1] // width)
        for plane in range(planes):
            strip_ref[i, plane] = jnp.where(
                in_first, object_ref[plane // 2, plane % 2, :, first], object_ref[plane // 2, plane % 2, :, second]
            )


PAIR = 2


def gradient_kernel(
    start, axis, counts_ref, place_ref, object_ref, probe_ref, measured_ref, fr_ref, fl_ref, pr_ref, pl_ref, *refs
):
    last_call = start > 0
    tile = lax.axis_index(axis)
    count = counts_ref[tile]
    modes, _, width, _ = probe_ref.shape
    slots = measured_ref.shape[0]
    rim_refs, refs = refs[: 1 + last_call], refs[1 + last_call :]
    rims = [(ref, i) for ref in rim_refs for i in range(ref.shape[0])]
    if last_call:
        before_ref, grad_ref, kept_ref, sent_ref, sums_ref = refs
        sums_ref[...] = before_ref[...]
    else:
        grad_ref, sums_ref = refs
        sums_ref[...] = jnp.zeros(sums_ref.shape, F32)
    probe = [(probe_ref[m, 0], probe_ref[m, 1]) for m in range(modes)]

    def visit(base):
        places = [
            window_place(place_ref, start + base + i, slots, width, object_ref.shape[-1] // width) for i in range(PAIR)
        ]

        def window(i, s, part):
            in_own, in_first, shift, first, second = places[i]
            own = jnp.where(in_first, object_ref[s, part, :, first], object_ref[s, part, :, second])
            rim_ref, at = rims[start + base + i]
            stored = jnp.where(in_own, own, rim_ref[at, 2 * s + part])
            stored = pltpu.roll(stored, lax.rem(width - place_ref[start + base + i], width), 0)
            return pltpu.roll(stored, lax.rem(width - shift, width), 1)

        def put(i, s, part, value):
            value = pltpu.roll(value, place_ref[start + base + i], 0)
            grad_ref[base + i, 2 * s + part] = pltpu.roll(value, places[i][2], 1)

        def split(blocks):
            return [blocks[i * modes : (i + 1) * modes] for i in range(PAIR)]

        ones = [(window(i, 0, 0), window(i, 0, 1)) for i in range(PAIR)]
        moved = split(two_sided([times(p, one) for one in ones for p in probe], pr_ref, pl_ref))
        twos = [(window(i, 1, 0), window(i, 1, 1)) for i in range(PAIR)]
        far = split(two_sided([times(w, two) for ws, two in zip(moved, twos) for w in ws], fr_ref, fl_ref))
        back = []
        for i in range(PAIR):
            intensity = sum(re * re + im * im for re, im in far[i])
            residue = 2.0 * (intensity - measured_ref[start + base + i])
            back += [(residue * re, -(residue * im)) for re, im in far[i]]
        back = split(two_sided(back, fr_ref, fl_ref))
        last = split(two_sided([times(g, two) for gs, two in zip(back, twos) for g in gs], pr_ref, pl_ref))
        for i in range(PAIR):
            terms = [times(w, g) for w, g in zip(moved[i], back[i])]
            put(i, 1, 0, sum(t[0] for t in terms))
            put(i, 1, 1, -sum(t[1] for t in terms))
            terms = [times(p, g) for p, g in zip(probe, last[i])]
            put(i, 0, 0, sum(t[0] for t in terms))
            put(i, 0, 1, -sum(t[1] for t in terms))
        live = [start + base + i < count for i in range(PAIR)]

        def summed(values):
            return sum(jnp.where(alive, value, 0.0) for alive, value in zip(live, values))

        for m in range(modes):
            grads = [times(one, g[m]) for one, g in zip(ones, last)]
            for part, sign in ((0, 1.0), (1, -1.0)):
                rows = pl.ds((2 * m + part) * width, width)
                sums_ref[rows] += sign * summed(g[part] for g in grads)
        sums_ref[pl.ds(2 * modes * width, width)] += summed(re * re + im * im for re, im in ones)

    for base in range(0, grad_ref.shape[0], PAIR):
        pl.when(start + base < count)(functools.partial(visit, base))
    if last_call:
        half = kept_ref.shape[0]
        side = lax.rem(tile, 2)
        kept_ref[...] = sums_ref[pl.ds(pl.multiple_of(side * half, 8), half)]
        sent_ref[...] = sums_ref[pl.ds(pl.multiple_of((1 - side) * half, 8), half)]


def add_windows(target_ref, counts_ref, place_ref, before_ref, axis, window_of):
    tile = lax.axis_index(axis)
    width, slots = target_ref.shape[0], place_ref.shape[0] // 2
    target_ref[...] = jnp.zeros(target_ref.shape, F32)
    for slot in range(slots):
        for own in (True, False):
            ref = place_ref if own else before_ref
            count = counts_ref[tile] if own else jnp.where(tile > 0, counts_ref[jnp.maximum(tile - 1, 0)], 0)

            @pl.when(slot < count)
            def _():
                in_own, in_first, shift, first, second = window_place(
                    ref, slot, slots, width, target_ref.shape[1] // width
                )
                value = window_of(ref, slot, own, shift)
                wanted = in_own if own else jnp.logical_not(in_own)
                value = jnp.where(wanted, value, 0.0)
                target_ref[:, first] += jnp.where(in_first, value, 0.0)
                target_ref[:, second] += jnp.where(in_first, 0.0, value)


def light_kernel(axis, counts_ref, place_ref, before_ref, probe_ref, lit_ref):
    modes = probe_ref.shape[0]
    power = sum(probe_ref[m, part] * probe_ref[m, part] for m in range(modes) for part in range(2))

    def window_of(ref, slot, own, shift):
        return pltpu.roll(pltpu.roll(power, ref[slot], 0), shift, 1)

    add_windows(lit_ref, counts_ref, place_ref, before_ref, axis, window_of)
    lit_ref[...] = 0.5 / (lit_ref[...] + 1.0)


def update_kernel(axis, sizes, counts_ref, place_ref, before_ref, object_ref, lit_ref, *refs):
    out_ref, sum_ref = refs[2 * len(sizes) :]
    plane = pl.program_id(0)
    parts = [(n, i) for n, size in enumerate(sizes) for i in range(size)]

    def window_of(ref, slot, own, shift):
        n, i = parts[slot]
        return refs[n + (0 if own else len(sizes))][i, plane]

    add_windows(sum_ref, counts_ref, place_ref, before_ref, axis, window_of)
    out_ref[0, 0] = object_ref[plane // 2, plane % 2] - sum_ref[...] * lit_ref[...]


def probe_kernel(axis, mine_ref, got_ref, probe_ref, out_ref, total_ref):
    modes, _, width, _ = probe_ref.shape
    half = mine_ref.shape[0]
    side = lax.rem(lax.axis_index(axis), 2)
    total_ref[pl.ds(pl.multiple_of(side * half, 8), half)] = mine_ref[...]
    total_ref[pl.ds(pl.multiple_of((1 - side) * half, 8), half)] = got_ref[...]
    scale = 0.5 / (total_ref[pl.ds(2 * modes * width, width)] + 1.0)
    for m in range(modes):
        for part in range(2):
            out_ref[m, part] = probe_ref[m, part] - total_ref[pl.ds((2 * m + part) * width, width)] * scale


def after(value, *others):
    return lax.optimization_barrier((value, *others))[0]


def halve_kernel(axis, bit, kept_ref, got_ref, next_kept_ref, next_sent_ref):
    half = next_kept_ref.shape[0]
    side = lax.rem(lax.axis_index(axis) // bit, 2)
    for ref, which in ((next_kept_ref, side), (next_sent_ref, 1 - side)):
        rows = pl.ds(pl.multiple_of(which * half, 8), half)
        ref[...] = kept_ref[rows] + got_ref[rows]


def add_kernel(kept_ref, got_ref, out_ref):
    out_ref[...] = kept_ref[...] + got_ref[...]


def join_kernel(axis, bit, mine_ref, got_ref, out_ref):
    half = mine_ref.shape[0]
    side = lax.rem(lax.axis_index(axis) // bit, 2)
    out_ref[pl.ds(pl.multiple_of(side * half, 8), half)] = mine_ref[...]
    out_ref[pl.ds(pl.multiple_of((1 - side) * half, 8), half)] = got_ref[...]


def half_sum(kept, sent, axis, beside, joins):
    count = lax.axis_size(axis)
    bits = [1 << b for b in range(count.bit_length() - 1)]
    vmem = pl.BlockSpec(memory_space=pltpu.VMEM)
    width = kept.shape[1]

    def exchanged(value, bit, step):
        value = after(value, *joins.get(step, ()))
        got = lax.ppermute(value, axis, [(i, i ^ bit) for i in range(count)])
        beside.get(step, lambda reached: None)(got)
        return pltpu.with_memory_space_constraint(got, pltpu.VMEM)

    def local(kernel, rows, *operands):
        return pl.pallas_call(
            kernel,
            out_shape=[pltpu.VMEM((n, width), F32) for n in rows],
            in_specs=[vmem] * 2,
            out_specs=[vmem] * len(rows),
            compiler_params=pltpu.CompilerParams(vmem_limit_bytes=4 << 20),
        )(*operands)

    got = exchanged(sent, bits[0], 0)
    halved = bits[1:3]
    for step, bit in enumerate(bits[1:], 1):
        rows = kept.shape[0]
        if bit in halved:
            kept, sent = local(functools.partial(halve_kernel, axis, bit), (rows // 2,) * 2, kept, got)
        else:
            (kept,) = local(add_kernel, (rows,), kept, got)
            sent = kept
        got = exchanged(sent, bit, step)
    (value,) = local(add_kernel, kept.shape[:1], kept, got)
    for step, bit in enumerate(reversed(halved), len(bits)):
        got = exchanged(value, bit, step)
        (value,) = local(functools.partial(join_kernel, axis, bit), (2 * value.shape[0],), value, got)
    return value, exchanged(value, bits[0], len(bits) + len(halved))


def body(object_field, probe_modes, measured, row_offset, col_offset, tile_counts):
    axis = "tile"
    slices, _, tile_rows, tile_cols = object_field.shape
    modes, _, width, _ = probe_modes.shape
    slots = measured.shape[0]
    dft, move = complex_tables(width)
    smem = pl.BlockSpec(memory_space=pltpu.SMEM)
    vmem = pl.BlockSpec(memory_space=pltpu.VMEM)
    params = pltpu.CompilerParams(vmem_limit_bytes=16 << 20)

    def held(value):
        return pltpu.with_memory_space_constraint(value, pltpu.VMEM)

    def held_like(value):
        return pltpu.VMEM(value.shape, value.dtype)

    place = jnp.concatenate([row_offset, col_offset])
    before = passed_along(place, axis, 1)
    loaded = [jnp.asarray(t) for t in (*real_forms(dft), *real_forms(move))]
    loaded = [object_field, probe_modes, measured, *loaded]
    objects, probe, patterns, *tables = pl.pallas_call(
        load_kernel,
        out_shape=tuple(map(held_like, loaded)),
        in_specs=[vmem] * len(loaded),
        out_specs=(vmem,) * len(loaded),
        compiler_params=params,
    )(*loaded)
    sizes = (PAIR, slots - PAIR)

    def windows(size):
        return pltpu.VMEM((size, 2 * slices, width, width), F32)

    rims, strip = [], before
    for start, size in ((0, slots // 2), (slots // 2, slots - slots // 2)):
        strip = pl.pallas_call(
            functools.partial(strip_kernel, start),
            out_shape=windows(size),
            in_specs=[smem, vmem],
            out_specs=vmem,
            compiler_params=params,
        )(after(before, strip), objects)
        rims.append(held(passed_along(strip, axis, -1)))
    lit = pl.pallas_call(
        functools.partial(light_kernel, axis),
        out_shape=pltpu.VMEM((tile_rows, tile_cols), F32),
        in_specs=[smem, smem, smem, vmem],
        out_specs=vmem,
        compiler_params=params,
    )(tile_counts, place, after(before, strip), probe)
    rows = (2 * modes + 1) * width
    whole, half = pltpu.VMEM((rows, width), F32), pltpu.VMEM((rows // 2, width), F32)
    common = (probe, patterns, *tables)
    grad_a, sums = pl.pallas_call(
        functools.partial(gradient_kernel, 0, axis),
        out_shape=(windows(sizes[0]), whole),
        in_specs=[smem] * 2 + [vmem] * 8,
        out_specs=(vmem,) * 2,
        compiler_params=params,
    )(tile_counts, after(place, lit), objects, *common, rims[0])
    arrived_a = passed_along(grad_a, axis, 1)
    grad_b, kept, sent = pl.pallas_call(
        functools.partial(gradient_kernel, sizes[0], axis),
        out_shape=(windows(sizes[1]), half, half),
        in_specs=[smem] * 2 + [vmem] * 10,
        out_specs=(vmem,) * 3,
        scratch_shapes=[whole],
        compiler_params=params,
        cost_estimate=pl.CostEstimate(flops=1, bytes_accessed=40 << 20, transcendentals=0),
    )(tile_counts, place, objects, *common, *rims, sums)
    arrived = [arrived_a]

    def send_rest(reached):
        arrived.append(passed_along(after(grad_b, reached), axis, 1))

    mine, got = half_sum(kept, sent, axis, {1: send_rest}, {1: arrived[:1], 5: arrived})
    updated_object = pl.pallas_call(
        functools.partial(update_kernel, axis, sizes),
        grid=(2 * slices,),
        out_shape=jax.ShapeDtypeStruct(object_field.shape, F32),
        in_specs=[smem] * 3 + [vmem] * 6,
        out_specs=pl.BlockSpec((1, 1, tile_rows, tile_cols), lambda plane: (plane // 2, plane % 2, 0, 0)),
        scratch_shapes=[pltpu.VMEM((tile_rows, tile_cols), F32)],
        compiler_params=params,
        cost_estimate=pl.CostEstimate(flops=1, bytes_accessed=12 << 20, transcendentals=0),
    )(tile_counts, place, before, objects, lit, grad_a, grad_b, *map(held, arrived))
    updated_probe = pl.pallas_call(
        functools.partial(probe_kernel, axis),
        out_shape=jax.ShapeDtypeStruct(probe_modes.shape, F32),
        in_specs=[vmem] * 3,
        out_specs=vmem,
        scratch_shapes=[pltpu.VMEM((rows, width), F32)],
        compiler_params=params,
    )(mine, got, probe)
    return (updated_object, updated_probe)


def solution(mesh):
    return jax.shard_map(
        body,
        mesh=mesh,
        in_specs=(
            P("groups", None, "tile", None),
            P("groups", None, None, None),
            P(("groups", "tile"), None, None),
            P(("groups", "tile")),
            P(("groups", "tile")),
            P("groups"),
        ),
        out_specs=(P("groups", None, "tile", None), P("groups", None, None, None)),
        check_vma=False,
    )
```

time: 123 us -> 88.6 us (0.72)
  the two profiles are of different devices: /device:TPU:12 before, /device:TPU:0 now
where the time goes in v1:
time: 88.6 us; the launch traced here: 88.9 us
  starting transfers between devices  43.8 us (49%)
  waiting for transfers between devices  23.5 us (27%)
  Pallas kernels  12.6 us (14%)
  local copies, waits for them, and re-layouts  7.43 us (8%)
    ppermute x7, starting transfers between devices, exchanged(): got = lax.ppermute(value, axis, [(i, i ^ bit) for i in range(count)])  25.7 us
    ppermute x7, waiting for transfers between devices, exchanged(): got = lax.ppermute(value, axis, [(i, i ^ bit) for i in range(count)])  21.5 us
    ppermute x5, starting transfers between devices, passed_along(): lax.ppermute(value, axis, [(source, source + steps) for source in range(l...  18.1 us
    unnamed x16, local copies, waits for them, and re-layouts  7.43 us
    pallas_call x1, Pallas kernels, body(): pl.pallas_call(functools.partial(gradient_kernel, 0, axis), out_shape=(wi...  5.18 us
    pallas_call x1, Pallas kernels, body(): pl.pallas_call(functools.partial(update_kernel, axis, sizes), grid=(2 * s...  2.88 us
    ppermute x5, waiting for transfers between devices, passed_along(): lax.ppermute(value, axis, [(source, source + steps) for source in range(l...  2.04 us
  transfers between devices with their start and end apart: 12, of which 7 were waited for; matrix products, arithmetic and copies ran while one was open for 0% of the time, Pallas kernels for 12%

profile of v1, /device:TPU:0, one launch (start us, length us, event | category | flops | bytes accessed | tf_op | source)
XLA Modules:
  0.0 88.9 jit_solution(3467489063356262949)
XLA Ops:
  1.4 2.3 %collective-permute-start = (s32[12]{0:T(128)S(1)}, s32[12]{0:T(128)S(1)}, u32[]{:S(2)}, u32[]{:S(2)}) collective-permute-start(s32[12]{0:T(128)S(1)} %pad_add_fusion.place_ref), channel_id=1, source_target_pairs={{0,1},{1,2},{2,3},{3,4},{4,5},{5,6},{6,7},{7,8},{8,9},{9,10},{10,1... | collective-permute-start | bytes 152 | tf_op jit(solution)/shard_map/ppermute | solution.py:19
  3.7 1.6 %copy-done = f32[2,2,128,1024]{3,2,1,0:T(8,128)S(1)} copy-done((f32[2,2,128,1024]{3,2,1,0:T(8,128)S(1)}, f32[2,2,128,1024]{3,2,1,0:T(8,128)}, u32[]{:S(2)}) %copy-start) | copy-done | bytes 2097176
  5.3 1.0 %copy-done.1 = f32[4,2,128,128]{3,2,1,0:T(8,128)S(1)} copy-done((f32[4,2,128,128]{3,2,1,0:T(8,128)S(1)}, f32[4,2,128,128]{3,2,1,0:T(8,128)}, u32[]{:S(2)}) %copy-start.1) | copy-done | bytes 524312
  6.4 1.0 %copy-done.2 = f32[6,128,128]{2,1,0:T(8,128)S(1)} copy-done((f32[6,128,128]{2,1,0:T(8,128)S(1)}, f32[6,128,128]{2,1,0:T(8,128)}, u32[]{:S(2)}) %copy-start.2) | copy-done | bytes 393240
  7.4 0.9 %copy-done.3 = bf16[512,256]{1,0:T(8,128)(2,1)S(1)} copy-done((bf16[512,256]{1,0:T(8,128)(2,1)S(1)}, bf16[512,256]{1,0:T(8,128)(2,1)}, u32[]{:S(2)}) %copy-start.3) | copy-done | bytes 262168
  9.3 0.9 %copy-done.5 = bf16[512,256]{1,0:T(8,128)(2,1)S(1)} copy-done((bf16[512,256]{1,0:T(8,128)(2,1)S(1)}, bf16[512,256]{1,0:T(8,128)(2,1)}, u32[]{:S(2)}) %copy-start.5) | copy-done | bytes 262168
  12.2 1.3 %collective-permute-start.1 = (f32[3,4,128,128]{3,2,1,0:T(8,128)S(1)}, f32[3,4,128,128]{3,2,1,0:T(8,128)S(1)}, u32[]{:S(2)}, u32[]{:S(2)}) collective-permute-start(f32[3,4,128,128]{3,2,1,0:T(8,128)S(1)} %shard_map.114), channel_id=1, source_target_pairs={{1,0},{2,1},{3,2},{4,3},{5,4},{6,5},{7,6},{8,7},{9,8},{10,9},{11,1... | collective-permute-start | bytes 2359304 | tf_op jit(solution)/shard_map/ppermute | solution.py:19
  14.3 1.3 %collective-permute-start.2 = (f32[3,4,128,128]{3,2,1,0:T(8,128)S(1)}, f32[3,4,128,128]{3,2,1,0:T(8,128)S(1)}, u32[]{:S(2)}, u32[]{:S(2)}) collective-permute-start(f32[3,4,128,128]{3,2,1,0:T(8,128)S(1)} %shard_map.115), channel_id=1, source_target_pairs={{1,0},{2,1},{3,2},{4,3},{5,4},{6,5},{7,6},{8,7},{9,8},{10,9},{11,1... | collective-permute-start | bytes 2359304 | tf_op jit(solution)/shard_map/ppermute | solution.py:19
  16.5 2.0 %collective-permute-done.1.refs_0_ = f32[3,4,128,128]{3,2,1,0:T(8,128)S(1)} collective-permute-done((f32[3,4,128,128]{3,2,1,0:T(8,128)S(1)}, f32[3,4,128,128]{3,2,1,0:T(8,128)S(1)}, u32[]{:S(2)}, u32[]{:S(2)}) %collective-permute-start.1) | collective-permute-done | bytes 786464 | tf_op jit(solution)/shard_map/ppermute | solution.py:19
  18.5 5.2 %shard_map.117 = (f32[2,4,128,128]{3,2,1,0:T(8,128)S(1)}, f32[1152,128]{1,0:T(8,128)S(1)}) custom-call(s32[16]{0:T(128)S(1)} %copy-done.7, s32[12]{0:T(128)S(1)} %pad_add_fusion.place_ref, f32[2,2,128,1024]{3,2,1,0:T(8,128)S(1)} %get-tuple-element.25.object_ref, f32[4,2,128,128]{3,2,1,0:T(8,128)S(1)} %get-tuple-element.29.probe_ref, ...), custom_call_target="tpu_custom_call" | custom-call | tf_op jit(solution)/shard_map/pallas_call | solution.py:370
  23.7 11.6 %collective-permute-start.3 = (f32[2,4,128,128]{3,2,1,0:T(8,128)S(1)}, f32[2,4,128,128]{3,2,1,0:T(8,128)S(1)}, u32[]{:S(2)}, u32[]{:S(2)}) collective-permute-start(f32[2,4,128,128]{3,2,1,0:T(8,128)S(1)} %get-tuple-element.36.refs_0_), channel_id=1, source_target_pairs={{0,1},{1,2},{2,3},{3,4},{4,5},{5,6},{6,7},{7,8},{8,9},{9,10},{10,1... | collective-permute-start | bytes 1572872 | tf_op jit(solution)/shard_map/ppermute | solution.py:19
  36.1 5.9 %collective-permute-start.4 = (f32[576,128]{1,0:T(8,128)S(1)}, f32[576,128]{1,0:T(8,128)S(1)}, u32[]{:S(2)}, u32[]{:S(2)}) collective-permute-start(f32[576,128]{1,0:T(8,128)S(1)} %get-tuple-element.40), channel_id=1, source_target_pairs={{0,1},{1,0},{2,3},{3,2},{4,5},{5,4},{6,7},{7,6},{8,9},{9,8},{10,11... | collective-permute-start | bytes 884744 | tf_op jit(solution)/shard_map/ppermute | solution.py:288
  42.0 1.2 %collective-permute-done.4.got_ref = f32[576,128]{1,0:T(8,128)S(1)} collective-permute-done((f32[576,128]{1,0:T(8,128)S(1)}, f32[576,128]{1,0:T(8,128)S(1)}, u32[]{:S(2)}, u32[]{:S(2)}) %collective-permute-start.4) | collective-permute-done | bytes 294944 | tf_op jit(solution)/shard_map/ppermute | solution.py:288
  43.3 6.1 %collective-permute-start.5 = (f32[288,128]{1,0:T(8,128)S(1)}, f32[288,128]{1,0:T(8,128)S(1)}, u32[]{:S(2)}, u32[]{:S(2)}) collective-permute-start(f32[288,128]{1,0:T(8,128)S(1)} %get-tuple-element.42), channel_id=1, source_target_pairs={{0,2},{1,3},{2,0},{3,1},{4,6},{5,7},{6,4},{7,5},{8,10},{9,11},{10,... | collective-permute-start | bytes 442376 | tf_op jit(solution)/shard_map/ppermute | solution.py:288
  49.4 4.1 %collective-permute-done.5.got_ref = f32[288,128]{1,0:T(8,128)S(1)} collective-permute-done((f32[288,128]{1,0:T(8,128)S(1)}, f32[288,128]{1,0:T(8,128)S(1)}, u32[]{:S(2)}, u32[]{:S(2)}) %collective-permute-start.5) | collective-permute-done | bytes 147488 | tf_op jit(solution)/shard_map/ppermute | solution.py:288
  53.5 1.6 %collective-permute-start.6 = (f32[4,4,128,128]{3,2,1,0:T(8,128)S(1)}, f32[4,4,128,128]{3,2,1,0:T(8,128)S(1)}, u32[]{:S(2)}, u32[]{:S(2)}) collective-permute-start(f32[4,4,128,128]{3,2,1,0:T(8,128)S(1)} %get-tuple-element.43.refs_1_), channel_id=1, source_target_pairs={{0,1},{1,2},{2,3},{3,4},{4,5},{5,6},{6,7},{7,8},{8,9},{9,10},{10,1... | collective-permute-start | bytes 3145736 | tf_op jit(solution)/shard_map/ppermute | solution.py:19
  55.2 3.2 %collective-permute-start.7 = (f32[144,128]{1,0:T(8,128)S(1)}, f32[144,128]{1,0:T(8,128)S(1)}, u32[]{:S(2)}, u32[]{:S(2)}) collective-permute-start(f32[144,128]{1,0:T(8,128)S(1)} %get-tuple-element.46), channel_id=1, source_target_pairs={{0,4},{1,5},{2,6},{3,7},{4,0},{5,1},{6,2},{7,3},{8,12},{9,13},{10,... | collective-permute-start | bytes 221192 | tf_op jit(solution)/shard_map/ppermute | solution.py:288
  58.4 2.3 %collective-permute-done.7.got_ref = f32[144,128]{1,0:T(8,128)S(1)} collective-permute-done((f32[144,128]{1,0:T(8,128)S(1)}, f32[144,128]{1,0:T(8,128)S(1)}, u32[]{:S(2)}, u32[]{:S(2)}) %collective-permute-start.7) | collective-permute-done | bytes 73760 | tf_op jit(solution)/shard_map/ppermute | solution.py:288
  60.7 2.3 %collective-permute-start.8 = (f32[144,128]{1,0:T(8,128)S(1)}, f32[144,128]{1,0:T(8,128)S(1)}, u32[]{:S(2)}, u32[]{:S(2)}) collective-permute-start(f32[144,128]{1,0:T(8,128)S(1)} %shard_map.122.kept_ref), channel_id=1, source_target_pairs={{0,8},{1,9},{2,10},{3,11},{4,12},{5,13},{6,14},{7,15},{8,0},{9,1},... | collective-permute-start | bytes 221192 | tf_op jit(solution)/shard_map/ppermute | solution.py:288
  63.1 5.4 %collective-permute-done.8.got_ref = f32[144,128]{1,0:T(8,128)S(1)} collective-permute-done((f32[144,128]{1,0:T(8,128)S(1)}, f32[144,128]{1,0:T(8,128)S(1)}, u32[]{:S(2)}, u32[]{:S(2)}) %collective-permute-start.8) | collective-permute-done | bytes 73760 | tf_op jit(solution)/shard_map/ppermute | solution.py:288
  69.0 3.8 %collective-permute-done.9.got_ref = f32[144,128]{1,0:T(8,128)S(1)} collective-permute-done((f32[144,128]{1,0:T(8,128)S(1)}, f32[144,128]{1,0:T(8,128)S(1)}, u32[]{:S(2)}, u32[]{:S(2)}) %collective-permute-start.9) | collective-permute-done | bytes 73760 | tf_op jit(solution)/shard_map/ppermute | solution.py:288
  73.5 4.6 %collective-permute-done.10.got_ref = f32[288,128]{1,0:T(8,128)S(1)} collective-permute-done((f32[288,128]{1,0:T(8,128)S(1)}, f32[288,128]{1,0:T(8,128)S(1)}, u32[]{:S(2)}, u32[]{:S(2)}) %collective-permute-start.10) | collective-permute-done | bytes 147488 | tf_op jit(solution)/shard_map/ppermute | solution.py:288
  78.1 7.0 %collective-permute-start.11 = (f32[576,128]{1,0:T(8,128)S(1)}, f32[576,128]{1,0:T(8,128)S(1)}, u32[]{:S(2)}, u32[]{:S(2)}) collective-permute-start(f32[576,128]{1,0:T(8,128)S(1)} %shard_map.125.mine_ref), channel_id=1, source_target_pairs={{0,1},{1,0},{2,3},{3,2},{4,5},{5,4},{6,7},{7,6},{8,9},{9,8},{10,11... | collective-permute-start | bytes 884744 | tf_op jit(solution)/shard_map/ppermute | solution.py:288
  85.1 2.9 %shard_map.120 = f32[2,2,128,1024]{3,2,1,0:T(8,128)} custom-call(s32[16]{0:T(128)S(1)} %copy-done.7, s32[12]{0:T(128)S(1)} %pad_add_fusion.place_ref, s32[12]{0:T(128)S(1)} %collective-permute-done.before_ref, f32[2,2,128,1024]{3,2,1,0:T(8,128)S(1)} %get-tuple-element.25.object_ref, f32[128,1024]{1,0:T(8,128)S(1)} %shard_map.116.lit_ref, ...), custom_call_target="tpu_custom_call" | custom-call | flops 1 | bytes 12582912 | tf_op jit(solution)/shard_map/pallas_call | solution.py:393
  (31 shorter events, 8.4 us)
Async XLA Ops:
  1.4 10.1 %collective-permute-start = (s32[12]{0:T(128)S(1)}, s32[12]{0:T(128)S(1)}, u32[]{:S(2)}, u32[]{:S(2)}) collective-permute-start(s32[12]{0:T(128)S(1)} %pad_add_fusion.place_ref), channel_id=1, source_target_pairs={{0,1},{1,2},{2,3},{3,4},{4,5},{5,6},{6,7},{7,8},{8,9},{9,10},{10,1... | collective-permute-start | bytes 152 | tf_op jit(solution)/shard_map/ppermute | solution.py:19
  3.7 1.6 %copy-start = (f32[2,2,128,1024]{3,2,1,0:T(8,128)S(1)}, f32[2,2,128,1024]{3,2,1,0:T(8,128)}, u32[]{:S(2)}) copy-start(f32[2,2,128,1024]{3,2,1,0:T(8,128)} %refs_0_.1) | copy-start | bytes 6291460
  5.3 1.0 %copy-start.1 = (f32[4,2,128,128]{3,2,1,0:T(8,128)S(1)}, f32[4,2,128,128]{3,2,1,0:T(8,128)}, u32[]{:S(2)}) copy-start(f32[4,2,128,128]{3,2,1,0:T(8,128)} %refs_1_.1) | copy-start | bytes 1572868
  6.4 1.0 %copy-start.2 = (f32[6,128,128]{2,1,0:T(8,128)S(1)}, f32[6,128,128]{2,1,0:T(8,128)}, u32[]{:S(2)}) copy-start(f32[6,128,128]{2,1,0:T(8,128)} %refs_2_.1) | copy-start | bytes 1179652
  7.4 0.9 %copy-start.3 = (bf16[512,256]{1,0:T(8,128)(2,1)S(1)}, bf16[512,256]{1,0:T(8,128)(2,1)}, u32[]{:S(2)}) copy-start(bf16[512,256]{1,0:T(8,128)(2,1)} %constant.11.clone.refs_6_) | copy-start | bytes 786436
  8.3 0.9 %copy-start.4 = (bf16[2,256,256]{2,1,0:T(8,128)(2,1)S(1)}, bf16[2,256,256]{2,1,0:T(8,128)(2,1)}, u32[]{:S(2)}) copy-start(bf16[2,256,256]{2,1,0:T(8,128)(2,1)} %constant.10.clone.refs_5_) | copy-start | bytes 786436
  9.3 0.9 %copy-start.5 = (bf16[512,256]{1,0:T(8,128)(2,1)S(1)}, bf16[512,256]{1,0:T(8,128)(2,1)}, u32[]{:S(2)}) copy-start(bf16[512,256]{1,0:T(8,128)(2,1)} %constant.9.clone.refs_4_) | copy-start | bytes 786436
  10.2 0.9 %copy-start.6 = (bf16[2,256,256]{2,1,0:T(8,128)(2,1)S(1)}, bf16[2,256,256]{2,1,0:T(8,128)(2,1)}, u32[]{:S(2)}) copy-start(bf16[2,256,256]{2,1,0:T(8,128)(2,1)} %constant.8.clone.refs_3_) | copy-start | bytes 786436
  12.2 3.4 %copy-start.7 = (s32[16]{0:T(128)S(1)}, s32[16]{0:T(128)}, u32[]{:S(2)}) copy-start(s32[16]{0:T(128)} %counts_ref.7) | copy-start | bytes 196
  12.2 6.3 %collective-permute-start.1 = (f32[3,4,128,128]{3,2,1,0:T(8,128)S(1)}, f32[3,4,128,128]{3,2,1,0:T(8,128)S(1)}, u32[]{:S(2)}, u32[]{:S(2)}) collective-permute-start(f32[3,4,128,128]{3,2,1,0:T(8,128)S(1)} %shard_map.114), channel_id=1, source_target_pairs={{1,0},{2,1},{3,2},{4,3},{5,4},{6,5},{7,6},{8,7},{9,8},{10,9},{11,1... | collective-permute-start | bytes 2359304 | tf_op jit(solution)/shard_map/ppermute | solution.py:19
  14.3 21.0 %collective-permute-start.2 = (f32[3,4,128,128]{3,2,1,0:T(8,128)S(1)}, f32[3,4,128,128]{3,2,1,0:T(8,128)S(1)}, u32[]{:S(2)}, u32[]{:S(2)}) collective-permute-start(f32[3,4,128,128]{3,2,1,0:T(8,128)S(1)} %shard_map.115), channel_id=1, source_target_pairs={{1,0},{2,1},{3,2},{4,3},{5,4},{6,5},{7,6},{8,7},{9,8},{10,9},{11,1... | collective-permute-start | bytes 2359304 | tf_op jit(solution)/shard_map/ppermute | solution.py:19
  23.7 19.6 %collective-permute-start.3 = (f32[2,4,128,128]{3,2,1,0:T(8,128)S(1)}, f32[2,4,128,128]{3,2,1,0:T(8,128)S(1)}, u32[]{:S(2)}, u32[]{:S(2)}) collective-permute-start(f32[2,4,128,128]{3,2,1,0:T(8,128)S(1)} %get-tuple-element.36.refs_0_), channel_id=1, source_target_pairs={{0,1},{1,2},{2,3},{3,4},{4,5},{5,6},{6,7},{7,8},{8,9},{9,10},{10,1... | collective-permute-start | bytes 1572872 | tf_op jit(solution)/shard_map/ppermute | solution.py:19
  36.1 7.1 %collective-permute-start.4 = (f32[576,128]{1,0:T(8,128)S(1)}, f32[576,128]{1,0:T(8,128)S(1)}, u32[]{:S(2)}, u32[]{:S(2)}) collective-permute-start(f32[576,128]{1,0:T(8,128)S(1)} %get-tuple-element.40), channel_id=1, source_target_pairs={{0,1},{1,0},{2,3},{3,2},{4,5},{5,4},{6,7},{7,6},{8,9},{9,8},{10,11... | collective-permute-start | bytes 884744 | tf_op jit(solution)/shard_map/ppermute | solution.py:288
  43.3 10.2 %collective-permute-start.5 = (f32[288,128]{1,0:T(8,128)S(1)}, f32[288,128]{1,0:T(8,128)S(1)}, u32[]{:S(2)}, u32[]{:S(2)}) collective-permute-start(f32[288,128]{1,0:T(8,128)S(1)} %get-tuple-element.42), channel_id=1, source_target_pairs={{0,2},{1,3},{2,0},{3,1},{4,6},{5,7},{6,4},{7,5},{8,10},{9,11},{10,... | collective-permute-start | bytes 442376 | tf_op jit(solution)/shard_map/ppermute | solution.py:288
  53.5 19.4 %collective-permute-start.6 = (f32[4,4,128,128]{3,2,1,0:T(8,128)S(1)}, f32[4,4,128,128]{3,2,1,0:T(8,128)S(1)}, u32[]{:S(2)}, u32[]{:S(2)}) collective-permute-start(f32[4,4,128,128]{3,2,1,0:T(8,128)S(1)} %get-tuple-element.43.refs_1_), channel_id=1, source_target_pairs={{0,1},{1,2},{2,3},{3,4},{4,5},{5,6},{6,7},{7,8},{8,9},{9,10},{10,1... | collective-permute-start | bytes 3145736 | tf_op jit(solution)/shard_map/ppermute | solution.py:19
  55.2 5.6 %collective-permute-start.7 = (f32[144,128]{1,0:T(8,128)S(1)}, f32[144,128]{1,0:T(8,128)S(1)}, u32[]{:S(2)}, u32[]{:S(2)}) collective-permute-start(f32[144,128]{1,0:T(8,128)S(1)} %get-tuple-element.46), channel_id=1, source_target_pairs={{0,4},{1,5},{2,6},{3,7},{4,0},{5,1},{6,2},{7,3},{8,12},{9,13},{10,... | collective-permute-start | bytes 221192 | tf_op jit(solution)/shard_map/ppermute | solution.py:288
  60.7 7.7 %collective-permute-start.8 = (f32[144,128]{1,0:T(8,128)S(1)}, f32[144,128]{1,0:T(8,128)S(1)}, u32[]{:S(2)}, u32[]{:S(2)}) collective-permute-start(f32[144,128]{1,0:T(8,128)S(1)} %shard_map.122.kept_ref), channel_id=1, source_target_pairs={{0,8},{1,9},{2,10},{3,11},{4,12},{5,13},{6,14},{7,15},{8,0},{9,1},... | collective-permute-start | bytes 221192 | tf_op jit(solution)/shard_map/ppermute | solution.py:288
  68.4 4.4 %collective-permute-start.9 = (f32[144,128]{1,0:T(8,128)S(1)}, f32[144,128]{1,0:T(8,128)S(1)}, u32[]{:S(2)}, u32[]{:S(2)}) collective-permute-start(f32[144,128]{1,0:T(8,128)S(1)} %shard_map.123.mine_ref), channel_id=1, source_target_pairs={{0,4},{1,5},{2,6},{3,7},{4,0},{5,1},{6,2},{7,3},{8,12},{9,13},{10,... | collective-permute-start | bytes 221192 | tf_op jit(solution)/shard_map/ppermute | solution.py:288
  72.9 5.2 %collective-permute-start.10 = (f32[288,128]{1,0:T(8,128)S(1)}, f32[288,128]{1,0:T(8,128)S(1)}, u32[]{:S(2)}, u32[]{:S(2)}) collective-permute-start(f32[288,128]{1,0:T(8,128)S(1)} %shard_map.124.mine_ref), channel_id=1, source_target_pairs={{0,2},{1,3},{2,0},{3,1},{4,6},{5,7},{6,4},{7,5},{8,10},{9,11},{10,... | collective-permute-start | bytes 442376 | tf_op jit(solution)/shard_map/ppermute | solution.py:288
  78.1 9.8 %collective-permute-start.11 = (f32[576,128]{1,0:T(8,128)S(1)}, f32[576,128]{1,0:T(8,128)S(1)}, u32[]{:S(2)}, u32[]{:S(2)}) collective-permute-start(f32[576,128]{1,0:T(8,128)S(1)} %shard_map.125.mine_ref), channel_id=1, source_target_pairs={{0,1},{1,0},{2,3},{3,2},{4,5},{5,4},{6,7},{7,6},{8,9},{9,8},{10,11... | collective-permute-start | bytes 884744 | tf_op jit(solution)/shard_map/ppermute | solution.py:288

commit v2 on v1

--- a/solution.py
+++ b/solution.py
@@ -117,43 +117,46 @@
             )
 
 
-PAIR = 2
+PAIR = 3
+PIECES = ((1, 1), (2, 1), (3, 1))
 
 
 def gradient_kernel(
     start, axis, counts_ref, place_ref, object_ref, probe_ref, measured_ref, fr_ref, fl_ref, pr_ref, pl_ref, *refs
 ):
-    last_call = start > 0
+    first_call = start == 0
     tile = lax.axis_index(axis)
     count = counts_ref[tile]
     modes, _, width, _ = probe_ref.shape
     slots = measured_ref.shape[0]
-    rim_refs, refs = refs[: 1 + last_call], refs[1 + last_call :]
-    rims = [(ref, i) for ref in rim_refs for i in range(ref.shape[0])]
+    last_call = start + PAIR == slots
+    rim_refs, refs = refs[:PAIR], refs[PAIR:]
+    before, refs = (refs[:1], refs[1:]) if not first_call else ((), refs)
     if last_call:
-        before_ref, grad_ref, kept_ref, sent_ref, sums_ref = refs
-        sums_ref[...] = before_ref[...]
+        *grad_refs, kept_ref, sent_ref, sums_ref = refs
     else:
-        grad_ref, sums_ref = refs
-        sums_ref[...] = jnp.zeros(sums_ref.shape, F32)
+        *grad_refs, sums_ref = refs
+    sums_ref[...] = jnp.zeros(sums_ref.shape, F32) if first_call else before[0][...]
     probe = [(probe_ref[m, 0], probe_ref[m, 1]) for m in range(modes)]
 
-    def visit(base):
+    @pl.when(start < count)
+    def _():
         places = [
-            window_place(place_ref, start + base + i, slots, width, object_ref.shape[-1] // width) for i in range(PAIR)
+            window_place(place_ref, start + i, slots, width, object_ref.shape[-1] // width) for i in range(PAIR)
         ]
 
         def window(i, s, part):
             in_own, in_first, shift, first, second = places[i]
             own = jnp.where(in_first, object_ref[s, part, :, first], object_ref[s, part, :, second])
-            rim_ref, at = rims[start + base + i]
-            stored = jnp.where(in_own, own, rim_ref[at, 2 * s + part])
-            stored = pltpu.roll(stored, lax.rem(width - place_ref[start + base + i], width), 0)
+            rim_ref = rim_refs[i]
+            stored = jnp.where(in_own, own, rim_ref[(start + i) % rim_ref.shape[0], 2 * s + part])
+            stored = pltpu.roll(stored, lax.rem(width - place_ref[start + i], width), 0)
             return pltpu.roll(stored, lax.rem(width - shift, width), 1)
 
         def put(i, s, part, value):
-            value = pltpu.roll(value, place_ref[start + base + i], 0)
-            grad_ref[base + i, 2 * s + part] = pltpu.roll(value, places[i][2], 1)
+            value = pltpu.roll(value, place_ref[start + i], 0)
+            grad_ref, at = [(ref, at) for ref in grad_refs for at in range(ref.shape[0])][i]
+            grad_ref[at, 2 * s + part] = pltpu.roll(value, places[i][2], 1)
 
         def split(blocks):
             return [blocks[i * modes : (i + 1) * modes] for i in range(PAIR)]
@@ -165,7 +168,7 @@
         back = []
         for i in range(PAIR):
             intensity = sum(re * re + im * im for re, im in far[i])
-            residue = 2.0 * (intensity - measured_ref[start + base + i])
+            residue = 2.0 * (intensity - measured_ref[start + i])
             back += [(residue * re, -(residue * im)) for re, im in far[i]]
         back = split(two_sided(back, fr_ref, fl_ref))
         last = split(two_sided([times(g, two) for gs, two in zip(back, twos) for g in gs], pr_ref, pl_ref))
@@ -176,7 +179,7 @@
             terms = [times(p, g) for p, g in zip(probe, last[i])]
             put(i, 0, 0, sum(t[0] for t in terms))
             put(i, 0, 1, -sum(t[1] for t in terms))
-        live = [start + base + i < count for i in range(PAIR)]
+        live = [start + i < count for i in range(PAIR)]
 
         def summed(values):
             return sum(jnp.where(alive, value, 0.0) for alive, value in zip(live, values))
@@ -187,9 +190,6 @@
                 rows = pl.ds((2 * m + part) * width, width)
                 sums_ref[rows] += sign * summed(g[part] for g in grads)
         sums_ref[pl.ds(2 * modes * width, width)] += summed(re * re + im * im for re, im in ones)
-
-    for base in range(0, grad_ref.shape[0], PAIR):
-        pl.when(start + base < count)(functools.partial(visit, base))
     if last_call:
         half = kept_ref.shape[0]
         side = lax.rem(tile, 2)
@@ -229,14 +229,18 @@
     lit_ref[...] = 0.5 / (lit_ref[...] + 1.0)
 
 
-def update_kernel(axis, sizes, counts_ref, place_ref, before_ref, object_ref, lit_ref, *refs):
-    out_ref, sum_ref = refs[2 * len(sizes) :]
+def copy_kernel(source_ref, out_ref):
+    out_ref[...] = source_ref[...]
+
+
+def update_kernel(axis, counts_ref, place_ref, before_ref, object_ref, lit_ref, *refs):
+    *refs, out_ref, sum_ref = refs
     plane = pl.program_id(0)
-    parts = [(n, i) for n, size in enumerate(sizes) for i in range(size)]
+    own_refs, rim_refs = refs[: len(refs) // 2], refs[len(refs) // 2 :]
 
     def window_of(ref, slot, own, shift):
-        n, i = parts[slot]
-        return refs[n + (0 if own else len(sizes))][i, plane]
+        parts = [(r, i) for r in (own_refs if own else rim_refs) for i in range(r.shape[0])]
+        return parts[slot][0][parts[slot][1], plane]
 
     add_windows(sum_ref, counts_ref, place_ref, before_ref, axis, window_of)
     out_ref[0, 0] = object_ref[plane // 2, plane % 2] - sum_ref[...] * lit_ref[...]
@@ -277,16 +281,16 @@
     out_ref[pl.ds(pl.multiple_of((1 - side) * half, 8), half)] = got_ref[...]
 
 
-def half_sum(kept, sent, axis, beside, joins):
+def half_sum(kept, sent, axis, beside, waits):
     count = lax.axis_size(axis)
     bits = [1 << b for b in range(count.bit_length() - 1)]
     vmem = pl.BlockSpec(memory_space=pltpu.VMEM)
     width = kept.shape[1]
 
     def exchanged(value, bit, step):
-        value = after(value, *joins.get(step, ()))
+        value = after(value, *waits(step))
         got = lax.ppermute(value, axis, [(i, i ^ bit) for i in range(count)])
-        beside.get(step, lambda reached: None)(got)
+        beside(step, value)
         return pltpu.with_memory_space_constraint(got, pltpu.VMEM)
 
     def local(kernel, rows, *operands):
@@ -328,35 +332,36 @@
     def held(value):
         return pltpu.with_memory_space_constraint(value, pltpu.VMEM)
 
-    def held_like(value):
-        return pltpu.VMEM(value.shape, value.dtype)
-
     place = jnp.concatenate([row_offset, col_offset])
     before = passed_along(place, axis, 1)
-    loaded = [jnp.asarray(t) for t in (*real_forms(dft), *real_forms(move))]
-    loaded = [object_field, probe_modes, measured, *loaded]
-    objects, probe, patterns, *tables = pl.pallas_call(
-        load_kernel,
-        out_shape=tuple(map(held_like, loaded)),
-        in_specs=[vmem] * len(loaded),
-        out_specs=(vmem,) * len(loaded),
-        compiler_params=params,
-    )(*loaded)
-    sizes = (PAIR, slots - PAIR)
+
+    def load(*arrays):
+        return pl.pallas_call(
+            load_kernel,
+            out_shape=tuple(pltpu.VMEM(a.shape, a.dtype) for a in arrays),
+            in_specs=[vmem] * len(arrays),
+            out_specs=(vmem,) * len(arrays),
+            compiler_params=params,
+        )(*arrays)
+
+    (objects,) = load(object_field)
+    in_chunk = PAIR
 
     def windows(size):
         return pltpu.VMEM((size, 2 * slices, width, width), F32)
 
     rims, strip = [], before
-    for start, size in ((0, slots // 2), (slots // 2, slots - slots // 2)):
+    for start in range(0, slots, in_chunk):
         strip = pl.pallas_call(
             functools.partial(strip_kernel, start),
-            out_shape=windows(size),
+            out_shape=windows(in_chunk),
             in_specs=[smem, vmem],
             out_specs=vmem,
             compiler_params=params,
         )(after(before, strip), objects)
         rims.append(held(passed_along(strip, axis, -1)))
+    tables = [jnp.asarray(t) for t in (*real_forms(dft), *real_forms(move))]
+    probe, patterns, *tables = load(*lax.optimization_barrier((strip, probe_modes, measured, *tables))[1:])
     lit = pl.pallas_call(
         functools.partial(light_kernel, axis),
         out_shape=pltpu.VMEM((tile_rows, tile_cols), F32),
@@ -367,39 +372,68 @@
     rows = (2 * modes + 1) * width
     whole, half = pltpu.VMEM((rows, width), F32), pltpu.VMEM((rows // 2, width), F32)
     common = (probe, patterns, *tables)
-    grad_a, sums = pl.pallas_call(
-        functools.partial(gradient_kernel, 0, axis),
-        out_shape=(windows(sizes[0]), whole),
-        in_specs=[smem] * 2 + [vmem] * 8,
-        out_specs=(vmem,) * 2,
-        compiler_params=params,
-    )(tile_counts, after(place, lit), objects, *common, rims[0])
-    arrived_a = passed_along(grad_a, axis, 1)
-    grad_b, kept, sent = pl.pallas_call(
-        functools.partial(gradient_kernel, sizes[0], axis),
-        out_shape=(windows(sizes[1]), half, half),
-        in_specs=[smem] * 2 + [vmem] * 10,
-        out_specs=(vmem,) * 3,
-        scratch_shapes=[whole],
-        compiler_params=params,
-        cost_estimate=pl.CostEstimate(flops=1, bytes_accessed=40 << 20, transcendentals=0),
-    )(tile_counts, place, objects, *common, *rims, sums)
-    arrived = [arrived_a]
-
-    def send_rest(reached):
-        arrived.append(passed_along(after(grad_b, reached), axis, 1))
-
-    mine, got = half_sum(kept, sent, axis, {1: send_rest}, {1: arrived[:1], 5: arrived})
-    updated_object = pl.pallas_call(
-        functools.partial(update_kernel, axis, sizes),
-        grid=(2 * slices,),
-        out_shape=jax.ShapeDtypeStruct(object_field.shape, F32),
-        in_specs=[smem] * 3 + [vmem] * 6,
-        out_specs=pl.BlockSpec((1, 1, tile_rows, tile_cols), lambda plane: (plane // 2, plane % 2, 0, 0)),
-        scratch_shapes=[pltpu.VMEM((tile_rows, tile_cols), F32)],
-        compiler_params=params,
-        cost_estimate=pl.CostEstimate(flops=1, bytes_accessed=12 << 20, transcendentals=0),
-    )(tile_counts, place, before, objects, lit, grad_a, grad_b, *map(held, arrived))
+    grads, arrived, sums = [], [], []
+    for start in range(0, slots, PAIR):
+        last_call = start + PAIR == slots
+        ready = arrived[: start // PAIR - 1] if start else [lit]
+        pieces = [windows(size) for _, size in PIECES] if last_call else [windows(PAIR)]
+        results = pieces + ([half, half] if last_call else [whole])
+        outs = pl.pallas_call(
+            functools.partial(gradient_kernel, start, axis),
+            out_shape=results,
+            in_specs=[smem] * 2 + [vmem] * (7 + PAIR + len(sums)),
+            out_specs=[vmem] * len(results),
+            scratch_shapes=[whole] if last_call else [],
+            compiler_params=params,
+            cost_estimate=pl.CostEstimate(flops=1, bytes_accessed=6 << 20, transcendentals=0),
+        )(
+            tile_counts, after(place, *ready), objects, *common,
+            *(rims[(start + i) // in_chunk] for i in range(PAIR)), *sums,
+        )
+        grads += outs[: len(pieces)]
+        sums = outs[len(pieces) :]
+        if not last_call:
+            arrived.append(passed_along(outs[0], axis, 1))
+
+    def beside(step, value):
+        for n, (when, size) in enumerate(PIECES):
+            if when == step:
+                piece = pl.pallas_call(
+                    copy_kernel,
+                    out_shape=windows(size),
+                    in_specs=[vmem],
+                    out_specs=vmem,
+                    compiler_params=params,
+                    cost_estimate=pl.CostEstimate(flops=1, bytes_accessed=6 << 20, transcendentals=0),
+                )(after(grads[n - len(PIECES)], value))
+                arrived.append(passed_along(piece, axis, 1))
+
+    updated = []
+
+    def waits(step):
+        if step == 1:
+            return arrived
+        last = lax.axis_size(axis).bit_length() - 1 + 2
+        if step == last - 1:
+            return arrived
+        if step == last:
+            updated.append(update())
+            return updated
+        return []
+
+    def update():
+        return pl.pallas_call(
+            functools.partial(update_kernel, axis),
+            grid=(2 * slices,),
+            out_shape=jax.ShapeDtypeStruct(object_field.shape, F32),
+            in_specs=[smem] * 3 + [vmem] * (2 + 2 * len(grads)),
+            out_specs=pl.BlockSpec((1, 1, tile_rows, tile_cols), lambda plane: (plane // 2, plane % 2, 0, 0)),
+            scratch_shapes=[pltpu.VMEM((tile_rows, tile_cols), F32)],
+            compiler_params=params,
+            cost_estimate=pl.CostEstimate(flops=1, bytes_accessed=12 << 20, transcendentals=0),
+        )(tile_counts, place, before, objects, lit, *grads, *map(held, arrived))
+
+    mine, got = half_sum(*sums, axis, beside, waits)
     updated_probe = pl.pallas_call(
         functools.partial(probe_kernel, axis),
         out_shape=jax.ShapeDtypeStruct(probe_modes.shape, F32),
@@ -408,7 +442,7 @@
         scratch_shapes=[pltpu.VMEM((rows, width), F32)],
         compiler_params=params,
     )(mine, got, probe)
-    return (updated_object, updated_probe)
+    return (updated[0], updated_probe)
 
 
 def solution(mesh):

time: 88.6 us -> 77.1 us (0.87)
  starting transfers between devices: 43.8 us -> 37.6 us
  local copies, waits for them, and re-layouts: 7.43 us -> 1.63 us
  waiting for transfers between devices: 23.5 us -> 21 us
  Pallas kernels: 12.6 us -> 14.9 us
    ppermute x7, starting transfers between devices: 25.7 us -> 14.5 us  [exchanged(): got = lax.ppermute(value, axis, [(i, i ^ bit) for i in range(count)])]
    unnamed x16, local copies, waits for them, and re-layouts: 7.43 us -> 1.63 us
    ppermute x5 -> x7, starting transfers between devices: 18.1 us -> 23.1 us  [passed_along(): lax.ppermute(value, axis, [(source, source + steps) for source in range(l...]
    ppermute x7, waiting for transfers between devices: 21.5 us -> 19.3 us  [exchanged(): got = lax.ppermute(value, axis, [(i, i ^ bit) for i in range(count)])]
    pallas_call x4 -> x8, Pallas kernels: 9.17 us -> 11.3 us  [the longest x2 7.97 us: body(): pl.pallas_call(functools.partial(gradient_kernel, start, axis), out_shape...]
    ppermute x5 -> x7, waiting for transfers between devices: 2.04 us -> 1.74 us  [passed_along(): lax.ppermute(value, axis, [(source, source + steps) for source in range(l...]
  transfers between devices with their start and end apart: 12 -> 14, of which waited for: 7 -> 7; matrix products, arithmetic and copies ran while one was open for 0% -> 0% of each run, Pallas kernels for 12% -> 17%
where the time goes in v2:
time: 77.1 us; the launch traced here: 76.8 us
  starting transfers between devices  37.6 us (49%)
  waiting for transfers between devices  21 us (27%)
  Pallas kernels  14.9 us (19%)
  local copies, waits for them, and re-layouts  1.63 us (2%)
  between operations  0.99 us (1%)
    ppermute x7, starting transfers between devices, passed_along(): lax.ppermute(value, axis, [(source, source + steps) for source in range(l...  23.1 us
    ppermute x7, waiting for transfers between devices, exchanged(): got = lax.ppermute(value, axis, [(i, i ^ bit) for i in range(count)])  19.3 us
    ppermute x7, starting transfers between devices, exchanged(): got = lax.ppermute(value, axis, [(i, i ^ bit) for i in range(count)])  14.5 us
    pallas_call x2, Pallas kernels, body(): pl.pallas_call(functools.partial(gradient_kernel, start, axis), out_shape...  7.97 us
    pallas_call x1, Pallas kernels, update(): pl.pallas_call(functools.partial(update_kernel, axis), grid=(2 * slices,)...  3.05 us
    ppermute x7, waiting for transfers between devices, passed_along(): lax.ppermute(value, axis, [(source, source + steps) for source in range(l...  1.74 us
    unnamed x16, local copies, waits for them, and re-layouts  1.63 us
  transfers between devices with their start and end apart: 14, of which 7 were waited for; matrix products, arithmetic and copies ran while one was open for 0% of the time, Pallas kernels for 17%

profile of v2, /device:TPU:0, one launch (start us, length us, event | category | flops | bytes accessed | tf_op | source)
XLA Modules:
  0.0 76.8 jit_solution(7329584896916762690)
XLA Ops:
  1.4 2.3 %collective-permute-start = (s32[12]{0:T(128)S(1)}, s32[12]{0:T(128)S(1)}, u32[]{:S(2)}, u32[]{:S(2)}) collective-permute-start(s32[12]{0:T(128)S(1)} %pad_add_fusion.place_ref), channel_id=1, source_target_pairs={{0,1},{1,2},{2,3},{3,4},{4,5},{5,6},{6,7},{7,8},{8,9},{9,10},{10,1... | collective-permute-start | bytes 152 | tf_op jit(solution)/shard_map/ppermute | solution.py:19
  3.7 1.6 %copy-done = f32[2,2,128,1024]{3,2,1,0:T(8,128)S(1)} copy-done((f32[2,2,128,1024]{3,2,1,0:T(8,128)S(1)}, f32[2,2,128,1024]{3,2,1,0:T(8,128)}, u32[]{:S(2)}) %copy-start) | copy-done | bytes 2097176
  6.3 1.4 %collective-permute-start.1 = (f32[3,4,128,128]{3,2,1,0:T(8,128)S(1)}, f32[3,4,128,128]{3,2,1,0:T(8,128)S(1)}, u32[]{:S(2)}, u32[]{:S(2)}) collective-permute-start(f32[3,4,128,128]{3,2,1,0:T(8,128)S(1)} %shard_map.114), channel_id=1, source_target_pairs={{1,0},{2,1},{3,2},{4,3},{5,4},{6,5},{7,6},{8,7},{9,8},{10,9},{11,1... | collective-permute-start | bytes 2359304 | tf_op jit(solution)/shard_map/ppermute | solution.py:19
  7.8 0.8 shard_map.115
  8.5 1.3 %collective-permute-start.2 = (f32[3,4,128,128]{3,2,1,0:T(8,128)S(1)}, f32[3,4,128,128]{3,2,1,0:T(8,128)S(1)}, u32[]{:S(2)}, u32[]{:S(2)}) collective-permute-start(f32[3,4,128,128]{3,2,1,0:T(8,128)S(1)} %shard_map.115), channel_id=1, source_target_pairs={{1,0},{2,1},{3,2},{4,3},{5,4},{6,5},{7,6},{8,7},{9,8},{10,9},{11,1... | collective-permute-start | bytes 2359304 | tf_op jit(solution)/shard_map/ppermute | solution.py:19
  10.0 1.0 %shard_map.117.lit_ref = f32[128,1024]{1,0:T(8,128)S(1)} custom-call(s32[16]{0:T(128)S(1)} %copy-done.7, s32[12]{0:T(128)S(1)} %pad_add_fusion.place_ref, s32[12]{0:T(128)S(1)} %collective-permute-done.before_ref, f32[4,2,128,128]{3,2,1,0:T(8,128)S(1)} %get-tuple-element.44.probe_ref), custom_call_target="tpu_custom_call" | custom-call | tf_op jit(solution)/shard_map/pallas_call | solution.py:365
  11.0 1.7 %collective-permute-done.1.refs_0_.refs_1_.refs_2_ = f32[3,4,128,128]{3,2,1,0:T(8,128)S(1)} collective-permute-done((f32[3,4,128,128]{3,2,1,0:T(8,128)S(1)}, f32[3,4,128,128]{3,2,1,0:T(8,128)S(1)}, u32[]{:S(2)}, u32[]{:S(2)}) %collective-permute-start.1) | collective-permute-done | bytes 786464 | tf_op jit(solution)/shard_map/ppermute | solution.py:19
  12.7 7.1 %shard_map.118 = (f32[3,4,128,128]{3,2,1,0:T(8,128)S(1)}, f32[1152,128]{1,0:T(8,128)S(1)}) custom-call(s32[16]{0:T(128)S(1)} %copy-done.7, s32[12]{0:T(128)S(1)} %pad_add_fusion.place_ref, f32[2,2,128,1024]{3,2,1,0:T(8,128)S(1)} %shard_map.113.object_ref, f32[4,2,128,128]{3,2,1,0:T(8,128)S(1)} %get-tuple-element.44.probe_ref, ...), custom_call_target="tpu_custom_call" | custom-call | flops 1 | bytes 6291456 | tf_op jit(solution)/shard_map/pallas_call | solution.py:381
  19.9 11.6 %collective-permute-start.3 = (f32[3,4,128,128]{3,2,1,0:T(8,128)S(1)}, f32[3,4,128,128]{3,2,1,0:T(8,128)S(1)}, u32[]{:S(2)}, u32[]{:S(2)}) collective-permute-start(f32[3,4,128,128]{3,2,1,0:T(8,128)S(1)} %get-tuple-element.51.refs_0_), channel_id=1, source_target_pairs={{0,1},{1,2},{2,3},{3,4},{4,5},{5,6},{6,7},{7,8},{8,9},{9,10},{10,1... | collective-permute-start | bytes 2359304 | tf_op jit(solution)/shard_map/ppermute | solution.py:19
  31.5 0.9 %shard_map.119 = (f32[1,4,128,128]{3,2,1,0:T(8,128)S(1)}, f32[1,4,128,128]{3,2,1,0:T(8,128)S(1)}, f32[1,4,128,128]{3,2,1,0:T(8,128)S(1)}, f32[576,128]{1,0:T(8,128)S(1)}, f32[576,128]{1,0:T(8,128)S(1)}) custom-call(s32[16]{0:T(128)S(1)} %copy-done.7, s32[12]{0:T(128)S(1)} %pad_add_fusion.place_ref, f32[2,2,128,1024]{3,2,1,0:T(8,128)S(1)} %shard_map.113.object_ref, ...), custom_call_target="tpu_custom_call" | custom-call | flops 1 | bytes 6291456 | tf_op jit(solution)/shard_map/pallas_call | solution.py:381
  32.4 1.6 %collective-permute-done.4.got_ref = f32[576,128]{1,0:T(8,128)S(1)} collective-permute-done((f32[576,128]{1,0:T(8,128)S(1)}, f32[576,128]{1,0:T(8,128)S(1)}, u32[]{:S(2)}, u32[]{:S(2)}) %collective-permute-start.4) | collective-permute-done | bytes 294944 | tf_op jit(solution)/shard_map/ppermute | solution.py:292
  34.0 9.0 %collective-permute-start.6 = (f32[288,128]{1,0:T(8,128)S(1)}, f32[288,128]{1,0:T(8,128)S(1)}, u32[]{:S(2)}, u32[]{:S(2)}) collective-permute-start(f32[288,128]{1,0:T(8,128)S(1)} %get-tuple-element.59), channel_id=1, source_target_pairs={{0,2},{1,3},{2,0},{3,1},{4,6},{5,7},{6,4},{7,5},{8,10},{9,11},{10,... | collective-permute-start | bytes 442376 | tf_op jit(solution)/shard_map/ppermute | solution.py:292
  43.0 4.1 %collective-permute-done.6.got_ref = f32[288,128]{1,0:T(8,128)S(1)} collective-permute-done((f32[288,128]{1,0:T(8,128)S(1)}, f32[288,128]{1,0:T(8,128)S(1)}, u32[]{:S(2)}, u32[]{:S(2)}) %collective-permute-start.6) | collective-permute-done | bytes 147488 | tf_op jit(solution)/shard_map/ppermute | solution.py:292
  47.2 2.7 %collective-permute-start.8 = (f32[144,128]{1,0:T(8,128)S(1)}, f32[144,128]{1,0:T(8,128)S(1)}, u32[]{:S(2)}, u32[]{:S(2)}) collective-permute-start(f32[144,128]{1,0:T(8,128)S(1)} %get-tuple-element.62), channel_id=1, source_target_pairs={{0,4},{1,5},{2,6},{3,7},{4,0},{5,1},{6,2},{7,3},{8,12},{9,13},{10,... | collective-permute-start | bytes 221192 | tf_op jit(solution)/shard_map/ppermute | solution.py:292
  49.8 1.3 %collective-permute-start.5 = (f32[1,4,128,128]{3,2,1,0:T(8,128)S(1)}, f32[1,4,128,128]{3,2,1,0:T(8,128)S(1)}, u32[]{:S(2)}, u32[]{:S(2)}) collective-permute-start(f32[1,4,128,128]{3,2,1,0:T(8,128)S(1)} %shard_map.121), channel_id=1, source_target_pairs={{0,1},{1,2},{2,3},{3,4},{4,5},{5,6},{6,7},{7,8},{8,9},{9,10},{10,1... | collective-permute-start | bytes 786440 | tf_op jit(solution)/shard_map/ppermute | solution.py:19
  51.2 3.2 %collective-permute-start.7 = (f32[1,4,128,128]{3,2,1,0:T(8,128)S(1)}, f32[1,4,128,128]{3,2,1,0:T(8,128)S(1)}, u32[]{:S(2)}, u32[]{:S(2)}) collective-permute-start(f32[1,4,128,128]{3,2,1,0:T(8,128)S(1)} %shard_map.123), channel_id=1, source_target_pairs={{0,1},{1,2},{2,3},{3,4},{4,5},{5,6},{6,7},{7,8},{8,9},{9,10},{10,1... | collective-permute-start | bytes 786440 | tf_op jit(solution)/shard_map/ppermute | solution.py:19
  54.5 1.9 %collective-permute-start.9 = (f32[1,4,128,128]{3,2,1,0:T(8,128)S(1)}, f32[1,4,128,128]{3,2,1,0:T(8,128)S(1)}, u32[]{:S(2)}, u32[]{:S(2)}) collective-permute-start(f32[1,4,128,128]{3,2,1,0:T(8,128)S(1)} %shard_map.125), channel_id=1, source_target_pairs={{0,1},{1,2},{2,3},{3,4},{4,5},{5,6},{6,7},{7,8},{8,9},{9,10},{10,1... | collective-permute-start | bytes 786440 | tf_op jit(solution)/shard_map/ppermute | solution.py:19
  56.4 2.1 %collective-permute-start.10 = (f32[144,128]{1,0:T(8,128)S(1)}, f32[144,128]{1,0:T(8,128)S(1)}, u32[]{:S(2)}, u32[]{:S(2)}) collective-permute-start(f32[144,128]{1,0:T(8,128)S(1)} %shard_map.124.kept_ref), channel_id=1, source_target_pairs={{0,8},{1,9},{2,10},{3,11},{4,12},{5,13},{6,14},{7,15},{8,0},{9,1},... | collective-permute-start | bytes 221192 | tf_op jit(solution)/shard_map/ppermute | solution.py:292
  58.5 4.7 %collective-permute-done.10.got_ref = f32[144,128]{1,0:T(8,128)S(1)} collective-permute-done((f32[144,128]{1,0:T(8,128)S(1)}, f32[144,128]{1,0:T(8,128)S(1)}, u32[]{:S(2)}, u32[]{:S(2)}) %collective-permute-start.10) | collective-permute-done | bytes 73760 | tf_op jit(solution)/shard_map/ppermute | solution.py:292
  63.3 4.3 %collective-permute-done.11.got_ref = f32[144,128]{1,0:T(8,128)S(1)} collective-permute-done((f32[144,128]{1,0:T(8,128)S(1)}, f32[144,128]{1,0:T(8,128)S(1)}, u32[]{:S(2)}, u32[]{:S(2)}) %collective-permute-start.11) | collective-permute-done | bytes 73760 | tf_op jit(solution)/shard_map/ppermute | solution.py:292
  68.3 3.1 %shard_map.126 = f32[2,2,128,1024]{3,2,1,0:T(8,128)} custom-call(s32[16]{0:T(128)S(1)} %copy-done.7, s32[12]{0:T(128)S(1)} %pad_add_fusion.place_ref, s32[12]{0:T(128)S(1)} %collective-permute-done.before_ref, f32[2,2,128,1024]{3,2,1,0:T(8,128)S(1)} %shard_map.113.object_ref, f32[128,1024]{1,0:T(8,128)S(1)} %shard_map.117.lit_ref, ...), custom_call_target="tpu_custom_call" | custom-call | flops 1 | bytes 12582912 | tf_op jit(solution)/shard_map/pallas_call | solution.py:425
  71.3 2.9 %collective-permute-done.12.got_ref = f32[288,128]{1,0:T(8,128)S(1)} collective-permute-done((f32[288,128]{1,0:T(8,128)S(1)}, f32[288,128]{1,0:T(8,128)S(1)}, u32[]{:S(2)}, u32[]{:S(2)}) %collective-permute-start.12) | collective-permute-done | bytes 147488 | tf_op jit(solution)/shard_map/ppermute | solution.py:292
  74.3 1.6 %collective-permute-done.13.got_ref = f32[576,128]{1,0:T(8,128)S(1)} collective-permute-done((f32[576,128]{1,0:T(8,128)S(1)}, f32[576,128]{1,0:T(8,128)S(1)}, u32[]{:S(2)}, u32[]{:S(2)}) %collective-permute-start.13) | collective-permute-done | bytes 294944 | tf_op jit(solution)/shard_map/ppermute | solution.py:292
  75.9 0.9 %shard_map.130 = f32[4,2,128,128]{3,2,1,0:T(8,128)} custom-call(f32[576,128]{1,0:T(8,128)S(1)} %shard_map.129.mine_ref, f32[576,128]{1,0:T(8,128)S(1)} %collective-permute-done.13.got_ref, f32[4,2,128,128]{3,2,1,0:T(8,128)S(1)} %get-tuple-element.44.probe_ref), custom_call_target="tpu_custom_call" | custom-call | tf_op jit(solution)/shard_map/pallas_call | solution.py:437
  (39 shorter events, 2.8 us)
Async XLA Ops:
  1.4 4.1 %collective-permute-start = (s32[12]{0:T(128)S(1)}, s32[12]{0:T(128)S(1)}, u32[]{:S(2)}, u32[]{:S(2)}) collective-permute-start(s32[12]{0:T(128)S(1)} %pad_add_fusion.place_ref), channel_id=1, source_target_pairs={{0,1},{1,2},{2,3},{3,4},{4,5},{5,6},{6,7},{7,8},{8,9},{9,10},{10,1... | collective-permute-start | bytes 152 | tf_op jit(solution)/shard_map/ppermute | solution.py:19
  3.7 1.6 %copy-start = (f32[2,2,128,1024]{3,2,1,0:T(8,128)S(1)}, f32[2,2,128,1024]{3,2,1,0:T(8,128)}, u32[]{:S(2)}) copy-start(f32[2,2,128,1024]{3,2,1,0:T(8,128)} %refs_0_.1) | copy-start | bytes 6291460
  6.2 3.6 %copy-start.1 = (f32[4,2,128,128]{3,2,1,0:T(8,128)S(1)}, f32[4,2,128,128]{3,2,1,0:T(8,128)}, u32[]{:S(2)}) copy-start(f32[4,2,128,128]{3,2,1,0:T(8,128)} %refs_0_.2) | copy-start | bytes 1572868
  6.3 3.6 %copy-start.2 = (f32[6,128,128]{2,1,0:T(8,128)S(1)}, f32[6,128,128]{2,1,0:T(8,128)}, u32[]{:S(2)}) copy-start(f32[6,128,128]{2,1,0:T(8,128)} %refs_1_) | copy-start | bytes 1179652
  6.3 3.6 %copy-start.3 = (bf16[2,256,256]{2,1,0:T(8,128)(2,1)S(1)}, bf16[2,256,256]{2,1,0:T(8,128)(2,1)}, u32[]{:S(2)}) copy-start(bf16[2,256,256]{2,1,0:T(8,128)(2,1)} %constant.8.clone.refs_2_) | copy-start | bytes 786436
  6.3 3.6 %copy-start.4 = (bf16[512,256]{1,0:T(8,128)(2,1)S(1)}, bf16[512,256]{1,0:T(8,128)(2,1)}, u32[]{:S(2)}) copy-start(bf16[512,256]{1,0:T(8,128)(2,1)} %constant.9.clone.refs_3_) | copy-start | bytes 786436
  6.3 3.6 %copy-start.5 = (bf16[2,256,256]{2,1,0:T(8,128)(2,1)S(1)}, bf16[2,256,256]{2,1,0:T(8,128)(2,1)}, u32[]{:S(2)}) copy-start(bf16[2,256,256]{2,1,0:T(8,128)(2,1)} %constant.10.clone.refs_4_) | copy-start | bytes 786436
  6.3 3.6 %copy-start.6 = (bf16[512,256]{1,0:T(8,128)(2,1)S(1)}, bf16[512,256]{1,0:T(8,128)(2,1)}, u32[]{:S(2)}) copy-start(bf16[512,256]{1,0:T(8,128)(2,1)} %constant.11.clone.refs_5_) | copy-start | bytes 786436
  6.3 3.7 %copy-start.7 = (s32[16]{0:T(128)S(1)}, s32[16]{0:T(128)}, u32[]{:S(2)}) copy-start(s32[16]{0:T(128)} %counts_ref.7) | copy-start | bytes 196
  6.3 6.4 %collective-permute-start.1 = (f32[3,4,128,128]{3,2,1,0:T(8,128)S(1)}, f32[3,4,128,128]{3,2,1,0:T(8,128)S(1)}, u32[]{:S(2)}, u32[]{:S(2)}) collective-permute-start(f32[3,4,128,128]{3,2,1,0:T(8,128)S(1)} %shard_map.114), channel_id=1, source_target_pairs={{1,0},{2,1},{3,2},{4,3},{5,4},{6,5},{7,6},{8,7},{9,8},{10,9},{11,1... | collective-permute-start | bytes 2359304 | tf_op jit(solution)/shard_map/ppermute | solution.py:19
  8.5 22.9 %collective-permute-start.2 = (f32[3,4,128,128]{3,2,1,0:T(8,128)S(1)}, f32[3,4,128,128]{3,2,1,0:T(8,128)S(1)}, u32[]{:S(2)}, u32[]{:S(2)}) collective-permute-start(f32[3,4,128,128]{3,2,1,0:T(8,128)S(1)} %shard_map.115), channel_id=1, source_target_pairs={{1,0},{2,1},{3,2},{4,3},{5,4},{6,5},{7,6},{8,7},{9,8},{10,9},{11,1... | collective-permute-start | bytes 2359304 | tf_op jit(solution)/shard_map/ppermute | solution.py:19
  19.9 14.1 %collective-permute-start.3 = (f32[3,4,128,128]{3,2,1,0:T(8,128)S(1)}, f32[3,4,128,128]{3,2,1,0:T(8,128)S(1)}, u32[]{:S(2)}, u32[]{:S(2)}) collective-permute-start(f32[3,4,128,128]{3,2,1,0:T(8,128)S(1)} %get-tuple-element.51.refs_0_), channel_id=1, source_target_pairs={{0,1},{1,2},{2,3},{3,4},{4,5},{5,6},{6,7},{7,8},{8,9},{9,10},{10,1... | collective-permute-start | bytes 2359304 | tf_op jit(solution)/shard_map/ppermute | solution.py:19
  32.3 1.6 %collective-permute-start.4 = (f32[576,128]{1,0:T(8,128)S(1)}, f32[576,128]{1,0:T(8,128)S(1)}, u32[]{:S(2)}, u32[]{:S(2)}) collective-permute-start(f32[576,128]{1,0:T(8,128)S(1)} %get-tuple-element.57), channel_id=1, source_target_pairs={{0,1},{1,0},{2,3},{3,2},{4,5},{5,4},{6,7},{7,6},{8,9},{9,8},{10,11... | collective-permute-start | bytes 884744 | tf_op jit(solution)/shard_map/ppermute | solution.py:292
  34.0 13.1 %collective-permute-start.6 = (f32[288,128]{1,0:T(8,128)S(1)}, f32[288,128]{1,0:T(8,128)S(1)}, u32[]{:S(2)}, u32[]{:S(2)}) collective-permute-start(f32[288,128]{1,0:T(8,128)S(1)} %get-tuple-element.59), channel_id=1, source_target_pairs={{0,2},{1,3},{2,0},{3,1},{4,6},{5,7},{6,4},{7,5},{8,10},{9,11},{10,... | collective-permute-start | bytes 442376 | tf_op jit(solution)/shard_map/ppermute | solution.py:292
  47.2 7.3 %collective-permute-start.8 = (f32[144,128]{1,0:T(8,128)S(1)}, f32[144,128]{1,0:T(8,128)S(1)}, u32[]{:S(2)}, u32[]{:S(2)}) collective-permute-start(f32[144,128]{1,0:T(8,128)S(1)} %get-tuple-element.62), channel_id=1, source_target_pairs={{0,4},{1,5},{2,6},{3,7},{4,0},{5,1},{6,2},{7,3},{8,12},{9,13},{10,... | collective-permute-start | bytes 221192 | tf_op jit(solution)/shard_map/ppermute | solution.py:292
  49.8 17.8 %collective-permute-start.5 = (f32[1,4,128,128]{3,2,1,0:T(8,128)S(1)}, f32[1,4,128,128]{3,2,1,0:T(8,128)S(1)}, u32[]{:S(2)}, u32[]{:S(2)}) collective-permute-start(f32[1,4,128,128]{3,2,1,0:T(8,128)S(1)} %shard_map.121), channel_id=1, source_target_pairs={{0,1},{1,2},{2,3},{3,4},{4,5},{5,6},{6,7},{7,8},{8,9},{9,10},{10,1... | collective-permute-start | bytes 786440 | tf_op jit(solution)/shard_map/ppermute | solution.py:19
  51.2 16.4 %collective-permute-start.7 = (f32[1,4,128,128]{3,2,1,0:T(8,128)S(1)}, f32[1,4,128,128]{3,2,1,0:T(8,128)S(1)}, u32[]{:S(2)}, u32[]{:S(2)}) collective-permute-start(f32[1,4,128,128]{3,2,1,0:T(8,128)S(1)} %shard_map.123), channel_id=1, source_target_pairs={{0,1},{1,2},{2,3},{3,4},{4,5},{5,6},{6,7},{7,8},{8,9},{9,10},{10,1... | collective-permute-start | bytes 786440 | tf_op jit(solution)/shard_map/ppermute | solution.py:19
  54.5 13.2 %collective-permute-start.9 = (f32[1,4,128,128]{3,2,1,0:T(8,128)S(1)}, f32[1,4,128,128]{3,2,1,0:T(8,128)S(1)}, u32[]{:S(2)}, u32[]{:S(2)}) collective-permute-start(f32[1,4,128,128]{3,2,1,0:T(8,128)S(1)} %shard_map.125), channel_id=1, source_target_pairs={{0,1},{1,2},{2,3},{3,4},{4,5},{5,6},{6,7},{7,8},{8,9},{9,10},{10,1... | collective-permute-start | bytes 786440 | tf_op jit(solution)/shard_map/ppermute | solution.py:19
  56.4 6.8 %collective-permute-start.10 = (f32[144,128]{1,0:T(8,128)S(1)}, f32[144,128]{1,0:T(8,128)S(1)}, u32[]{:S(2)}, u32[]{:S(2)}) collective-permute-start(f32[144,128]{1,0:T(8,128)S(1)} %shard_map.124.kept_ref), channel_id=1, source_target_pairs={{0,8},{1,9},{2,10},{3,11},{4,12},{5,13},{6,14},{7,15},{8,0},{9,1},... | collective-permute-start | bytes 221192 | tf_op jit(solution)/shard_map/ppermute | solution.py:292
  63.2 4.4 %collective-permute-start.11 = (f32[144,128]{1,0:T(8,128)S(1)}, f32[144,128]{1,0:T(8,128)S(1)}, u32[]{:S(2)}, u32[]{:S(2)}) collective-permute-start(f32[144,128]{1,0:T(8,128)S(1)} %shard_map.127.mine_ref), channel_id=1, source_target_pairs={{0,4},{1,5},{2,6},{3,7},{4,0},{5,1},{6,2},{7,3},{8,12},{9,13},{10,... | collective-permute-start | bytes 221192 | tf_op jit(solution)/shard_map/ppermute | solution.py:292
  67.7 6.6 %collective-permute-start.12 = (f32[288,128]{1,0:T(8,128)S(1)}, f32[288,128]{1,0:T(8,128)S(1)}, u32[]{:S(2)}, u32[]{:S(2)}) collective-permute-start(f32[288,128]{1,0:T(8,128)S(1)} %shard_map.128.mine_ref), channel_id=1, source_target_pairs={{0,2},{1,3},{2,0},{3,1},{4,6},{5,7},{6,4},{7,5},{8,10},{9,11},{10,... | collective-permute-start | bytes 442376 | tf_op jit(solution)/shard_map/ppermute | solution.py:292
  74.3 1.6 %collective-permute-start.13 = (f32[576,128]{1,0:T(8,128)S(1)}, f32[576,128]{1,0:T(8,128)S(1)}, u32[]{:S(2)}, u32[]{:S(2)}) collective-permute-start(f32[576,128]{1,0:T(8,128)S(1)} %shard_map.129.mine_ref), channel_id=1, source_target_pairs={{0,1},{1,0},{2,3},{3,2},{4,5},{5,4},{6,7},{7,6},{8,9},{9,8},{10,11... | collective-permute-start | bytes 884744 | tf_op jit(solution)/shard_map/ppermute | solution.py:292

commit v3 on v2

--- a/solution.py
+++ b/solution.py
@@ -118,7 +118,7 @@
 
 
 PAIR = 3
-PIECES = ((1, 1), (2, 1), (3, 1))
+PIECES = ((0, 1), (1, 1), (2, 1))
 
 
 def gradient_kernel(
@@ -284,6 +284,7 @@
 def half_sum(kept, sent, axis, beside, waits):
     count = lax.axis_size(axis)
     bits = [1 << b for b in range(count.bit_length() - 1)]
+    bits = bits[:1] + bits[2:] + bits[1:2]
     vmem = pl.BlockSpec(memory_space=pltpu.VMEM)
     width = kept.shape[1]
 
@@ -411,11 +412,11 @@
     updated = []
 
     def waits(step):
-        if step == 1:
-            return arrived
+        if step == 3:
+            return arrived[: (1 if step == 3 else 9)]
         last = lax.axis_size(axis).bit_length() - 1 + 2
         if step == last - 1:
-            return arrived
+            return arrived[: (1 if step == 3 else 9)]
         if step == last:
             updated.append(update())
             return updated

time: 77.1 us -> 76 us (0.986)
  starting transfers between devices: 37.6 us -> 34.5 us
  waiting for transfers between devices: 21 us -> 22.9 us
    ppermute x7, starting transfers between devices: 14.5 us -> 3.04 us  [exchanged(): got = lax.ppermute(value, axis, [(i, i ^ bit) for i in range(count)])]
    ppermute x7, starting transfers between devices: 23.1 us -> 31.4 us  [passed_along(): lax.ppermute(value, axis, [(source, source + steps) for source in range(l...]
    ppermute x7, waiting for transfers between devices: 19.3 us -> 21.3 us  [exchanged(): got = lax.ppermute(value, axis, [(i, i ^ bit) for i in range(count)])]
  transfers between devices with their start and end apart: 14 -> 14, of which waited for: 7 -> 7; matrix products, arithmetic and copies ran while one was open for 0% -> 0% of each run, Pallas kernels for 17% -> 18%
where the time goes in v3:
time: 76 us; the launch traced here: 75.9 us
  starting transfers between devices  34.5 us (45%)
  waiting for transfers between devices  22.9 us (30%)
  Pallas kernels  15.1 us (20%)
  local copies, waits for them, and re-layouts  1.63 us (2%)
  between operations  1 us (1%)
    ppermute x7, starting transfers between devices, passed_along(): lax.ppermute(value, axis, [(source, source + steps) for source in range(l...  31.4 us
    ppermute x7, waiting for transfers between devices, exchanged(): got = lax.ppermute(value, axis, [(i, i ^ bit) for i in range(count)])  21.3 us
    pallas_call x2, Pallas kernels, body(): pl.pallas_call(functools.partial(gradient_kernel, start, axis), out_shape...  7.96 us
    pallas_call x1, Pallas kernels, update(): pl.pallas_call(functools.partial(update_kernel, axis), grid=(2 * slices,)...  3.19 us
    ppermute x7, starting transfers between devices, exchanged(): got = lax.ppermute(value, axis, [(i, i ^ bit) for i in range(count)])  3.04 us
    unnamed x16, local copies, waits for them, and re-layouts  1.63 us
    ppermute x7, waiting for transfers between devices, passed_along(): lax.ppermute(value, axis, [(source, source + steps) for source in range(l...  1.63 us
  transfers between devices with their start and end apart: 14, of which 7 were waited for; matrix products, arithmetic and copies ran while one was open for 0% of the time, Pallas kernels for 18%

profile of v3, /device:TPU:0, one launch (start us, length us, event | category | flops | bytes accessed | tf_op | source)
XLA Modules:
  0.0 75.9 jit_solution(6088791744689457930)
XLA Ops:
  1.4 2.3 %collective-permute-start = (s32[12]{0:T(128)S(1)}, s32[12]{0:T(128)S(1)}, u32[]{:S(2)}, u32[]{:S(2)}) collective-permute-start(s32[12]{0:T(128)S(1)} %pad_add_fusion.place_ref), channel_id=1, source_target_pairs={{0,1},{1,2},{2,3},{3,4},{4,5},{5,6},{6,7},{7,8},{8,9},{9,10},{10,1... | collective-permute-start | bytes 152 | tf_op jit(solution)/shard_map/ppermute | solution.py:19
  3.7 1.6 %copy-done = f32[2,2,128,1024]{3,2,1,0:T(8,128)S(1)} copy-done((f32[2,2,128,1024]{3,2,1,0:T(8,128)S(1)}, f32[2,2,128,1024]{3,2,1,0:T(8,128)}, u32[]{:S(2)}) %copy-start) | copy-done | bytes 2097176
  5.5 0.8 shard_map.114
  6.3 1.4 %collective-permute-start.1 = (f32[3,4,128,128]{3,2,1,0:T(8,128)S(1)}, f32[3,4,128,128]{3,2,1,0:T(8,128)S(1)}, u32[]{:S(2)}, u32[]{:S(2)}) collective-permute-start(f32[3,4,128,128]{3,2,1,0:T(8,128)S(1)} %shard_map.114), channel_id=1, source_target_pairs={{1,0},{2,1},{3,2},{4,3},{5,4},{6,5},{7,6},{8,7},{9,8},{10,9},{11,1... | collective-permute-start | bytes 2359304 | tf_op jit(solution)/shard_map/ppermute | solution.py:19
  7.8 0.8 shard_map.115
  8.5 1.3 %collective-permute-start.2 = (f32[3,4,128,128]{3,2,1,0:T(8,128)S(1)}, f32[3,4,128,128]{3,2,1,0:T(8,128)S(1)}, u32[]{:S(2)}, u32[]{:S(2)}) collective-permute-start(f32[3,4,128,128]{3,2,1,0:T(8,128)S(1)} %shard_map.115), channel_id=1, source_target_pairs={{1,0},{2,1},{3,2},{4,3},{5,4},{6,5},{7,6},{8,7},{9,8},{10,9},{11,1... | collective-permute-start | bytes 2359304 | tf_op jit(solution)/shard_map/ppermute | solution.py:19
  10.0 1.1 %shard_map.117.lit_ref = f32[128,1024]{1,0:T(8,128)S(1)} custom-call(s32[16]{0:T(128)S(1)} %copy-done.7, s32[12]{0:T(128)S(1)} %pad_add_fusion.place_ref, s32[12]{0:T(128)S(1)} %collective-permute-done.before_ref, f32[4,2,128,128]{3,2,1,0:T(8,128)S(1)} %get-tuple-element.44.probe_ref), custom_call_target="tpu_custom_call" | custom-call | tf_op jit(solution)/shard_map/pallas_call | solution.py:366
  11.1 1.6 %collective-permute-done.1.refs_0_.refs_1_.refs_2_ = f32[3,4,128,128]{3,2,1,0:T(8,128)S(1)} collective-permute-done((f32[3,4,128,128]{3,2,1,0:T(8,128)S(1)}, f32[3,4,128,128]{3,2,1,0:T(8,128)S(1)}, u32[]{:S(2)}, u32[]{:S(2)}) %collective-permute-start.1) | collective-permute-done | bytes 786464 | tf_op jit(solution)/shard_map/ppermute | solution.py:19
  12.7 7.1 %shard_map.118 = (f32[3,4,128,128]{3,2,1,0:T(8,128)S(1)}, f32[1152,128]{1,0:T(8,128)S(1)}) custom-call(s32[16]{0:T(128)S(1)} %copy-done.7, s32[12]{0:T(128)S(1)} %pad_add_fusion.place_ref, f32[2,2,128,1024]{3,2,1,0:T(8,128)S(1)} %shard_map.113.object_ref, f32[4,2,128,128]{3,2,1,0:T(8,128)S(1)} %get-tuple-element.44.probe_ref, ...), custom_call_target="tpu_custom_call" | custom-call | flops 1 | bytes 6291456 | tf_op jit(solution)/shard_map/pallas_call | solution.py:382
  19.9 11.6 %collective-permute-start.3 = (f32[3,4,128,128]{3,2,1,0:T(8,128)S(1)}, f32[3,4,128,128]{3,2,1,0:T(8,128)S(1)}, u32[]{:S(2)}, u32[]{:S(2)}) collective-permute-start(f32[3,4,128,128]{3,2,1,0:T(8,128)S(1)} %get-tuple-element.51.refs_0_), channel_id=1, source_target_pairs={{0,1},{1,2},{2,3},{3,4},{4,5},{5,6},{6,7},{7,8},{8,9},{9,10},{10,1... | collective-permute-start | bytes 2359304 | tf_op jit(solution)/shard_map/ppermute | solution.py:19
  31.5 0.9 %shard_map.119 = (f32[1,4,128,128]{3,2,1,0:T(8,128)S(1)}, f32[1,4,128,128]{3,2,1,0:T(8,128)S(1)}, f32[1,4,128,128]{3,2,1,0:T(8,128)S(1)}, f32[576,128]{1,0:T(8,128)S(1)}, f32[576,128]{1,0:T(8,128)S(1)}) custom-call(s32[16]{0:T(128)S(1)} %copy-done.7, s32[12]{0:T(128)S(1)} %pad_add_fusion.place_ref, f32[2,2,128,1024]{3,2,1,0:T(8,128)S(1)} %shard_map.113.object_ref, ...), custom_call_target="tpu_custom_call" | custom-call | flops 1 | bytes 6291456 | tf_op jit(solution)/shard_map/pallas_call | solution.py:382
  32.4 1.6 %collective-permute-done.5.got_ref = f32[576,128]{1,0:T(8,128)S(1)} collective-permute-done((f32[576,128]{1,0:T(8,128)S(1)}, f32[576,128]{1,0:T(8,128)S(1)}, u32[]{:S(2)}, u32[]{:S(2)}) %collective-permute-start.5) | collective-permute-done | bytes 294944 | tf_op jit(solution)/shard_map/ppermute | solution.py:293
  34.0 1.6 %collective-permute-start.7 = (f32[288,128]{1,0:T(8,128)S(1)}, f32[288,128]{1,0:T(8,128)S(1)}, u32[]{:S(2)}, u32[]{:S(2)}) collective-permute-start(f32[288,128]{1,0:T(8,128)S(1)} %get-tuple-element.59), channel_id=1, source_target_pairs={{0,4},{1,5},{2,6},{3,7},{4,0},{5,1},{6,2},{7,3},{8,12},{9,13},{10,... | collective-permute-start | bytes 442376 | tf_op jit(solution)/shard_map/ppermute | solution.py:293
  35.6 1.8 %collective-permute-start.4 = (f32[1,4,128,128]{3,2,1,0:T(8,128)S(1)}, f32[1,4,128,128]{3,2,1,0:T(8,128)S(1)}, u32[]{:S(2)}, u32[]{:S(2)}) collective-permute-start(f32[1,4,128,128]{3,2,1,0:T(8,128)S(1)} %shard_map.120), channel_id=1, source_target_pairs={{0,1},{1,2},{2,3},{3,4},{4,5},{5,6},{6,7},{7,8},{8,9},{9,10},{10,1... | collective-permute-start | bytes 786440 | tf_op jit(solution)/shard_map/ppermute | solution.py:19
  37.5 11.1 %collective-permute-start.6 = (f32[1,4,128,128]{3,2,1,0:T(8,128)S(1)}, f32[1,4,128,128]{3,2,1,0:T(8,128)S(1)}, u32[]{:S(2)}, u32[]{:S(2)}) collective-permute-start(f32[1,4,128,128]{3,2,1,0:T(8,128)S(1)} %shard_map.122), channel_id=1, source_target_pairs={{0,1},{1,2},{2,3},{3,4},{4,5},{5,6},{6,7},{7,8},{8,9},{9,10},{10,1... | collective-permute-start | bytes 786440 | tf_op jit(solution)/shard_map/ppermute | solution.py:19
  48.6 1.9 %collective-permute-start.8 = (f32[1,4,128,128]{3,2,1,0:T(8,128)S(1)}, f32[1,4,128,128]{3,2,1,0:T(8,128)S(1)}, u32[]{:S(2)}, u32[]{:S(2)}) collective-permute-start(f32[1,4,128,128]{3,2,1,0:T(8,128)S(1)} %shard_map.124), channel_id=1, source_target_pairs={{0,1},{1,2},{2,3},{3,4},{4,5},{5,6},{6,7},{7,8},{8,9},{9,10},{10,1... | collective-permute-start | bytes 786440 | tf_op jit(solution)/shard_map/ppermute | solution.py:19
  50.5 1.1 %collective-permute-start.9 = (f32[144,128]{1,0:T(8,128)S(1)}, f32[144,128]{1,0:T(8,128)S(1)}, u32[]{:S(2)}, u32[]{:S(2)}) collective-permute-start(f32[144,128]{1,0:T(8,128)S(1)} %get-tuple-element.62), channel_id=1, source_target_pairs={{0,8},{1,9},{2,10},{3,11},{4,12},{5,13},{6,14},{7,15},{8,0},{9,1},... | collective-permute-start | bytes 221192 | tf_op jit(solution)/shard_map/ppermute | solution.py:293
  51.6 6.0 %collective-permute-done.9.got_ref = f32[144,128]{1,0:T(8,128)S(1)} collective-permute-done((f32[144,128]{1,0:T(8,128)S(1)}, f32[144,128]{1,0:T(8,128)S(1)}, u32[]{:S(2)}, u32[]{:S(2)}) %collective-permute-start.9) | collective-permute-done | bytes 73760 | tf_op jit(solution)/shard_map/ppermute | solution.py:293
  57.8 4.3 %collective-permute-done.10.got_ref = f32[144,128]{1,0:T(8,128)S(1)} collective-permute-done((f32[144,128]{1,0:T(8,128)S(1)}, f32[144,128]{1,0:T(8,128)S(1)}, u32[]{:S(2)}, u32[]{:S(2)}) %collective-permute-start.10) | collective-permute-done | bytes 73760 | tf_op jit(solution)/shard_map/ppermute | solution.py:293
  62.2 5.8 %collective-permute-done.11.got_ref = f32[144,128]{1,0:T(8,128)S(1)} collective-permute-done((f32[144,128]{1,0:T(8,128)S(1)}, f32[144,128]{1,0:T(8,128)S(1)}, u32[]{:S(2)}, u32[]{:S(2)}) %collective-permute-start.11) | collective-permute-done | bytes 73760 | tf_op jit(solution)/shard_map/ppermute | solution.py:293
  68.2 3.2 %shard_map.125 = f32[2,2,128,1024]{3,2,1,0:T(8,128)} custom-call(s32[16]{0:T(128)S(1)} %copy-done.7, s32[12]{0:T(128)S(1)} %pad_add_fusion.place_ref, s32[12]{0:T(128)S(1)} %collective-permute-done.before_ref, f32[2,2,128,1024]{3,2,1,0:T(8,128)S(1)} %shard_map.113.object_ref, f32[128,1024]{1,0:T(8,128)S(1)} %shard_map.117.lit_ref, ...), custom_call_target="tpu_custom_call" | custom-call | flops 1 | bytes 12582912 | tf_op jit(solution)/shard_map/pallas_call | solution.py:426
  71.4 1.9 %collective-permute-done.12.got_ref = f32[288,128]{1,0:T(8,128)S(1)} collective-permute-done((f32[288,128]{1,0:T(8,128)S(1)}, f32[288,128]{1,0:T(8,128)S(1)}, u32[]{:S(2)}, u32[]{:S(2)}) %collective-permute-start.12) | collective-permute-done | bytes 147488 | tf_op jit(solution)/shard_map/ppermute | solution.py:293
  73.4 1.6 %collective-permute-done.13.got_ref = f32[576,128]{1,0:T(8,128)S(1)} collective-permute-done((f32[576,128]{1,0:T(8,128)S(1)}, f32[576,128]{1,0:T(8,128)S(1)}, u32[]{:S(2)}, u32[]{:S(2)}) %collective-permute-start.13) | collective-permute-done | bytes 294944 | tf_op jit(solution)/shard_map/ppermute | solution.py:293
  75.0 0.9 %shard_map.130 = f32[4,2,128,128]{3,2,1,0:T(8,128)} custom-call(f32[576,128]{1,0:T(8,128)S(1)} %shard_map.129.mine_ref, f32[576,128]{1,0:T(8,128)S(1)} %collective-permute-done.13.got_ref, f32[4,2,128,128]{3,2,1,0:T(8,128)S(1)} %get-tuple-element.44.probe_ref), custom_call_target="tpu_custom_call" | custom-call | tf_op jit(solution)/shard_map/pallas_call | solution.py:438
  (39 shorter events, 1.6 us)
Async XLA Ops:
  1.4 4.1 %collective-permute-start = (s32[12]{0:T(128)S(1)}, s32[12]{0:T(128)S(1)}, u32[]{:S(2)}, u32[]{:S(2)}) collective-permute-start(s32[12]{0:T(128)S(1)} %pad_add_fusion.place_ref), channel_id=1, source_target_pairs={{0,1},{1,2},{2,3},{3,4},{4,5},{5,6},{6,7},{7,8},{8,9},{9,10},{10,1... | collective-permute-start | bytes 152 | tf_op jit(solution)/shard_map/ppermute | solution.py:19
  3.7 1.6 %copy-start = (f32[2,2,128,1024]{3,2,1,0:T(8,128)S(1)}, f32[2,2,128,1024]{3,2,1,0:T(8,128)}, u32[]{:S(2)}) copy-start(f32[2,2,128,1024]{3,2,1,0:T(8,128)} %refs_0_.1) | copy-start | bytes 6291460
  6.2 3.6 %copy-start.1 = (f32[4,2,128,128]{3,2,1,0:T(8,128)S(1)}, f32[4,2,128,128]{3,2,1,0:T(8,128)}, u32[]{:S(2)}) copy-start(f32[4,2,128,128]{3,2,1,0:T(8,128)} %refs_0_.2) | copy-start | bytes 1572868
  6.3 3.6 %copy-start.2 = (f32[6,128,128]{2,1,0:T(8,128)S(1)}, f32[6,128,128]{2,1,0:T(8,128)}, u32[]{:S(2)}) copy-start(f32[6,128,128]{2,1,0:T(8,128)} %refs_1_) | copy-start | bytes 1179652
  6.3 3.6 %copy-start.3 = (bf16[512,256]{1,0:T(8,128)(2,1)S(1)}, bf16[512,256]{1,0:T(8,128)(2,1)}, u32[]{:S(2)}) copy-start(bf16[512,256]{1,0:T(8,128)(2,1)} %constant.11.clone.refs_5_) | copy-start | bytes 786436
  6.3 3.6 %copy-start.4 = (bf16[2,256,256]{2,1,0:T(8,128)(2,1)S(1)}, bf16[2,256,256]{2,1,0:T(8,128)(2,1)}, u32[]{:S(2)}) copy-start(bf16[2,256,256]{2,1,0:T(8,128)(2,1)} %constant.10.clone.refs_4_) | copy-start | bytes 786436
  6.3 3.6 %copy-start.5 = (bf16[512,256]{1,0:T(8,128)(2,1)S(1)}, bf16[512,256]{1,0:T(8,128)(2,1)}, u32[]{:S(2)}) copy-start(bf16[512,256]{1,0:T(8,128)(2,1)} %constant.9.clone.refs_3_) | copy-start | bytes 786436
  6.3 3.6 %copy-start.6 = (bf16[2,256,256]{2,1,0:T(8,128)(2,1)S(1)}, bf16[2,256,256]{2,1,0:T(8,128)(2,1)}, u32[]{:S(2)}) copy-start(bf16[2,256,256]{2,1,0:T(8,128)(2,1)} %constant.8.clone.refs_2_) | copy-start | bytes 786436
  6.3 3.7 %copy-start.7 = (s32[16]{0:T(128)S(1)}, s32[16]{0:T(128)}, u32[]{:S(2)}) copy-start(s32[16]{0:T(128)} %counts_ref.7) | copy-start | bytes 196
  6.3 6.4 %collective-permute-start.1 = (f32[3,4,128,128]{3,2,1,0:T(8,128)S(1)}, f32[3,4,128,128]{3,2,1,0:T(8,128)S(1)}, u32[]{:S(2)}, u32[]{:S(2)}) collective-permute-start(f32[3,4,128,128]{3,2,1,0:T(8,128)S(1)} %shard_map.114), channel_id=1, source_target_pairs={{1,0},{2,1},{3,2},{4,3},{5,4},{6,5},{7,6},{8,7},{9,8},{10,9},{11,1... | collective-permute-start | bytes 2359304 | tf_op jit(solution)/shard_map/ppermute | solution.py:19
  8.5 22.9 %collective-permute-start.2 = (f32[3,4,128,128]{3,2,1,0:T(8,128)S(1)}, f32[3,4,128,128]{3,2,1,0:T(8,128)S(1)}, u32[]{:S(2)}, u32[]{:S(2)}) collective-permute-start(f32[3,4,128,128]{3,2,1,0:T(8,128)S(1)} %shard_map.115), channel_id=1, source_target_pairs={{1,0},{2,1},{3,2},{4,3},{5,4},{6,5},{7,6},{8,7},{9,8},{10,9},{11,1... | collective-permute-start | bytes 2359304 | tf_op jit(solution)/shard_map/ppermute | solution.py:19
  19.9 37.8 %collective-permute-start.3 = (f32[3,4,128,128]{3,2,1,0:T(8,128)S(1)}, f32[3,4,128,128]{3,2,1,0:T(8,128)S(1)}, u32[]{:S(2)}, u32[]{:S(2)}) collective-permute-start(f32[3,4,128,128]{3,2,1,0:T(8,128)S(1)} %get-tuple-element.51.refs_0_), channel_id=1, source_target_pairs={{0,1},{1,2},{2,3},{3,4},{4,5},{5,6},{6,7},{7,8},{8,9},{9,10},{10,1... | collective-permute-start | bytes 2359304 | tf_op jit(solution)/shard_map/ppermute | solution.py:19
  32.3 1.6 %collective-permute-start.5 = (f32[576,128]{1,0:T(8,128)S(1)}, f32[576,128]{1,0:T(8,128)S(1)}, u32[]{:S(2)}, u32[]{:S(2)}) collective-permute-start(f32[576,128]{1,0:T(8,128)S(1)} %get-tuple-element.56), channel_id=1, source_target_pairs={{0,1},{1,0},{2,3},{3,2},{4,5},{5,4},{6,7},{7,6},{8,9},{9,8},{10,11... | collective-permute-start | bytes 884744 | tf_op jit(solution)/shard_map/ppermute | solution.py:293
  34.0 14.5 %collective-permute-start.7 = (f32[288,128]{1,0:T(8,128)S(1)}, f32[288,128]{1,0:T(8,128)S(1)}, u32[]{:S(2)}, u32[]{:S(2)}) collective-permute-start(f32[288,128]{1,0:T(8,128)S(1)} %get-tuple-element.59), channel_id=1, source_target_pairs={{0,4},{1,5},{2,6},{3,7},{4,0},{5,1},{6,2},{7,3},{8,12},{9,13},{10,... | collective-permute-start | bytes 442376 | tf_op jit(solution)/shard_map/ppermute | solution.py:293
  35.6 32.4 %collective-permute-start.4 = (f32[1,4,128,128]{3,2,1,0:T(8,128)S(1)}, f32[1,4,128,128]{3,2,1,0:T(8,128)S(1)}, u32[]{:S(2)}, u32[]{:S(2)}) collective-permute-start(f32[1,4,128,128]{3,2,1,0:T(8,128)S(1)} %shard_map.120), channel_id=1, source_target_pairs={{0,1},{1,2},{2,3},{3,4},{4,5},{5,6},{6,7},{7,8},{8,9},{9,10},{10,1... | collective-permute-start | bytes 786440 | tf_op jit(solution)/shard_map/ppermute | solution.py:19
  37.5 30.6 %collective-permute-start.6 = (f32[1,4,128,128]{3,2,1,0:T(8,128)S(1)}, f32[1,4,128,128]{3,2,1,0:T(8,128)S(1)}, u32[]{:S(2)}, u32[]{:S(2)}) collective-permute-start(f32[1,4,128,128]{3,2,1,0:T(8,128)S(1)} %shard_map.122), channel_id=1, source_target_pairs={{0,1},{1,2},{2,3},{3,4},{4,5},{5,6},{6,7},{7,8},{8,9},{9,10},{10,1... | collective-permute-start | bytes 786440 | tf_op jit(solution)/shard_map/ppermute | solution.py:19
  48.6 19.5 %collective-permute-start.8 = (f32[1,4,128,128]{3,2,1,0:T(8,128)S(1)}, f32[1,4,128,128]{3,2,1,0:T(8,128)S(1)}, u32[]{:S(2)}, u32[]{:S(2)}) collective-permute-start(f32[1,4,128,128]{3,2,1,0:T(8,128)S(1)} %shard_map.124), channel_id=1, source_target_pairs={{0,1},{1,2},{2,3},{3,4},{4,5},{5,6},{6,7},{7,8},{8,9},{9,10},{10,1... | collective-permute-start | bytes 786440 | tf_op jit(solution)/shard_map/ppermute | solution.py:19
  50.5 7.1 %collective-permute-start.9 = (f32[144,128]{1,0:T(8,128)S(1)}, f32[144,128]{1,0:T(8,128)S(1)}, u32[]{:S(2)}, u32[]{:S(2)}) collective-permute-start(f32[144,128]{1,0:T(8,128)S(1)} %get-tuple-element.62), channel_id=1, source_target_pairs={{0,8},{1,9},{2,10},{3,11},{4,12},{5,13},{6,14},{7,15},{8,0},{9,1},... | collective-permute-start | bytes 221192 | tf_op jit(solution)/shard_map/ppermute | solution.py:293
  57.7 4.4 %collective-permute-start.10 = (f32[144,128]{1,0:T(8,128)S(1)}, f32[144,128]{1,0:T(8,128)S(1)}, u32[]{:S(2)}, u32[]{:S(2)}) collective-permute-start(f32[144,128]{1,0:T(8,128)S(1)} %shard_map.126.kept_ref), channel_id=1, source_target_pairs={{0,2},{1,3},{2,0},{3,1},{4,6},{5,7},{6,4},{7,5},{8,10},{9,11},{10,... | collective-permute-start | bytes 221192 | tf_op jit(solution)/shard_map/ppermute | solution.py:293
  62.1 5.9 %collective-permute-start.11 = (f32[144,128]{1,0:T(8,128)S(1)}, f32[144,128]{1,0:T(8,128)S(1)}, u32[]{:S(2)}, u32[]{:S(2)}) collective-permute-start(f32[144,128]{1,0:T(8,128)S(1)} %shard_map.127.mine_ref), channel_id=1, source_target_pairs={{0,8},{1,9},{2,10},{3,11},{4,12},{5,13},{6,14},{7,15},{8,0},{9,1},... | collective-permute-start | bytes 221192 | tf_op jit(solution)/shard_map/ppermute | solution.py:293
  68.1 5.2 %collective-permute-start.12 = (f32[288,128]{1,0:T(8,128)S(1)}, f32[288,128]{1,0:T(8,128)S(1)}, u32[]{:S(2)}, u32[]{:S(2)}) collective-permute-start(f32[288,128]{1,0:T(8,128)S(1)} %shard_map.128.mine_ref), channel_id=1, source_target_pairs={{0,4},{1,5},{2,6},{3,7},{4,0},{5,1},{6,2},{7,3},{8,12},{9,13},{10,... | collective-permute-start | bytes 442376 | tf_op jit(solution)/shard_map/ppermute | solution.py:293
  73.3 1.6 %collective-permute-start.13 = (f32[576,128]{1,0:T(8,128)S(1)}, f32[576,128]{1,0:T(8,128)S(1)}, u32[]{:S(2)}, u32[]{:S(2)}) collective-permute-start(f32[576,128]{1,0:T(8,128)S(1)} %shard_map.129.mine_ref), channel_id=1, source_target_pairs={{0,1},{1,0},{2,3},{3,2},{4,5},{5,4},{6,7},{7,6},{8,9},{9,8},{10,11... | collective-permute-start | bytes 884744 | tf_op jit(solution)/shard_map/ppermute | solution.py:293

commit v4 on v3

--- a/solution.py
+++ b/solution.py
@@ -79,7 +79,7 @@
     ]
 
 
-def two_sided(blocks, right_ref, left_ref, group=2):
+def two_sided(blocks, right_ref, left_ref, group=4):
     width = blocks[0][0].shape[0]
     firsts = [right_stage(blocks[i : i + group], right_ref) for i in range(0, len(blocks), group)]
     return [block for first in firsts for block in left_stage(first, width, left_ref)]
@@ -118,7 +118,7 @@
 
 
 PAIR = 3
-PIECES = ((0, 1), (1, 1), (2, 1))
+PIECES = ((1, 1), (2, 1), (3, 1))
 
 
 def gradient_kernel(
@@ -284,7 +284,7 @@
 def half_sum(kept, sent, axis, beside, waits):
     count = lax.axis_size(axis)
     bits = [1 << b for b in range(count.bit_length() - 1)]
-    bits = bits[:1] + bits[2:] + bits[1:2]
+    bits = bits[:1] + bits[2:3] + bits[1:2] + bits[3:]
     vmem = pl.BlockSpec(memory_space=pltpu.VMEM)
     width = kept.shape[1]
 

time: 76 us -> 75.3 us (level)
    ppermute x7, starting transfers between devices: 3.04 us -> 12 us  [exchanged(): got = lax.ppermute(value, axis, [(i, i ^ bit) for i in range(count)])]
    ppermute x7, starting transfers between devices: 31.4 us -> 22.5 us  [passed_along(): lax.ppermute(value, axis, [(source, source + steps) for source in range(l...]
  transfers between devices with their start and end apart: 14 -> 14, of which waited for: 7 -> 7; matrix products, arithmetic and copies ran while one was open for 0% -> 0% of each run, Pallas kernels for 18% -> 17%
where the time goes in v4:
time: 75.3 us; the launch traced here: 75.1 us
  starting transfers between devices  34.6 us (46%)
  waiting for transfers between devices  22.4 us (30%)
  Pallas kernels  14.7 us (20%)
  local copies, waits for them, and re-layouts  1.63 us (2%)
  between operations  0.99 us (1%)
    ppermute x7, starting transfers between devices, passed_along(): lax.ppermute(value, axis, [(source, source + steps) for source in range(l...  22.5 us
    ppermute x7, waiting for transfers between devices, exchanged(): got = lax.ppermute(value, axis, [(i, i ^ bit) for i in range(count)])  20.7 us
    ppermute x7, starting transfers between devices, exchanged(): got = lax.ppermute(value, axis, [(i, i ^ bit) for i in range(count)])  12 us
    pallas_call x2, Pallas kernels, body(): pl.pallas_call(functools.partial(gradient_kernel, start, axis), out_shape...  7.81 us
    pallas_call x1, Pallas kernels, update(): pl.pallas_call(functools.partial(update_kernel, axis), grid=(2 * slices,)...  3.05 us
    ppermute x7, waiting for transfers between devices, passed_along(): lax.ppermute(value, axis, [(source, source + steps) for source in range(l...  1.74 us
    unnamed x16, local copies, waits for them, and re-layouts  1.63 us
    pallas_call x2, Pallas kernels, body(): pl.pallas_call(functools.partial(strip_kernel, start), out_shape=windows(...  1.51 us
  transfers between devices with their start and end apart: 14, of which 7 were waited for; matrix products, arithmetic and copies ran while one was open for 0% of the time, Pallas kernels for 17%

profile of v4, /device:TPU:0, one launch (start us, length us, event | category | flops | bytes accessed | tf_op | source)
XLA Modules:
  0.0 75.1 jit_solution(5078188563408302532)
XLA Ops:
  1.4 2.3 %collective-permute-start = (s32[12]{0:T(128)S(1)}, s32[12]{0:T(128)S(1)}, u32[]{:S(2)}, u32[]{:S(2)}) collective-permute-start(s32[12]{0:T(128)S(1)} %pad_add_fusion.place_ref), channel_id=1, source_target_pairs={{0,1},{1,2},{2,3},{3,4},{4,5},{5,6},{6,7},{7,8},{8,9},{9,10},{10,1... | collective-permute-start | bytes 152 | tf_op jit(solution)/shard_map/ppermute | solution.py:19
  3.7 1.6 %copy-done = f32[2,2,128,1024]{3,2,1,0:T(8,128)S(1)} copy-done((f32[2,2,128,1024]{3,2,1,0:T(8,128)S(1)}, f32[2,2,128,1024]{3,2,1,0:T(8,128)}, u32[]{:S(2)}) %copy-start) | copy-done | bytes 2097176
  5.5 0.8 %shard_map.114 = f32[3,4,128,128]{3,2,1,0:T(8,128)S(1)} custom-call(s32[12]{0:T(128)S(1)} %collective-permute-done.before_ref, f32[2,2,128,1024]{3,2,1,0:T(8,128)S(1)} %shard_map.113.object_ref), custom_call_target="tpu_custom_call" | custom-call | tf_op jit(solution)/shard_map/pallas_call | solution.py:356
  6.3 1.4 %collective-permute-start.1 = (f32[3,4,128,128]{3,2,1,0:T(8,128)S(1)}, f32[3,4,128,128]{3,2,1,0:T(8,128)S(1)}, u32[]{:S(2)}, u32[]{:S(2)}) collective-permute-start(f32[3,4,128,128]{3,2,1,0:T(8,128)S(1)} %shard_map.114), channel_id=1, source_target_pairs={{1,0},{2,1},{3,2},{4,3},{5,4},{6,5},{7,6},{8,7},{9,8},{10,9},{11,1... | collective-permute-start | bytes 2359304 | tf_op jit(solution)/shard_map/ppermute | solution.py:19
  8.5 1.3 %collective-permute-start.2 = (f32[3,4,128,128]{3,2,1,0:T(8,128)S(1)}, f32[3,4,128,128]{3,2,1,0:T(8,128)S(1)}, u32[]{:S(2)}, u32[]{:S(2)}) collective-permute-start(f32[3,4,128,128]{3,2,1,0:T(8,128)S(1)} %shard_map.115), channel_id=1, source_target_pairs={{1,0},{2,1},{3,2},{4,3},{5,4},{6,5},{7,6},{8,7},{9,8},{10,9},{11,1... | collective-permute-start | bytes 2359304 | tf_op jit(solution)/shard_map/ppermute | solution.py:19
  10.0 1.0 %shard_map.117.lit_ref = f32[128,1024]{1,0:T(8,128)S(1)} custom-call(s32[16]{0:T(128)S(1)} %copy-done.7, s32[12]{0:T(128)S(1)} %pad_add_fusion.place_ref, s32[12]{0:T(128)S(1)} %collective-permute-done.before_ref, f32[4,2,128,128]{3,2,1,0:T(8,128)S(1)} %get-tuple-element.44.probe_ref), custom_call_target="tpu_custom_call" | custom-call | tf_op jit(solution)/shard_map/pallas_call | solution.py:366
  11.0 1.7 %collective-permute-done.1.refs_0_.refs_1_.refs_2_ = f32[3,4,128,128]{3,2,1,0:T(8,128)S(1)} collective-permute-done((f32[3,4,128,128]{3,2,1,0:T(8,128)S(1)}, f32[3,4,128,128]{3,2,1,0:T(8,128)S(1)}, u32[]{:S(2)}, u32[]{:S(2)}) %collective-permute-start.1) | collective-permute-done | bytes 786464 | tf_op jit(solution)/shard_map/ppermute | solution.py:19
  12.7 7.0 %shard_map.118 = (f32[3,4,128,128]{3,2,1,0:T(8,128)S(1)}, f32[1152,128]{1,0:T(8,128)S(1)}) custom-call(s32[16]{0:T(128)S(1)} %copy-done.7, s32[12]{0:T(128)S(1)} %pad_add_fusion.place_ref, f32[2,2,128,1024]{3,2,1,0:T(8,128)S(1)} %shard_map.113.object_ref, f32[4,2,128,128]{3,2,1,0:T(8,128)S(1)} %get-tuple-element.44.probe_ref, ...), custom_call_target="tpu_custom_call" | custom-call | flops 1 | bytes 6291456 | tf_op jit(solution)/shard_map/pallas_call | solution.py:382
  19.7 11.6 %collective-permute-start.3 = (f32[3,4,128,128]{3,2,1,0:T(8,128)S(1)}, f32[3,4,128,128]{3,2,1,0:T(8,128)S(1)}, u32[]{:S(2)}, u32[]{:S(2)}) collective-permute-start(f32[3,4,128,128]{3,2,1,0:T(8,128)S(1)} %get-tuple-element.51.refs_0_), channel_id=1, source_target_pairs={{0,1},{1,2},{2,3},{3,4},{4,5},{5,6},{6,7},{7,8},{8,9},{9,10},{10,1... | collective-permute-start | bytes 2359304 | tf_op jit(solution)/shard_map/ppermute | solution.py:19
  31.3 0.9 %shard_map.119 = (f32[1,4,128,128]{3,2,1,0:T(8,128)S(1)}, f32[1,4,128,128]{3,2,1,0:T(8,128)S(1)}, f32[1,4,128,128]{3,2,1,0:T(8,128)S(1)}, f32[576,128]{1,0:T(8,128)S(1)}, f32[576,128]{1,0:T(8,128)S(1)}) custom-call(s32[16]{0:T(128)S(1)} %copy-done.7, s32[12]{0:T(128)S(1)} %pad_add_fusion.place_ref, f32[2,2,128,1024]{3,2,1,0:T(8,128)S(1)} %shard_map.113.object_ref, ...), custom_call_target="tpu_custom_call" | custom-call | flops 1 | bytes 6291456 | tf_op jit(solution)/shard_map/pallas_call | solution.py:382
  32.2 1.6 %collective-permute-done.4.got_ref = f32[576,128]{1,0:T(8,128)S(1)} collective-permute-done((f32[576,128]{1,0:T(8,128)S(1)}, f32[576,128]{1,0:T(8,128)S(1)}, u32[]{:S(2)}, u32[]{:S(2)}) %collective-permute-start.4) | collective-permute-done | bytes 294944 | tf_op jit(solution)/shard_map/ppermute | solution.py:293
  33.9 1.6 %collective-permute-start.6 = (f32[288,128]{1,0:T(8,128)S(1)}, f32[288,128]{1,0:T(8,128)S(1)}, u32[]{:S(2)}, u32[]{:S(2)}) collective-permute-start(f32[288,128]{1,0:T(8,128)S(1)} %get-tuple-element.58), channel_id=1, source_target_pairs={{0,4},{1,5},{2,6},{3,7},{4,0},{5,1},{6,2},{7,3},{8,12},{9,13},{10,... | collective-permute-start | bytes 442376 | tf_op jit(solution)/shard_map/ppermute | solution.py:293
  35.4 4.4 %collective-permute-done.6.got_ref = f32[288,128]{1,0:T(8,128)S(1)} collective-permute-done((f32[288,128]{1,0:T(8,128)S(1)}, f32[288,128]{1,0:T(8,128)S(1)}, u32[]{:S(2)}, u32[]{:S(2)}) %collective-permute-start.6) | collective-permute-done | bytes 147488 | tf_op jit(solution)/shard_map/ppermute | solution.py:293
  39.8 8.8 %collective-permute-start.8 = (f32[144,128]{1,0:T(8,128)S(1)}, f32[144,128]{1,0:T(8,128)S(1)}, u32[]{:S(2)}, u32[]{:S(2)}) collective-permute-start(f32[144,128]{1,0:T(8,128)S(1)} %get-tuple-element.61), channel_id=1, source_target_pairs={{0,2},{1,3},{2,0},{3,1},{4,6},{5,7},{6,4},{7,5},{8,10},{9,11},{10,... | collective-permute-start | bytes 221192 | tf_op jit(solution)/shard_map/ppermute | solution.py:293
  48.6 1.3 %collective-permute-start.5 = (f32[1,4,128,128]{3,2,1,0:T(8,128)S(1)}, f32[1,4,128,128]{3,2,1,0:T(8,128)S(1)}, u32[]{:S(2)}, u32[]{:S(2)}) collective-permute-start(f32[1,4,128,128]{3,2,1,0:T(8,128)S(1)} %shard_map.121), channel_id=1, source_target_pairs={{0,1},{1,2},{2,3},{3,4},{4,5},{5,6},{6,7},{7,8},{8,9},{9,10},{10,1... | collective-permute-start | bytes 786440 | tf_op jit(solution)/shard_map/ppermute | solution.py:19
  50.0 2.7 %collective-permute-start.7 = (f32[1,4,128,128]{3,2,1,0:T(8,128)S(1)}, f32[1,4,128,128]{3,2,1,0:T(8,128)S(1)}, u32[]{:S(2)}, u32[]{:S(2)}) collective-permute-start(f32[1,4,128,128]{3,2,1,0:T(8,128)S(1)} %shard_map.123), channel_id=1, source_target_pairs={{0,1},{1,2},{2,3},{3,4},{4,5},{5,6},{6,7},{7,8},{8,9},{9,10},{10,1... | collective-permute-start | bytes 786440 | tf_op jit(solution)/shard_map/ppermute | solution.py:19
  52.7 1.9 %collective-permute-start.9 = (f32[1,4,128,128]{3,2,1,0:T(8,128)S(1)}, f32[1,4,128,128]{3,2,1,0:T(8,128)S(1)}, u32[]{:S(2)}, u32[]{:S(2)}) collective-permute-start(f32[1,4,128,128]{3,2,1,0:T(8,128)S(1)} %shard_map.125), channel_id=1, source_target_pairs={{0,1},{1,2},{2,3},{3,4},{4,5},{5,6},{6,7},{7,8},{8,9},{9,10},{10,1... | collective-permute-start | bytes 786440 | tf_op jit(solution)/shard_map/ppermute | solution.py:19
  54.7 7.0 %collective-permute-done.10.got_ref = f32[144,128]{1,0:T(8,128)S(1)} collective-permute-done((f32[144,128]{1,0:T(8,128)S(1)}, f32[144,128]{1,0:T(8,128)S(1)}, u32[]{:S(2)}, u32[]{:S(2)}) %collective-permute-start.10) | collective-permute-done | bytes 73760 | tf_op jit(solution)/shard_map/ppermute | solution.py:293
  61.7 1.3 %collective-permute-start.11 = (f32[144,128]{1,0:T(8,128)S(1)}, f32[144,128]{1,0:T(8,128)S(1)}, u32[]{:S(2)}, u32[]{:S(2)}) collective-permute-start(f32[144,128]{1,0:T(8,128)S(1)} %shard_map.127.mine_ref), channel_id=1, source_target_pairs={{0,2},{1,3},{2,0},{3,1},{4,6},{5,7},{6,4},{7,5},{8,10},{9,11},{10,... | collective-permute-start | bytes 221192 | tf_op jit(solution)/shard_map/ppermute | solution.py:293
  63.0 3.7 %collective-permute-done.11.got_ref = f32[144,128]{1,0:T(8,128)S(1)} collective-permute-done((f32[144,128]{1,0:T(8,128)S(1)}, f32[144,128]{1,0:T(8,128)S(1)}, u32[]{:S(2)}, u32[]{:S(2)}) %collective-permute-start.11) | collective-permute-done | bytes 73760 | tf_op jit(solution)/shard_map/ppermute | solution.py:293
  66.9 3.1 %shard_map.126 = f32[2,2,128,1024]{3,2,1,0:T(8,128)} custom-call(s32[16]{0:T(128)S(1)} %copy-done.7, s32[12]{0:T(128)S(1)} %pad_add_fusion.place_ref, s32[12]{0:T(128)S(1)} %collective-permute-done.before_ref, f32[2,2,128,1024]{3,2,1,0:T(8,128)S(1)} %shard_map.113.object_ref, f32[128,1024]{1,0:T(8,128)S(1)} %shard_map.117.lit_ref, ...), custom_call_target="tpu_custom_call" | custom-call | flops 1 | bytes 12582912 | tf_op jit(solution)/shard_map/pallas_call | solution.py:426
  69.9 2.5 %collective-permute-done.12.got_ref = f32[288,128]{1,0:T(8,128)S(1)} collective-permute-done((f32[288,128]{1,0:T(8,128)S(1)}, f32[288,128]{1,0:T(8,128)S(1)}, u32[]{:S(2)}, u32[]{:S(2)}) %collective-permute-start.12) | collective-permute-done | bytes 147488 | tf_op jit(solution)/shard_map/ppermute | solution.py:293
  72.6 1.6 %collective-permute-done.13.got_ref = f32[576,128]{1,0:T(8,128)S(1)} collective-permute-done((f32[576,128]{1,0:T(8,128)S(1)}, f32[576,128]{1,0:T(8,128)S(1)}, u32[]{:S(2)}, u32[]{:S(2)}) %collective-permute-start.13) | collective-permute-done | bytes 294944 | tf_op jit(solution)/shard_map/ppermute | solution.py:293
  74.1 0.9 %shard_map.130 = f32[4,2,128,128]{3,2,1,0:T(8,128)} custom-call(f32[576,128]{1,0:T(8,128)S(1)} %shard_map.129.mine_ref, f32[576,128]{1,0:T(8,128)S(1)} %collective-permute-done.13.got_ref, f32[4,2,128,128]{3,2,1,0:T(8,128)S(1)} %get-tuple-element.44.probe_ref), custom_call_target="tpu_custom_call" | custom-call | tf_op jit(solution)/shard_map/pallas_call | solution.py:438
  (39 shorter events, 2.4 us)
Async XLA Ops:
  1.4 4.1 %collective-permute-start = (s32[12]{0:T(128)S(1)}, s32[12]{0:T(128)S(1)}, u32[]{:S(2)}, u32[]{:S(2)}) collective-permute-start(s32[12]{0:T(128)S(1)} %pad_add_fusion.place_ref), channel_id=1, source_target_pairs={{0,1},{1,2},{2,3},{3,4},{4,5},{5,6},{6,7},{7,8},{8,9},{9,10},{10,1... | collective-permute-start | bytes 152 | tf_op jit(solution)/shard_map/ppermute | solution.py:19
  3.7 1.6 %copy-start = (f32[2,2,128,1024]{3,2,1,0:T(8,128)S(1)}, f32[2,2,128,1024]{3,2,1,0:T(8,128)}, u32[]{:S(2)}) copy-start(f32[2,2,128,1024]{3,2,1,0:T(8,128)} %refs_0_.1) | copy-start | bytes 6291460
  6.2 3.6 %copy-start.1 = (f32[4,2,128,128]{3,2,1,0:T(8,128)S(1)}, f32[4,2,128,128]{3,2,1,0:T(8,128)}, u32[]{:S(2)}) copy-start(f32[4,2,128,128]{3,2,1,0:T(8,128)} %refs_0_.2) | copy-start | bytes 1572868
  6.3 3.6 %copy-start.2 = (f32[6,128,128]{2,1,0:T(8,128)S(1)}, f32[6,128,128]{2,1,0:T(8,128)}, u32[]{:S(2)}) copy-start(f32[6,128,128]{2,1,0:T(8,128)} %refs_1_) | copy-start | bytes 1179652
  6.3 3.6 %copy-start.3 = (bf16[2,256,256]{2,1,0:T(8,128)(2,1)S(1)}, bf16[2,256,256]{2,1,0:T(8,128)(2,1)}, u32[]{:S(2)}) copy-start(bf16[2,256,256]{2,1,0:T(8,128)(2,1)} %constant.8.clone.refs_2_) | copy-start | bytes 786436
  6.3 3.6 %copy-start.4 = (bf16[512,256]{1,0:T(8,128)(2,1)S(1)}, bf16[512,256]{1,0:T(8,128)(2,1)}, u32[]{:S(2)}) copy-start(bf16[512,256]{1,0:T(8,128)(2,1)} %constant.9.clone.refs_3_) | copy-start | bytes 786436
  6.3 3.6 %copy-start.5 = (bf16[2,256,256]{2,1,0:T(8,128)(2,1)S(1)}, bf16[2,256,256]{2,1,0:T(8,128)(2,1)}, u32[]{:S(2)}) copy-start(bf16[2,256,256]{2,1,0:T(8,128)(2,1)} %constant.10.clone.refs_4_) | copy-start | bytes 786436
  6.3 3.6 %copy-start.6 = (bf16[512,256]{1,0:T(8,128)(2,1)S(1)}, bf16[512,256]{1,0:T(8,128)(2,1)}, u32[]{:S(2)}) copy-start(bf16[512,256]{1,0:T(8,128)(2,1)} %constant.11.clone.refs_5_) | copy-start | bytes 786436
  6.3 3.7 %copy-start.7 = (s32[16]{0:T(128)S(1)}, s32[16]{0:T(128)}, u32[]{:S(2)}) copy-start(s32[16]{0:T(128)} %counts_ref.7) | copy-start | bytes 196
  6.3 6.4 %collective-permute-start.1 = (f32[3,4,128,128]{3,2,1,0:T(8,128)S(1)}, f32[3,4,128,128]{3,2,1,0:T(8,128)S(1)}, u32[]{:S(2)}, u32[]{:S(2)}) collective-permute-start(f32[3,4,128,128]{3,2,1,0:T(8,128)S(1)} %shard_map.114), channel_id=1, source_target_pairs={{1,0},{2,1},{3,2},{4,3},{5,4},{6,5},{7,6},{8,7},{9,8},{10,9},{11,1... | collective-permute-start | bytes 2359304 | tf_op jit(solution)/shard_map/ppermute | solution.py:19
  8.5 22.8 %collective-permute-start.2 = (f32[3,4,128,128]{3,2,1,0:T(8,128)S(1)}, f32[3,4,128,128]{3,2,1,0:T(8,128)S(1)}, u32[]{:S(2)}, u32[]{:S(2)}) collective-permute-start(f32[3,4,128,128]{3,2,1,0:T(8,128)S(1)} %shard_map.115), channel_id=1, source_target_pairs={{1,0},{2,1},{3,2},{4,3},{5,4},{6,5},{7,6},{8,7},{9,8},{10,9},{11,1... | collective-permute-start | bytes 2359304 | tf_op jit(solution)/shard_map/ppermute | solution.py:19
  19.7 33.0 %collective-permute-start.3 = (f32[3,4,128,128]{3,2,1,0:T(8,128)S(1)}, f32[3,4,128,128]{3,2,1,0:T(8,128)S(1)}, u32[]{:S(2)}, u32[]{:S(2)}) collective-permute-start(f32[3,4,128,128]{3,2,1,0:T(8,128)S(1)} %get-tuple-element.51.refs_0_), channel_id=1, source_target_pairs={{0,1},{1,2},{2,3},{3,4},{4,5},{5,6},{6,7},{7,8},{8,9},{9,10},{10,1... | collective-permute-start | bytes 2359304 | tf_op jit(solution)/shard_map/ppermute | solution.py:19
  32.2 1.6 %collective-permute-start.4 = (f32[576,128]{1,0:T(8,128)S(1)}, f32[576,128]{1,0:T(8,128)S(1)}, u32[]{:S(2)}, u32[]{:S(2)}) collective-permute-start(f32[576,128]{1,0:T(8,128)S(1)} %get-tuple-element.57), channel_id=1, source_target_pairs={{0,1},{1,0},{2,3},{3,2},{4,5},{5,4},{6,7},{7,6},{8,9},{9,8},{10,11... | collective-permute-start | bytes 884744 | tf_op jit(solution)/shard_map/ppermute | solution.py:293
  33.9 6.0 %collective-permute-start.6 = (f32[288,128]{1,0:T(8,128)S(1)}, f32[288,128]{1,0:T(8,128)S(1)}, u32[]{:S(2)}, u32[]{:S(2)}) collective-permute-start(f32[288,128]{1,0:T(8,128)S(1)} %get-tuple-element.58), channel_id=1, source_target_pairs={{0,4},{1,5},{2,6},{3,7},{4,0},{5,1},{6,2},{7,3},{8,12},{9,13},{10,... | collective-permute-start | bytes 442376 | tf_op jit(solution)/shard_map/ppermute | solution.py:293
  39.8 12.8 %collective-permute-start.8 = (f32[144,128]{1,0:T(8,128)S(1)}, f32[144,128]{1,0:T(8,128)S(1)}, u32[]{:S(2)}, u32[]{:S(2)}) collective-permute-start(f32[144,128]{1,0:T(8,128)S(1)} %get-tuple-element.61), channel_id=1, source_target_pairs={{0,2},{1,3},{2,0},{3,1},{4,6},{5,7},{6,4},{7,5},{8,10},{9,11},{10,... | collective-permute-start | bytes 221192 | tf_op jit(solution)/shard_map/ppermute | solution.py:293
  48.6 18.1 %collective-permute-start.5 = (f32[1,4,128,128]{3,2,1,0:T(8,128)S(1)}, f32[1,4,128,128]{3,2,1,0:T(8,128)S(1)}, u32[]{:S(2)}, u32[]{:S(2)}) collective-permute-start(f32[1,4,128,128]{3,2,1,0:T(8,128)S(1)} %shard_map.121), channel_id=1, source_target_pairs={{0,1},{1,2},{2,3},{3,4},{4,5},{5,6},{6,7},{7,8},{8,9},{9,10},{10,1... | collective-permute-start | bytes 786440 | tf_op jit(solution)/shard_map/ppermute | solution.py:19
  50.0 16.8 %collective-permute-start.7 = (f32[1,4,128,128]{3,2,1,0:T(8,128)S(1)}, f32[1,4,128,128]{3,2,1,0:T(8,128)S(1)}, u32[]{:S(2)}, u32[]{:S(2)}) collective-permute-start(f32[1,4,128,128]{3,2,1,0:T(8,128)S(1)} %shard_map.123), channel_id=1, source_target_pairs={{0,1},{1,2},{2,3},{3,4},{4,5},{5,6},{6,7},{7,8},{8,9},{9,10},{10,1... | collective-permute-start | bytes 786440 | tf_op jit(solution)/shard_map/ppermute | solution.py:19
  52.7 14.0 %collective-permute-start.9 = (f32[1,4,128,128]{3,2,1,0:T(8,128)S(1)}, f32[1,4,128,128]{3,2,1,0:T(8,128)S(1)}, u32[]{:S(2)}, u32[]{:S(2)}) collective-permute-start(f32[1,4,128,128]{3,2,1,0:T(8,128)S(1)} %shard_map.125), channel_id=1, source_target_pairs={{0,1},{1,2},{2,3},{3,4},{4,5},{5,6},{6,7},{7,8},{8,9},{9,10},{10,1... | collective-permute-start | bytes 786440 | tf_op jit(solution)/shard_map/ppermute | solution.py:19
  54.6 7.1 %collective-permute-start.10 = (f32[144,128]{1,0:T(8,128)S(1)}, f32[144,128]{1,0:T(8,128)S(1)}, u32[]{:S(2)}, u32[]{:S(2)}) collective-permute-start(f32[144,128]{1,0:T(8,128)S(1)} %shard_map.124.kept_ref), channel_id=1, source_target_pairs={{0,8},{1,9},{2,10},{3,11},{4,12},{5,13},{6,14},{7,15},{8,0},{9,1},... | collective-permute-start | bytes 221192 | tf_op jit(solution)/shard_map/ppermute | solution.py:293
  61.7 5.0 %collective-permute-start.11 = (f32[144,128]{1,0:T(8,128)S(1)}, f32[144,128]{1,0:T(8,128)S(1)}, u32[]{:S(2)}, u32[]{:S(2)}) collective-permute-start(f32[144,128]{1,0:T(8,128)S(1)} %shard_map.127.mine_ref), channel_id=1, source_target_pairs={{0,2},{1,3},{2,0},{3,1},{4,6},{5,7},{6,4},{7,5},{8,10},{9,11},{10,... | collective-permute-start | bytes 221192 | tf_op jit(solution)/shard_map/ppermute | solution.py:293
  66.7 5.7 %collective-permute-start.12 = (f32[288,128]{1,0:T(8,128)S(1)}, f32[288,128]{1,0:T(8,128)S(1)}, u32[]{:S(2)}, u32[]{:S(2)}) collective-permute-start(f32[288,128]{1,0:T(8,128)S(1)} %shard_map.128.mine_ref), channel_id=1, source_target_pairs={{0,4},{1,5},{2,6},{3,7},{4,0},{5,1},{6,2},{7,3},{8,12},{9,13},{10,... | collective-permute-start | bytes 442376 | tf_op jit(solution)/shard_map/ppermute | solution.py:293
  72.5 1.6 %collective-permute-start.13 = (f32[576,128]{1,0:T(8,128)S(1)}, f32[576,128]{1,0:T(8,128)S(1)}, u32[]{:S(2)}, u32[]{:S(2)}) collective-permute-start(f32[576,128]{1,0:T(8,128)S(1)} %shard_map.129.mine_ref), channel_id=1, source_target_pairs={{0,1},{1,0},{2,3},{3,2},{4,5},{5,4},{6,7},{7,6},{8,9},{9,8},{10,11... | collective-permute-start | bytes 884744 | tf_op jit(solution)/shard_map/ppermute | solution.py:293

commit v5 on v3

--- a/solution.py
+++ b/solution.py
@@ -79,7 +79,7 @@
     ]
 
 
-def two_sided(blocks, right_ref, left_ref, group=2):
+def two_sided(blocks, right_ref, left_ref, group=4):
     width = blocks[0][0].shape[0]
     firsts = [right_stage(blocks[i : i + group], right_ref) for i in range(0, len(blocks), group)]
     return [block for first in firsts for block in left_stage(first, width, left_ref)]

time: 76 us -> 75.2 us (0.989)
  waiting for transfers between devices: 22.9 us -> 19.1 us
  starting transfers between devices: 34.5 us -> 37.9 us
    ppermute x7, starting transfers between devices: 3.04 us -> 8.03 us  [exchanged(): got = lax.ppermute(value, axis, [(i, i ^ bit) for i in range(count)])]
    ppermute x7, waiting for transfers between devices: 21.3 us -> 17.3 us  [exchanged(): got = lax.ppermute(value, axis, [(i, i ^ bit) for i in range(count)])]
    ppermute x7, starting transfers between devices: 31.4 us -> 29.8 us  [passed_along(): lax.ppermute(value, axis, [(source, source + steps) for source in range(l...]
  transfers between devices with their start and end apart: 14 -> 14, of which waited for: 7 -> 7; matrix products, arithmetic and copies ran while one was open for 0% -> 0% of each run, Pallas kernels for 18% -> 17%
where the time goes in v5:
time: 75.2 us; the launch traced here: 75.1 us
  starting transfers between devices  37.9 us (50%)
  waiting for transfers between devices  19.1 us (25%)
  Pallas kernels  14.8 us (20%)
  local copies, waits for them, and re-layouts  1.63 us (2%)
  between operations  0.98 us (1%)
    ppermute x7, starting transfers between devices, passed_along(): lax.ppermute(value, axis, [(source, source + steps) for source in range(l...  29.8 us
    ppermute x7, waiting for transfers between devices, exchanged(): got = lax.ppermute(value, axis, [(i, i ^ bit) for i in range(count)])  17.3 us
    ppermute x7, starting transfers between devices, exchanged(): got = lax.ppermute(value, axis, [(i, i ^ bit) for i in range(count)])  8.03 us
    pallas_call x2, Pallas kernels, body(): pl.pallas_call(functools.partial(gradient_kernel, start, axis), out_shape...  7.81 us
    pallas_call x1, Pallas kernels, update(): pl.pallas_call(functools.partial(update_kernel, axis), grid=(2 * slices,)...  3.11 us
    ppermute x7, waiting for transfers between devices, passed_along(): lax.ppermute(value, axis, [(source, source + steps) for source in range(l...  1.74 us
    unnamed x16, local copies, waits for them, and re-layouts  1.63 us
    pallas_call x2, Pallas kernels, body(): pl.pallas_call(functools.partial(strip_kernel, start), out_shape=windows(...  1.51 us
  transfers between devices with their start and end apart: 14, of which 7 were waited for; matrix products, arithmetic and copies ran while one was open for 0% of the time, Pallas kernels for 17%

profile of v5, /device:TPU:0, one launch (start us, length us, event | category | flops | bytes accessed | tf_op | source)
XLA Modules:
  0.0 75.1 jit_solution(7442025618319914781)
XLA Ops:
  1.4 2.3 %collective-permute-start = (s32[12]{0:T(128)S(1)}, s32[12]{0:T(128)S(1)}, u32[]{:S(2)}, u32[]{:S(2)}) collective-permute-start(s32[12]{0:T(128)S(1)} %pad_add_fusion.place_ref), channel_id=1, source_target_pairs={{0,1},{1,2},{2,3},{3,4},{4,5},{5,6},{6,7},{7,8},{8,9},{9,10},{10,1... | collective-permute-start | bytes 152 | tf_op jit(solution)/shard_map/ppermute | solution.py:19
  3.7 1.6 %copy-done = f32[2,2,128,1024]{3,2,1,0:T(8,128)S(1)} copy-done((f32[2,2,128,1024]{3,2,1,0:T(8,128)S(1)}, f32[2,2,128,1024]{3,2,1,0:T(8,128)}, u32[]{:S(2)}) %copy-start) | copy-done | bytes 2097176
  6.3 1.4 %collective-permute-start.1 = (f32[3,4,128,128]{3,2,1,0:T(8,128)S(1)}, f32[3,4,128,128]{3,2,1,0:T(8,128)S(1)}, u32[]{:S(2)}, u32[]{:S(2)}) collective-permute-start(f32[3,4,128,128]{3,2,1,0:T(8,128)S(1)} %shard_map.114), channel_id=1, source_target_pairs={{1,0},{2,1},{3,2},{4,3},{5,4},{6,5},{7,6},{8,7},{9,8},{10,9},{11,1... | collective-permute-start | bytes 2359304 | tf_op jit(solution)/shard_map/ppermute | solution.py:19
  8.5 1.3 %collective-permute-start.2 = (f32[3,4,128,128]{3,2,1,0:T(8,128)S(1)}, f32[3,4,128,128]{3,2,1,0:T(8,128)S(1)}, u32[]{:S(2)}, u32[]{:S(2)}) collective-permute-start(f32[3,4,128,128]{3,2,1,0:T(8,128)S(1)} %shard_map.115), channel_id=1, source_target_pairs={{1,0},{2,1},{3,2},{4,3},{5,4},{6,5},{7,6},{8,7},{9,8},{10,9},{11,1... | collective-permute-start | bytes 2359304 | tf_op jit(solution)/shard_map/ppermute | solution.py:19
  10.0 1.0 %shard_map.117.lit_ref = f32[128,1024]{1,0:T(8,128)S(1)} custom-call(s32[16]{0:T(128)S(1)} %copy-done.7, s32[12]{0:T(128)S(1)} %pad_add_fusion.place_ref, s32[12]{0:T(128)S(1)} %collective-permute-done.before_ref, f32[4,2,128,128]{3,2,1,0:T(8,128)S(1)} %get-tuple-element.44.probe_ref), custom_call_target="tpu_custom_call" | custom-call | tf_op jit(solution)/shard_map/pallas_call | solution.py:366
  11.0 1.7 %collective-permute-done.1.refs_0_.refs_1_.refs_2_ = f32[3,4,128,128]{3,2,1,0:T(8,128)S(1)} collective-permute-done((f32[3,4,128,128]{3,2,1,0:T(8,128)S(1)}, f32[3,4,128,128]{3,2,1,0:T(8,128)S(1)}, u32[]{:S(2)}, u32[]{:S(2)}) %collective-permute-start.1) | collective-permute-done | bytes 786464 | tf_op jit(solution)/shard_map/ppermute | solution.py:19
  12.7 7.0 %shard_map.118 = (f32[3,4,128,128]{3,2,1,0:T(8,128)S(1)}, f32[1152,128]{1,0:T(8,128)S(1)}) custom-call(s32[16]{0:T(128)S(1)} %copy-done.7, s32[12]{0:T(128)S(1)} %pad_add_fusion.place_ref, f32[2,2,128,1024]{3,2,1,0:T(8,128)S(1)} %shard_map.113.object_ref, f32[4,2,128,128]{3,2,1,0:T(8,128)S(1)} %get-tuple-element.44.probe_ref, ...), custom_call_target="tpu_custom_call" | custom-call | flops 1 | bytes 6291456 | tf_op jit(solution)/shard_map/pallas_call | solution.py:382
  19.7 11.6 %collective-permute-start.3 = (f32[3,4,128,128]{3,2,1,0:T(8,128)S(1)}, f32[3,4,128,128]{3,2,1,0:T(8,128)S(1)}, u32[]{:S(2)}, u32[]{:S(2)}) collective-permute-start(f32[3,4,128,128]{3,2,1,0:T(8,128)S(1)} %get-tuple-element.51.refs_0_), channel_id=1, source_target_pairs={{0,1},{1,2},{2,3},{3,4},{4,5},{5,6},{6,7},{7,8},{8,9},{9,10},{10,1... | collective-permute-start | bytes 2359304 | tf_op jit(solution)/shard_map/ppermute | solution.py:19
  31.3 0.9 %shard_map.119 = (f32[1,4,128,128]{3,2,1,0:T(8,128)S(1)}, f32[1,4,128,128]{3,2,1,0:T(8,128)S(1)}, f32[1,4,128,128]{3,2,1,0:T(8,128)S(1)}, f32[576,128]{1,0:T(8,128)S(1)}, f32[576,128]{1,0:T(8,128)S(1)}) custom-call(s32[16]{0:T(128)S(1)} %copy-done.7, s32[12]{0:T(128)S(1)} %pad_add_fusion.place_ref, f32[2,2,128,1024]{3,2,1,0:T(8,128)S(1)} %shard_map.113.object_ref, ...), custom_call_target="tpu_custom_call" | custom-call | flops 1 | bytes 6291456 | tf_op jit(solution)/shard_map/pallas_call | solution.py:382
  32.3 1.6 %collective-permute-done.5.got_ref = f32[576,128]{1,0:T(8,128)S(1)} collective-permute-done((f32[576,128]{1,0:T(8,128)S(1)}, f32[576,128]{1,0:T(8,128)S(1)}, u32[]{:S(2)}, u32[]{:S(2)}) %collective-permute-start.5) | collective-permute-done | bytes 294944 | tf_op jit(solution)/shard_map/ppermute | solution.py:293
  33.9 1.6 %collective-permute-start.7 = (f32[288,128]{1,0:T(8,128)S(1)}, f32[288,128]{1,0:T(8,128)S(1)}, u32[]{:S(2)}, u32[]{:S(2)}) collective-permute-start(f32[288,128]{1,0:T(8,128)S(1)} %get-tuple-element.59), channel_id=1, source_target_pairs={{0,4},{1,5},{2,6},{3,7},{4,0},{5,1},{6,2},{7,3},{8,12},{9,13},{10,... | collective-permute-start | bytes 442376 | tf_op jit(solution)/shard_map/ppermute | solution.py:293
  35.5 1.8 %collective-permute-start.4 = (f32[1,4,128,128]{3,2,1,0:T(8,128)S(1)}, f32[1,4,128,128]{3,2,1,0:T(8,128)S(1)}, u32[]{:S(2)}, u32[]{:S(2)}) collective-permute-start(f32[1,4,128,128]{3,2,1,0:T(8,128)S(1)} %shard_map.120), channel_id=1, source_target_pairs={{0,1},{1,2},{2,3},{3,4},{4,5},{5,6},{6,7},{7,8},{8,9},{9,10},{10,1... | collective-permute-start | bytes 786440 | tf_op jit(solution)/shard_map/ppermute | solution.py:19
  37.3 9.3 %collective-permute-start.6 = (f32[1,4,128,128]{3,2,1,0:T(8,128)S(1)}, f32[1,4,128,128]{3,2,1,0:T(8,128)S(1)}, u32[]{:S(2)}, u32[]{:S(2)}) collective-permute-start(f32[1,4,128,128]{3,2,1,0:T(8,128)S(1)} %shard_map.122), channel_id=1, source_target_pairs={{0,1},{1,2},{2,3},{3,4},{4,5},{5,6},{6,7},{7,8},{8,9},{9,10},{10,1... | collective-permute-start | bytes 786440 | tf_op jit(solution)/shard_map/ppermute | solution.py:19
  46.7 2.0 %collective-permute-start.8 = (f32[1,4,128,128]{3,2,1,0:T(8,128)S(1)}, f32[1,4,128,128]{3,2,1,0:T(8,128)S(1)}, u32[]{:S(2)}, u32[]{:S(2)}) collective-permute-start(f32[1,4,128,128]{3,2,1,0:T(8,128)S(1)} %shard_map.124), channel_id=1, source_target_pairs={{0,1},{1,2},{2,3},{3,4},{4,5},{5,6},{6,7},{7,8},{8,9},{9,10},{10,1... | collective-permute-start | bytes 786440 | tf_op jit(solution)/shard_map/ppermute | solution.py:19
  48.8 1.6 %collective-permute-start.9 = (f32[144,128]{1,0:T(8,128)S(1)}, f32[144,128]{1,0:T(8,128)S(1)}, u32[]{:S(2)}, u32[]{:S(2)}) collective-permute-start(f32[144,128]{1,0:T(8,128)S(1)} %get-tuple-element.62), channel_id=1, source_target_pairs={{0,8},{1,9},{2,10},{3,11},{4,12},{5,13},{6,14},{7,15},{8,0},{9,1},... | collective-permute-start | bytes 221192 | tf_op jit(solution)/shard_map/ppermute | solution.py:293
  50.4 3.7 %collective-permute-done.9.got_ref = f32[144,128]{1,0:T(8,128)S(1)} collective-permute-done((f32[144,128]{1,0:T(8,128)S(1)}, f32[144,128]{1,0:T(8,128)S(1)}, u32[]{:S(2)}, u32[]{:S(2)}) %collective-permute-start.9) | collective-permute-done | bytes 73760 | tf_op jit(solution)/shard_map/ppermute | solution.py:293
  54.1 3.6 %collective-permute-start.10 = (f32[144,128]{1,0:T(8,128)S(1)}, f32[144,128]{1,0:T(8,128)S(1)}, u32[]{:S(2)}, u32[]{:S(2)}) collective-permute-start(f32[144,128]{1,0:T(8,128)S(1)} %shard_map.126.kept_ref), channel_id=1, source_target_pairs={{0,2},{1,3},{2,0},{3,1},{4,6},{5,7},{6,4},{7,5},{8,10},{9,11},{10,... | collective-permute-start | bytes 221192 | tf_op jit(solution)/shard_map/ppermute | solution.py:293
  57.8 2.8 %collective-permute-done.10.got_ref = f32[144,128]{1,0:T(8,128)S(1)} collective-permute-done((f32[144,128]{1,0:T(8,128)S(1)}, f32[144,128]{1,0:T(8,128)S(1)}, u32[]{:S(2)}, u32[]{:S(2)}) %collective-permute-start.10) | collective-permute-done | bytes 73760 | tf_op jit(solution)/shard_map/ppermute | solution.py:293
  60.6 1.0 %collective-permute-start.11 = (f32[144,128]{1,0:T(8,128)S(1)}, f32[144,128]{1,0:T(8,128)S(1)}, u32[]{:S(2)}, u32[]{:S(2)}) collective-permute-start(f32[144,128]{1,0:T(8,128)S(1)} %shard_map.127.mine_ref), channel_id=1, source_target_pairs={{0,8},{1,9},{2,10},{3,11},{4,12},{5,13},{6,14},{7,15},{8,0},{9,1},... | collective-permute-start | bytes 221192 | tf_op jit(solution)/shard_map/ppermute | solution.py:293
  61.6 5.6 %collective-permute-done.11.got_ref = f32[144,128]{1,0:T(8,128)S(1)} collective-permute-done((f32[144,128]{1,0:T(8,128)S(1)}, f32[144,128]{1,0:T(8,128)S(1)}, u32[]{:S(2)}, u32[]{:S(2)}) %collective-permute-start.11) | collective-permute-done | bytes 73760 | tf_op jit(solution)/shard_map/ppermute | solution.py:293
  67.4 3.1 %shard_map.125 = f32[2,2,128,1024]{3,2,1,0:T(8,128)} custom-call(s32[16]{0:T(128)S(1)} %copy-done.7, s32[12]{0:T(128)S(1)} %pad_add_fusion.place_ref, s32[12]{0:T(128)S(1)} %collective-permute-done.before_ref, f32[2,2,128,1024]{3,2,1,0:T(8,128)S(1)} %shard_map.113.object_ref, f32[128,1024]{1,0:T(8,128)S(1)} %shard_map.117.lit_ref, ...), custom_call_target="tpu_custom_call" | custom-call | flops 1 | bytes 12582912 | tf_op jit(solution)/shard_map/pallas_call | solution.py:426
  70.5 2.0 %collective-permute-done.12.got_ref = f32[288,128]{1,0:T(8,128)S(1)} collective-permute-done((f32[288,128]{1,0:T(8,128)S(1)}, f32[288,128]{1,0:T(8,128)S(1)}, u32[]{:S(2)}, u32[]{:S(2)}) %collective-permute-start.12) | collective-permute-done | bytes 147488 | tf_op jit(solution)/shard_map/ppermute | solution.py:293
  72.6 1.6 %collective-permute-done.13.got_ref = f32[576,128]{1,0:T(8,128)S(1)} collective-permute-done((f32[576,128]{1,0:T(8,128)S(1)}, f32[576,128]{1,0:T(8,128)S(1)}, u32[]{:S(2)}, u32[]{:S(2)}) %collective-permute-start.13) | collective-permute-done | bytes 294944 | tf_op jit(solution)/shard_map/ppermute | solution.py:293
  74.2 0.9 %shard_map.130 = f32[4,2,128,128]{3,2,1,0:T(8,128)} custom-call(f32[576,128]{1,0:T(8,128)S(1)} %shard_map.129.mine_ref, f32[576,128]{1,0:T(8,128)S(1)} %collective-permute-done.13.got_ref, f32[4,2,128,128]{3,2,1,0:T(8,128)S(1)} %get-tuple-element.44.probe_ref), custom_call_target="tpu_custom_call" | custom-call | tf_op jit(solution)/shard_map/pallas_call | solution.py:438
  (39 shorter events, 3.0 us)
Async XLA Ops:
  1.4 4.1 %collective-permute-start = (s32[12]{0:T(128)S(1)}, s32[12]{0:T(128)S(1)}, u32[]{:S(2)}, u32[]{:S(2)}) collective-permute-start(s32[12]{0:T(128)S(1)} %pad_add_fusion.place_ref), channel_id=1, source_target_pairs={{0,1},{1,2},{2,3},{3,4},{4,5},{5,6},{6,7},{7,8},{8,9},{9,10},{10,1... | collective-permute-start | bytes 152 | tf_op jit(solution)/shard_map/ppermute | solution.py:19
  3.7 1.6 %copy-start = (f32[2,2,128,1024]{3,2,1,0:T(8,128)S(1)}, f32[2,2,128,1024]{3,2,1,0:T(8,128)}, u32[]{:S(2)}) copy-start(f32[2,2,128,1024]{3,2,1,0:T(8,128)} %refs_0_.1) | copy-start | bytes 6291460
  6.2 3.6 %copy-start.1 = (f32[4,2,128,128]{3,2,1,0:T(8,128)S(1)}, f32[4,2,128,128]{3,2,1,0:T(8,128)}, u32[]{:S(2)}) copy-start(f32[4,2,128,128]{3,2,1,0:T(8,128)} %refs_0_.2) | copy-start | bytes 1572868
  6.3 3.6 %copy-start.2 = (f32[6,128,128]{2,1,0:T(8,128)S(1)}, f32[6,128,128]{2,1,0:T(8,128)}, u32[]{:S(2)}) copy-start(f32[6,128,128]{2,1,0:T(8,128)} %refs_1_) | copy-start | bytes 1179652
  6.3 3.6 %copy-start.3 = (bf16[512,256]{1,0:T(8,128)(2,1)S(1)}, bf16[512,256]{1,0:T(8,128)(2,1)}, u32[]{:S(2)}) copy-start(bf16[512,256]{1,0:T(8,128)(2,1)} %constant.11.clone.refs_5_) | copy-start | bytes 786436
  6.3 3.6 %copy-start.4 = (bf16[2,256,256]{2,1,0:T(8,128)(2,1)S(1)}, bf16[2,256,256]{2,1,0:T(8,128)(2,1)}, u32[]{:S(2)}) copy-start(bf16[2,256,256]{2,1,0:T(8,128)(2,1)} %constant.10.clone.refs_4_) | copy-start | bytes 786436
  6.3 3.6 %copy-start.5 = (bf16[512,256]{1,0:T(8,128)(2,1)S(1)}, bf16[512,256]{1,0:T(8,128)(2,1)}, u32[]{:S(2)}) copy-start(bf16[512,256]{1,0:T(8,128)(2,1)} %constant.9.clone.refs_3_) | copy-start | bytes 786436
  6.3 3.6 %copy-start.6 = (bf16[2,256,256]{2,1,0:T(8,128)(2,1)S(1)}, bf16[2,256,256]{2,1,0:T(8,128)(2,1)}, u32[]{:S(2)}) copy-start(bf16[2,256,256]{2,1,0:T(8,128)(2,1)} %constant.8.clone.refs_2_) | copy-start | bytes 786436
  6.3 3.7 %copy-start.7 = (s32[16]{0:T(128)S(1)}, s32[16]{0:T(128)}, u32[]{:S(2)}) copy-start(s32[16]{0:T(128)} %counts_ref.7) | copy-start | bytes 196
  6.3 6.4 %collective-permute-start.1 = (f32[3,4,128,128]{3,2,1,0:T(8,128)S(1)}, f32[3,4,128,128]{3,2,1,0:T(8,128)S(1)}, u32[]{:S(2)}, u32[]{:S(2)}) collective-permute-start(f32[3,4,128,128]{3,2,1,0:T(8,128)S(1)} %shard_map.114), channel_id=1, source_target_pairs={{1,0},{2,1},{3,2},{4,3},{5,4},{6,5},{7,6},{8,7},{9,8},{10,9},{11,1... | collective-permute-start | bytes 2359304 | tf_op jit(solution)/shard_map/ppermute | solution.py:19
  8.5 22.8 %collective-permute-start.2 = (f32[3,4,128,128]{3,2,1,0:T(8,128)S(1)}, f32[3,4,128,128]{3,2,1,0:T(8,128)S(1)}, u32[]{:S(2)}, u32[]{:S(2)}) collective-permute-start(f32[3,4,128,128]{3,2,1,0:T(8,128)S(1)} %shard_map.115), channel_id=1, source_target_pairs={{1,0},{2,1},{3,2},{4,3},{5,4},{6,5},{7,6},{8,7},{9,8},{10,9},{11,1... | collective-permute-start | bytes 2359304 | tf_op jit(solution)/shard_map/ppermute | solution.py:19
  19.7 34.4 %collective-permute-start.3 = (f32[3,4,128,128]{3,2,1,0:T(8,128)S(1)}, f32[3,4,128,128]{3,2,1,0:T(8,128)S(1)}, u32[]{:S(2)}, u32[]{:S(2)}) collective-permute-start(f32[3,4,128,128]{3,2,1,0:T(8,128)S(1)} %get-tuple-element.51.refs_0_), channel_id=1, source_target_pairs={{0,1},{1,2},{2,3},{3,4},{4,5},{5,6},{6,7},{7,8},{8,9},{9,10},{10,1... | collective-permute-start | bytes 2359304 | tf_op jit(solution)/shard_map/ppermute | solution.py:19
  32.2 1.6 %collective-permute-start.5 = (f32[576,128]{1,0:T(8,128)S(1)}, f32[576,128]{1,0:T(8,128)S(1)}, u32[]{:S(2)}, u32[]{:S(2)}) collective-permute-start(f32[576,128]{1,0:T(8,128)S(1)} %get-tuple-element.56), channel_id=1, source_target_pairs={{0,1},{1,0},{2,3},{3,2},{4,5},{5,4},{6,7},{7,6},{8,9},{9,8},{10,11... | collective-permute-start | bytes 884744 | tf_op jit(solution)/shard_map/ppermute | solution.py:293
  33.9 12.8 %collective-permute-start.7 = (f32[288,128]{1,0:T(8,128)S(1)}, f32[288,128]{1,0:T(8,128)S(1)}, u32[]{:S(2)}, u32[]{:S(2)}) collective-permute-start(f32[288,128]{1,0:T(8,128)S(1)} %get-tuple-element.59), channel_id=1, source_target_pairs={{0,4},{1,5},{2,6},{3,7},{4,0},{5,1},{6,2},{7,3},{8,12},{9,13},{10,... | collective-permute-start | bytes 442376 | tf_op jit(solution)/shard_map/ppermute | solution.py:293
  35.5 31.8 %collective-permute-start.4 = (f32[1,4,128,128]{3,2,1,0:T(8,128)S(1)}, f32[1,4,128,128]{3,2,1,0:T(8,128)S(1)}, u32[]{:S(2)}, u32[]{:S(2)}) collective-permute-start(f32[1,4,128,128]{3,2,1,0:T(8,128)S(1)} %shard_map.120), channel_id=1, source_target_pairs={{0,1},{1,2},{2,3},{3,4},{4,5},{5,6},{6,7},{7,8},{8,9},{9,10},{10,1... | collective-permute-start | bytes 786440 | tf_op jit(solution)/shard_map/ppermute | solution.py:19
  37.3 29.9 %collective-permute-start.6 = (f32[1,4,128,128]{3,2,1,0:T(8,128)S(1)}, f32[1,4,128,128]{3,2,1,0:T(8,128)S(1)}, u32[]{:S(2)}, u32[]{:S(2)}) collective-permute-start(f32[1,4,128,128]{3,2,1,0:T(8,128)S(1)} %shard_map.122), channel_id=1, source_target_pairs={{0,1},{1,2},{2,3},{3,4},{4,5},{5,6},{6,7},{7,8},{8,9},{9,10},{10,1... | collective-permute-start | bytes 786440 | tf_op jit(solution)/shard_map/ppermute | solution.py:19
  46.7 20.5 %collective-permute-start.8 = (f32[1,4,128,128]{3,2,1,0:T(8,128)S(1)}, f32[1,4,128,128]{3,2,1,0:T(8,128)S(1)}, u32[]{:S(2)}, u32[]{:S(2)}) collective-permute-start(f32[1,4,128,128]{3,2,1,0:T(8,128)S(1)} %shard_map.124), channel_id=1, source_target_pairs={{0,1},{1,2},{2,3},{3,4},{4,5},{5,6},{6,7},{7,8},{8,9},{9,10},{10,1... | collective-permute-start | bytes 786440 | tf_op jit(solution)/shard_map/ppermute | solution.py:19
  48.8 5.3 %collective-permute-start.9 = (f32[144,128]{1,0:T(8,128)S(1)}, f32[144,128]{1,0:T(8,128)S(1)}, u32[]{:S(2)}, u32[]{:S(2)}) collective-permute-start(f32[144,128]{1,0:T(8,128)S(1)} %get-tuple-element.62), channel_id=1, source_target_pairs={{0,8},{1,9},{2,10},{3,11},{4,12},{5,13},{6,14},{7,15},{8,0},{9,1},... | collective-permute-start | bytes 221192 | tf_op jit(solution)/shard_map/ppermute | solution.py:293
  54.1 6.5 %collective-permute-start.10 = (f32[144,128]{1,0:T(8,128)S(1)}, f32[144,128]{1,0:T(8,128)S(1)}, u32[]{:S(2)}, u32[]{:S(2)}) collective-permute-start(f32[144,128]{1,0:T(8,128)S(1)} %shard_map.126.kept_ref), channel_id=1, source_target_pairs={{0,2},{1,3},{2,0},{3,1},{4,6},{5,7},{6,4},{7,5},{8,10},{9,11},{10,... | collective-permute-start | bytes 221192 | tf_op jit(solution)/shard_map/ppermute | solution.py:293
  60.6 6.6 %collective-permute-start.11 = (f32[144,128]{1,0:T(8,128)S(1)}, f32[144,128]{1,0:T(8,128)S(1)}, u32[]{:S(2)}, u32[]{:S(2)}) collective-permute-start(f32[144,128]{1,0:T(8,128)S(1)} %shard_map.127.mine_ref), channel_id=1, source_target_pairs={{0,8},{1,9},{2,10},{3,11},{4,12},{5,13},{6,14},{7,15},{8,0},{9,1},... | collective-permute-start | bytes 221192 | tf_op jit(solution)/shard_map/ppermute | solution.py:293
  67.3 5.2 %collective-permute-start.12 = (f32[288,128]{1,0:T(8,128)S(1)}, f32[288,128]{1,0:T(8,128)S(1)}, u32[]{:S(2)}, u32[]{:S(2)}) collective-permute-start(f32[288,128]{1,0:T(8,128)S(1)} %shard_map.128.mine_ref), channel_id=1, source_target_pairs={{0,4},{1,5},{2,6},{3,7},{4,0},{5,1},{6,2},{7,3},{8,12},{9,13},{10,... | collective-permute-start | bytes 442376 | tf_op jit(solution)/shard_map/ppermute | solution.py:293
  72.5 1.6 %collective-permute-start.13 = (f32[576,128]{1,0:T(8,128)S(1)}, f32[576,128]{1,0:T(8,128)S(1)}, u32[]{:S(2)}, u32[]{:S(2)}) collective-permute-start(f32[576,128]{1,0:T(8,128)S(1)} %shard_map.129.mine_ref), channel_id=1, source_target_pairs={{0,1},{1,0},{2,3},{3,2},{4,5},{5,4},{6,7},{7,6},{8,9},{9,8},{10,11... | collective-permute-start | bytes 884744 | tf_op jit(solution)/shard_map/ppermute | solution.py:293
